TPU v7x, 512 devices: a whole 4x4x16 slice. The times are simulated.
512 devices in a mesh: seq: 32 (over y, x, core), dp: 16 (over z).
Axes of the slice: x: 4, y: 4, z: 16, core: 2. Of those that a mesh axis runs over, the one named last changes fastest.
Arguments:
- q_raw: bfloat16 [16, 4096, 4096], P('dp', 'seq'), may hold values from -21 to 21
- k_raw: bfloat16 [16, 4096, 1024], P('dp', 'seq'), may hold values from -21 to 21
- v_raw: bfloat16 [16, 4096, 1024], P('dp', 'seq'), may hold values from -6 to 6
- q_gain: float32 [128], P('dp'), may hold values from 0.5 to 6
- k_gain: float32 [128], P('dp'), may hold values from 0.5 to 6
- key_blocks: int32 [32, 32, 6], P('seq'), may hold values from -1 to 31, as said below
- d_context: bfloat16 [16, 4096, 4096], P('dp', 'seq'), may hold values from -21 to 21
Outputs:
- q_raw_grad: bfloat16 [16, 4096, 4096], P('dp', 'seq')
- k_raw_grad: bfloat16 [16, 4096, 1024], P('dp', 'seq')
- v_grad: bfloat16 [16, 4096, 1024], P('dp', 'seq')
- q_gain_grad: float32 [128], P('dp')
- k_gain_grad: float32 [128], P('dp')
Inputs may be any that keep to these rules, and one draw needn't show every extreme that they name: key_blocks[h, b, 0] = b; slots 1 and 2 hold b - 1 and b + 1, or -1 past the ends of the sequence; the next 1 slots hold blocks 0 to 0; the last 2 slots hold drawn blocks, which may repeat earlier slots.
All inputs are finite; a program needn't handle non-finite values.
Results may differ from a plain program's by a relative error of at most 0.017.
The roundings to bfloat16 on the way count: a program that leaves them out, or rounds other values in their place, can miss the bound.
Values may be sent and summed in bfloat16 or wider, within the bound.
No kernel may reach another device: no remote copies, remote signals or barrier semaphores. Data moves between devices by JAX's collectives and lax.ppermute only.
A program may use at most 64 MiB of HBM per device.

v0:
```python
import math

import jax
import jax.numpy as jnp
from jax import lax
from jax.sharding import PartitionSpec as P

BLK = 128
GLOB = 1


EPSILON = 1e-06


def slot_keep(pattern):
    slot_count = pattern.shape[-1]
    present = pattern >= 0
    same_block = pattern[:, :, None] == pattern[:, None, :]
    earlier = jnp.arange(slot_count)[None, :] < jnp.arange(slot_count)[:, None]
    repeated = jnp.any(same_block & earlier[None, :, :], axis=2)
    return present & jnp.logical_not(repeated)


def norm_rows(raw_rows, gain_vec):
    length_total = raw_rows.shape[0]
    width = gain_vec.shape[0]
    values = raw_rows.astype(jnp.float32).reshape(length_total, -1, width)
    inverse = lax.rsqrt(jnp.mean(values * values, axis=-1, keepdims=True) + EPSILON)
    normed = (values * inverse * gain_vec).astype(jnp.bfloat16).reshape(length_total, -1)
    return (normed, inverse)


def norm_back(raw_rows, inverse, gain_vec, d_normed):
    length_total = raw_rows.shape[0]
    width = gain_vec.shape[0]
    values = raw_rows.astype(jnp.float32).reshape(length_total, -1, width)
    upstream = d_normed.astype(jnp.float32).reshape(length_total, -1, width)
    scaled = gain_vec * upstream
    row_total = jnp.sum(scaled * values, axis=-1, keepdims=True)
    d_raw = inverse * scaled - inverse * inverse * inverse * values * row_total / width
    gain_part = jnp.sum(upstream * values * inverse, axis=(0, 1))
    return (d_raw.astype(jnp.bfloat16).reshape(length_total, -1), gain_part)


def softmax_rows(score_matrix, axes):
    row_peak = jnp.max(score_matrix, axis=axes, keepdims=True)
    raised = jnp.exp(score_matrix - row_peak)
    return raised / jnp.sum(raised, axis=axes, keepdims=True)


def tile_layout(head_array):
    length_total, width_per_head = head_array.shape
    return head_array.reshape(length_total // BLK, BLK, width_per_head)


def group_size(blocks):
    return math.gcd(blocks, max(1, 1024 // BLK))


def backward_head(q_head, k_head, v_head, d_head, pattern):
    length_total, width_per_head = q_head.shape
    blocks = length_total // BLK
    lead_rows = GLOB * BLK
    logit_scale = 1.0 / math.sqrt(width_per_head)
    keep_slot = slot_keep(pattern)
    picked = jnp.maximum(pattern, 0)
    query_tiles = tile_layout(q_head)
    k_tiles = tile_layout(k_head)
    v_tiles = tile_layout(v_head)
    tile_gradient = tile_layout(d_head)
    group_len = group_size(blocks)
    top_precision = lax.Precision.HIGHEST

    def one_group(carry, group_index):
        k_acc, v_acc = carry
        first_block = group_index * group_len
        query_rows = lax.dynamic_slice_in_dim(query_tiles, first_block, group_len, 0)
        grad_rows = lax.dynamic_slice_in_dim(tile_gradient, first_block, group_len, 0)
        chosen = lax.dynamic_slice_in_dim(picked, first_block, group_len, 0)
        allowed = lax.dynamic_slice_in_dim(keep_slot, first_block, group_len, 0)
        selected_keys = k_tiles[chosen]
        selected_values = v_tiles[chosen]
        score_matrix = (
            jnp.einsum(
                "gqd,gskd->gqsk", query_rows, selected_keys, preferred_element_type=jnp.float32
            )
            * logit_scale
        )
        score_matrix = jnp.where(allowed[:, None, :, None], score_matrix, -jnp.inf)
        weights = softmax_rows(score_matrix, (2, 3))
        weight_reduced = weights.astype(jnp.bfloat16)
        sparse_query_row = (first_block + jnp.arange(group_len) >= GLOB)[:, None, None, None]
        weight_gradient = jnp.einsum(
            "gqd,gskd->gqsk", grad_rows, selected_values, preferred_element_type=jnp.float32
        )
        row_delta = jnp.sum(weights * weight_gradient, axis=(2, 3), keepdims=True)
        score_gradient = jnp.where(
            sparse_query_row, weights * (weight_gradient - row_delta) * logit_scale, 0.0
        ).astype(jnp.bfloat16)
        d_query = jnp.einsum(
            "gqsk,gskd->gqd", score_gradient, selected_keys, preferred_element_type=jnp.float32
        )
        key_pieces = jnp.einsum(
            "gqsk,gqd->gskd", score_gradient, query_rows, preferred_element_type=jnp.float32
        )
        kept_low = jnp.where(sparse_query_row, weight_reduced, jnp.zeros_like(weight_reduced))
        value_pieces = jnp.einsum(
            "gqsk,gqd->gskd", kept_low, grad_rows, preferred_element_type=jnp.float32
        )
        one_hot = (
            (chosen[:, :, None] == jnp.arange(blocks)[None, None, :]) & allowed[:, :, None]
        ).astype(jnp.float32)
        k_acc = k_acc + jnp.einsum("gsn,gskd->nkd", one_hot, key_pieces, precision=top_precision)
        v_acc = v_acc + jnp.einsum("gsn,gskd->nkd", one_hot, value_pieces, precision=top_precision)
        return ((k_acc, v_acc), d_query)

    zero_acc = jnp.zeros((blocks, BLK, width_per_head), jnp.float32)
    sums, q_groups = lax.scan(one_group, (zero_acc, zero_acc), jnp.arange(blocks // group_len))
    query_sparse = q_groups.reshape(length_total, width_per_head)
    k_sparse = sums[0].reshape(length_total, width_per_head)
    v_sparse = sums[1].reshape(length_total, width_per_head)
    q_lead = q_head[:lead_rows]
    d_lead = d_head[:lead_rows]
    lead_scores = (
        jnp.einsum("qd,kd->qk", q_lead, k_head, preferred_element_type=jnp.float32) * logit_scale
    )
    lead_weights = softmax_rows(lead_scores, (1,))
    lead_low = lead_weights.astype(jnp.bfloat16)
    lead_dprob = jnp.einsum("qd,kd->qk", d_lead, v_head, preferred_element_type=jnp.float32)
    lead_delta = jnp.sum(lead_weights * lead_dprob, axis=1, keepdims=True)
    lead_dscore = (lead_weights * (lead_dprob - lead_delta) * logit_scale).astype(jnp.bfloat16)
    lead_dq = jnp.dot(lead_dscore, k_head, preferred_element_type=jnp.float32)
    lead_dk = jnp.einsum("qk,qd->kd", lead_dscore, q_lead, preferred_element_type=jnp.float32)
    lead_dv = jnp.einsum("qk,qd->kd", lead_low, d_lead, preferred_element_type=jnp.float32)
    d_query = jnp.concatenate([lead_dq, query_sparse[lead_rows:]], axis=0).astype(jnp.bfloat16)
    return (d_query, k_sparse + lead_dk, v_sparse + lead_dv)


def widen_heads(rows, width_per_head, group_len):
    tokens = rows.shape[0]
    kv_count = rows.shape[1] // width_per_head
    spread = jnp.broadcast_to(
        rows.reshape(tokens, kv_count, 1, width_per_head),
        (tokens, kv_count, group_len, width_per_head),
    )
    return spread.reshape(tokens, kv_count * group_len * width_per_head)


def shards(q_raw, k_raw, v_raw, q_gain, k_gain, key_blocks, d_context):
    q_full, k_full = (
        lax.all_gather(q_gain, "dp", axis=0, tiled=True),
        lax.all_gather(k_gain, "dp", axis=0, tiled=True),
    )
    q_normed, q_inverse = norm_rows(q_raw[0], q_full)
    k_normed, k_inverse = norm_rows(k_raw[0], k_full)
    width_per_head = q_full.shape[0]
    group_len = q_raw.shape[2] // k_raw.shape[2]
    tokens = q_raw.shape[1]
    k_wide = widen_heads(k_normed, width_per_head, group_len)
    v_wide = widen_heads(v_raw[0], width_per_head, group_len)
    q_heads, k_heads, v_heads, d_heads = (
        lax.all_to_all(q_normed, "seq", split_axis=1, concat_axis=0, tiled=True),
        lax.all_to_all(k_wide, "seq", split_axis=1, concat_axis=0, tiled=True),
        lax.all_to_all(v_wide, "seq", split_axis=1, concat_axis=0, tiled=True),
        lax.all_to_all(d_context[0], "seq", split_axis=1, concat_axis=0, tiled=True),
    )
    length_total = q_heads.shape[0]
    head_count = key_blocks.shape[0]

    def split_heads(head_array):
        return head_array.reshape(length_total, head_count, width_per_head)

    def merge_heads(head_array):
        return head_array.reshape(length_total, head_count * width_per_head)

    backward = jax.vmap(backward_head, in_axes=(1, 1, 1, 1, 0), out_axes=1)
    dq_heads, dk_heads, dv_heads = backward(
        split_heads(q_heads),
        split_heads(k_heads),
        split_heads(v_heads),
        split_heads(d_heads),
        key_blocks,
    )
    dq_heads = merge_heads(dq_heads)
    dk_heads = merge_heads(dk_heads)
    dv_heads = merge_heads(dv_heads)
    d_q_normed = lax.all_to_all(dq_heads, "seq", split_axis=0, concat_axis=1, tiled=True)
    dk_terms, dv_terms = (
        lax.all_to_all(dk_heads, "seq", split_axis=0, concat_axis=1, tiled=True),
        lax.all_to_all(dv_heads, "seq", split_axis=0, concat_axis=1, tiled=True),
    )
    kv_count = k_raw.shape[2] // width_per_head
    d_k_normed = (
        jnp.sum(dk_terms.reshape(tokens, kv_count, group_len, width_per_head), axis=2)
        .astype(jnp.bfloat16)
        .reshape(tokens, kv_count * width_per_head)
    )
    v_grad = (
        jnp.sum(dv_terms.reshape(tokens, kv_count, group_len, width_per_head), axis=2)
        .astype(jnp.bfloat16)
        .reshape(tokens, kv_count * width_per_head)
    )
    q_grad, q_part = norm_back(q_raw[0], q_inverse, q_full, d_q_normed)
    k_grad, k_part = norm_back(k_raw[0], k_inverse, k_full, d_k_normed)
    q_total, k_total = lax.psum((q_part, k_part), ("seq", "dp"))
    shard_len = q_gain.shape[0]
    offset = lax.axis_index("dp") * shard_len
    q_gain_grad = lax.dynamic_slice_in_dim(q_total, offset, shard_len)
    k_gain_grad = lax.dynamic_slice_in_dim(k_total, offset, shard_len)
    return (q_grad[None], k_grad[None], v_grad[None], q_gain_grad, k_gain_grad)


def solution(mesh):
    placed = (
        P("dp", "seq", None),
        P("dp", "seq", None),
        P("dp", "seq", None),
        P("dp"),
        P("dp"),
        P("seq", None, None),
        P("dp", "seq", None),
    )
    return jax.shard_map(
        shards,
        mesh=mesh,
        in_specs=placed,
        out_specs=(
            P("dp", "seq", None),
            P("dp", "seq", None),
            P("dp", "seq", None),
            P("dp"),
            P("dp"),
        ),
        check_vma=False,
    )
```

profile of v0, /device:TPU:1, one launch (start us, length us, event | category | flops | bytes accessed | tf_op | source)
XLA Modules:
  0.0 443.7 jit_solution(1916653222187452751)
XLA Ops:
  5.7 30.3 %all-reduce.4 = (f32[128]{0:T(128)S(1)}, f32[128]{0:T(128)S(1)}) all-reduce(f32[128]{0:T(128)S(1)} %dynamic-update-slice.4, f32[128]{0:T(128)S(1)} %dynamic-update-slice.5), channel_id=1, replica_groups=mesh['seq'=32,'dp'=16] {'dp'}, use_global_device_ids=true, to_apply=%add.1 | all-reduce | flops 256 | bytes 2048
  37.4 14.8 %all-to-all-start.1 = ((bf16[128,32,128]{2,0,1:T(8,128)(2,1)}), bf16[128,32,128]{2,0,1:T(8,128)(2,1)S(1)}, u32[]{:S(2)}, u32[]{:S(2)}) async-start(bf16[128,32,128]{2,0,1:T(8,128)(2,1)} %bitcast.6), calls=%async_computation.1 | async-start | bytes 2097152 | tf_op jit(solution)/shard_map/all_to_all | solution.py:163
  52.3 16.9 %all-to-all-done.1 = bf16[128,32,128]{2,0,1:T(8,128)(2,1)S(1)} async-done(((bf16[128,32,128]{2,0,1:T(8,128)(2,1)}), bf16[128,32,128]{2,0,1:T(8,128)(2,1)S(1)}, u32[]{:S(2)}, u32[]{:S(2)}) %all-to-all-start.1) | async-done | bytes 1048608 | tf_op jit(solution)/shard_map/all_to_all | solution.py:163
  70.5 4.0 all-to-all-start.3
  74.5 2.3 copy.127
  78.2 2.6 fusion.49
  80.9 10.8 %all-to-all-done.3 = bf16[128,32,128]{2,0,1:T(8,128)(2,1)S(1)} async-done(((bf16[128,32,128]{2,0,1:T(8,128)(2,1)}), bf16[128,32,128]{2,0,1:T(8,128)(2,1)S(1)}, u32[]{:S(2)}, u32[]{:S(2)}) %all-to-all-start.3) | async-done | bytes 1048608 | tf_op jit(solution)/shard_map/all_to_all | solution.py:164
  91.7 4.6 %all-to-all-start = ((bf16[128,32,128]{0,2,1:T(8,128)(2,1)}), bf16[128,32,128]{0,2,1:T(8,128)(2,1)}, u32[]{:S(2)}, u32[]{:S(2)}) async-start(bf16[128,32,128]{0,2,1:T(8,128)(2,1)} %fusion.49), calls=%async_computation | async-start | bytes 2097152 | tf_op jit(solution)/shard_map/all_to_all | solution.py:162
  96.3 2.3 copy.130
  98.6 14.9 %all-to-all-done = bf16[128,32,128]{0,2,1:T(8,128)(2,1)} async-done(((bf16[128,32,128]{0,2,1:T(8,128)(2,1)}), bf16[128,32,128]{0,2,1:T(8,128)(2,1)}, u32[]{:S(2)}, u32[]{:S(2)}) %all-to-all-start) | async-done | bytes 1048608 | tf_op jit(solution)/shard_map/all_to_all | solution.py:162
  113.5 4.6 %all-to-all-start.2 = ((bf16[128,32,128]{0,2,1:T(8,128)(2,1)}), bf16[128,32,128]{0,2,1:T(8,128)(2,1)}, u32[]{:S(2)}, u32[]{:S(2)}) async-start(bf16[128,32,128]{0,2,1:T(8,128)(2,1)} %bitcast.261), calls=%async_computation.2 | async-start | bytes 2097152 | tf_op jit(solution)/shard_map/all_to_all | solution.py:165
  118.3 17.0 %all-to-all-done.2 = bf16[128,32,128]{0,2,1:T(8,128)(2,1)} async-done(((bf16[128,32,128]{0,2,1:T(8,128)(2,1)}), bf16[128,32,128]{0,2,1:T(8,128)(2,1)}, u32[]{:S(2)}, u32[]{:S(2)}) %all-to-all-start.2) | async-done | bytes 1048608 | tf_op jit(solution)/shard_map/all_to_all | solution.py:165
  135.4 107.4 %while.19 = (s32[]{:T(128)}, f32[1,32,128,128]{3,1,2,0:T(8,128)}, f32[1,32,128,128]{3,1,2,0:T(8,128)}, bf16[4,1,8,128,128]{4,3,2,1,0:T(8,128)(2,1)}, s32[4]{0:T(...) while((s32[]{:T(128)}, f32[1,32,128,128]{3,1,2,0:T(8,128)}, ...), condition=%wide.region_10.11_spmd.clone, body=%wide.region_6.10_spmd.clone.sunk | while | flops 1634733440 | bytes 100189440 | solution.py:118
  149.9 4.5 %bitcast_add_fusion.5 = f32[1,32,128,128]{3,1,2,0:T(8,128)S(1)} fusion(f32[1,32,128,128]{3,1,2,0:T(8,128)S(1)} %copy-done.2, f32[8,6,128,128]{3,2,1,0:T(8,128)S(1)} %fusion.122, pred[]{:T(512)S(6)} %compare.8, s32[8,6]{0,1:T(8,128)S(1)} %fusion.120, pred[8,6]{0,1:T(8,128)(4,1)S(1)} %fusion.121), kind=kOutput, calls=%fused_computation.13.clone.1 | convolution fusion | flops 303041536 | bytes 7340273 | tf_op jit(solution)/shard_map/vmap()/while/body/eval_jaxpr/gsn,gskd->nkd/dot_general | solution.py:114
  156.2 4.8 %bitcast_add_fusion.4 = f32[1,32,128,128]{3,1,2,0:T(8,128)} fusion(f32[1,32,128,128]{3,1,2,0:T(8,128)} %get-tuple-element.361, f32[8,6,128,128]{3,2,1,0:T(8,128)S(1)} %fusion.119, pred[]{:T(512)S(6)} %compare.8, s32[8,6]{0,1:T(8,128)S(1)} %fusion.120, pred[8,6]{0,1:T(8,128)(4,1)S(1)} %fusion.121), kind=kOutput, calls=%fused_computation.14.clone.1 | convolution fusion | flops 303041536 | bytes 7340273 | tf_op jit(solution)/shard_map/vmap()/while/body/eval_jaxpr/gsn,gskd->nkd/dot_general | solution.py:113
  175.5 4.5 %bitcast_add_fusion.5 = f32[1,32,128,128]{3,1,2,0:T(8,128)S(1)} fusion(f32[1,32,128,128]{3,1,2,0:T(8,128)S(1)} %copy-done.2, f32[8,6,128,128]{3,2,1,0:T(8,128)S(1)} %fusion.122, pred[]{:T(512)S(6)} %compare.8, s32[8,6]{0,1:T(8,128)S(1)} %fusion.120, pred[8,6]{0,1:T(8,128)(4,1)S(1)} %fusion.121), kind=kOutput, calls=%fused_computation.13.clone.1 | convolution fusion | flops 303041536 | bytes 7340273 | tf_op jit(solution)/shard_map/vmap()/while/body/eval_jaxpr/gsn,gskd->nkd/dot_general | solution.py:114
  181.8 6.4 %bitcast_add_fusion.4 = f32[1,32,128,128]{3,1,2,0:T(8,128)} fusion(f32[1,32,128,128]{3,1,2,0:T(8,128)} %get-tuple-element.361, f32[8,6,128,128]{3,2,1,0:T(8,128)S(1)} %fusion.119, pred[]{:T(512)S(6)} %compare.8, s32[8,6]{0,1:T(8,128)S(1)} %fusion.120, pred[8,6]{0,1:T(8,128)(4,1)S(1)} %fusion.121), kind=kOutput, calls=%fused_computation.14.clone.1 | convolution fusion | flops 303041536 | bytes 7340273 | tf_op jit(solution)/shard_map/vmap()/while/body/eval_jaxpr/gsn,gskd->nkd/dot_general | solution.py:113
  202.8 4.5 %bitcast_add_fusion.5 = f32[1,32,128,128]{3,1,2,0:T(8,128)S(1)} fusion(f32[1,32,128,128]{3,1,2,0:T(8,128)S(1)} %copy-done.2, f32[8,6,128,128]{3,2,1,0:T(8,128)S(1)} %fusion.122, pred[]{:T(512)S(6)} %compare.8, s32[8,6]{0,1:T(8,128)S(1)} %fusion.120, pred[8,6]{0,1:T(8,128)(4,1)S(1)} %fusion.121), kind=kOutput, calls=%fused_computation.13.clone.1 | convolution fusion | flops 303041536 | bytes 7340273 | tf_op jit(solution)/shard_map/vmap()/while/body/eval_jaxpr/gsn,gskd->nkd/dot_general | solution.py:114
  209.1 6.4 %bitcast_add_fusion.4 = f32[1,32,128,128]{3,1,2,0:T(8,128)} fusion(f32[1,32,128,128]{3,1,2,0:T(8,128)} %get-tuple-element.361, f32[8,6,128,128]{3,2,1,0:T(8,128)S(1)} %fusion.119, pred[]{:T(512)S(6)} %compare.8, s32[8,6]{0,1:T(8,128)S(1)} %fusion.120, pred[8,6]{0,1:T(8,128)(4,1)S(1)} %fusion.121), kind=kOutput, calls=%fused_computation.14.clone.1 | convolution fusion | flops 303041536 | bytes 7340273 | tf_op jit(solution)/shard_map/vmap()/while/body/eval_jaxpr/gsn,gskd->nkd/dot_general | solution.py:113
  230.1 4.5 %bitcast_add_fusion.5 = f32[1,32,128,128]{3,1,2,0:T(8,128)S(1)} fusion(f32[1,32,128,128]{3,1,2,0:T(8,128)S(1)} %copy-done.2, f32[8,6,128,128]{3,2,1,0:T(8,128)S(1)} %fusion.122, pred[]{:T(512)S(6)} %compare.8, s32[8,6]{0,1:T(8,128)S(1)} %fusion.120, pred[8,6]{0,1:T(8,128)(4,1)S(1)} %fusion.121), kind=kOutput, calls=%fused_computation.13.clone.1 | convolution fusion | flops 303041536 | bytes 7340273 | tf_op jit(solution)/shard_map/vmap()/while/body/eval_jaxpr/gsn,gskd->nkd/dot_general | solution.py:114
  236.3 6.4 %bitcast_add_fusion.4 = f32[1,32,128,128]{3,1,2,0:T(8,128)} fusion(f32[1,32,128,128]{3,1,2,0:T(8,128)} %get-tuple-element.361, f32[8,6,128,128]{3,2,1,0:T(8,128)S(1)} %fusion.119, pred[]{:T(512)S(6)} %compare.8, s32[8,6]{0,1:T(8,128)S(1)} %fusion.120, pred[8,6]{0,1:T(8,128)(4,1)S(1)} %fusion.121), kind=kOutput, calls=%fused_computation.14.clone.1 | convolution fusion | flops 303041536 | bytes 7340273 | tf_op jit(solution)/shard_map/vmap()/while/body/eval_jaxpr/gsn,gskd->nkd/dot_general | solution.py:113
  250.0 4.0 all-to-all-start.4
  253.9 2.8 copy.140
  256.7 2.5 convolution_add_fusion.1
  259.3 11.8 %all-to-all-done.4 = bf16[32,128,128]{1,2,0:T(8,128)(2,1)S(1)} async-done(((bf16[32,128,128]{1,2,0:T(8,128)(2,1)}), bf16[32,128,128]{1,2,0:T(8,128)(2,1)S(1)}, u32[]{:S(2)}, u32[]{:S(2)}) %all-to-all-start.4) | async-done | bytes 1048608 | tf_op jit(solution)/shard_map/all_to_all | solution.py:187
  272.1 4.9 %all-to-all-start.5 = ((f32[32,128,128]{2,1,0:T(8,128)}), f32[32,128,128]{2,1,0:T(8,128)}, u32[]{:S(2)}, u32[]{:S(2)}) async-start(f32[32,128,128]{2,1,0:T(8,128)} %bitcast.258), calls=%async_computation.5 | async-start | bytes 4194304 | tf_op jit(solution)/shard_map/all_to_all | solution.py:189
  278.6 2.8 convolution_add_fusion
  281.3 24.0 %all-to-all-done.5 = f32[32,128,128]{2,1,0:T(8,128)} async-done(((f32[32,128,128]{2,1,0:T(8,128)}), f32[32,128,128]{2,1,0:T(8,128)}, u32[]{:S(2)}, u32[]{:S(2)}) %all-to-all-start.5) | async-done | bytes 2097184 | tf_op jit(solution)/shard_map/all_to_all | solution.py:189
  305.3 5.9 %all-to-all-start.6 = ((f32[32,128,128]{2,1,0:T(8,128)}), f32[32,128,128]{2,1,0:T(8,128)S(1)}, u32[]{:S(2)}, u32[]{:S(2)}) async-start(f32[32,128,128]{2,1,0:T(8,128)} %bitcast.265), calls=%async_computation.6 | async-start | bytes 4194304 | tf_op jit(solution)/shard_map/all_to_all | solution.py:190
  311.3 3.6 fusion.53
  321.8 17.8 %all-to-all-done.6 = f32[32,128,128]{2,1,0:T(8,128)S(1)} async-done(((f32[32,128,128]{2,1,0:T(8,128)}), f32[32,128,128]{2,1,0:T(8,128)S(1)}, u32[]{:S(2)}, u32[]{:S(2)}) %all-to-all-start.6) | async-done | bytes 2097184 | tf_op jit(solution)/shard_map/all_to_all | solution.py:190
  341.1 100.5 %all-reduce.3 = (f32[128]{0:T(128)S(1)}, f32[128]{0:T(128)S(1)}) all-reduce(f32[128]{0:T(128)S(1)} %fusion.55, f32[128]{0:T(128)S(1)} %bitcast_reduce_fusion.2), channel_id=1, replica_groups=mesh['seq'=32,'dp'=16] {'seq','dp'}, use_global_device_ids=true, to_apply=%region_16.17 | all-reduce | flops 256 | bytes 2048 | tf_op jit(solution)/shard_map/psum | solution.py:205
  (215 shorter events, 91.2 us)
Async XLA Ops:
  2.0 35.4 %copy-start.9 = (f32[128,8,128]{2,0,1:T(8,128)}, f32[128,8,128]{2,0,1:T(8,128)S(1)}, u32[]{:S(2)}) copy-start(f32[128,8,128]{2,0,1:T(8,128)S(1)} %copy.129) | copy-start | bytes 1572868
  36.0 16.2 %copy-start.15 = (bf16[1,128,1024]{2,1,0:T(8,128)(2,1)S(1)}, bf16[1,128,1024]{2,1,0:T(8,128)(2,1)}, u32[]{:S(2)}) copy-start(bf16[1,128,1024]{2,1,0:T(8,128)(2,1)} %param.11) | copy-start | bytes 786436
  37.4 31.8 %all-to-all-start.1 = ((bf16[128,32,128]{2,0,1:T(8,128)(2,1)}), bf16[128,32,128]{2,0,1:T(8,128)(2,1)S(1)}, u32[]{:S(2)}, u32[]{:S(2)}) async-start(bf16[128,32,128]{2,0,1:T(8,128)(2,1)} %bitcast.6), calls=%async_computation.1 | async-start | bytes 2097152 | tf_op jit(solution)/shard_map/all_to_all | solution.py:163
  70.5 21.1 %all-to-all-start.3 = ((bf16[128,32,128]{2,0,1:T(8,128)(2,1)}), bf16[128,32,128]{2,0,1:T(8,128)(2,1)S(1)}, u32[]{:S(2)}, u32[]{:S(2)}) async-start(bf16[128,32,128]{2,0,1:T(8,128)(2,1)} %bitcast.260), calls=%async_computation.3 | async-start | bytes 2097152 | tf_op jit(solution)/shard_map/all_to_all | solution.py:164
  91.7 21.9 %all-to-all-start = ((bf16[128,32,128]{0,2,1:T(8,128)(2,1)}), bf16[128,32,128]{0,2,1:T(8,128)(2,1)}, u32[]{:S(2)}, u32[]{:S(2)}) async-start(bf16[128,32,128]{0,2,1:T(8,128)(2,1)} %fusion.49), calls=%async_computation | async-start | bytes 2097152 | tf_op jit(solution)/shard_map/all_to_all | solution.py:162
  96.3 21.9 %copy-start.16 = (s32[1,32,6]{1,0,2:T(1,128)S(1)}, s32[1,32,6]{1,0,2:T(1,128)}, u32[]{:S(2)}) copy-start(s32[1,32,6]{1,0,2:T(1,128)} %param.14) | copy-start | bytes 2308
  113.5 21.9 %all-to-all-start.2 = ((bf16[128,32,128]{0,2,1:T(8,128)(2,1)}), bf16[128,32,128]{0,2,1:T(8,128)(2,1)}, u32[]{:S(2)}, u32[]{:S(2)}) async-start(bf16[128,32,128]{0,2,1:T(8,128)(2,1)} %bitcast.261), calls=%async_computation.2 | async-start | bytes 2097152 | tf_op jit(solution)/shard_map/all_to_all | solution.py:165
  135.4 4.2 copy-start
  147.6 2.3 copy-start.14
  147.7 2.3 copy-start.2
  154.4 6.6 %copy-start.3 = (f32[1,32,128,128]{3,1,2,0:T(8,128)}, f32[1,32,128,128]{3,1,2,0:T(8,128)S(1)}, u32[]{:S(2)}) copy-start(f32[1,32,128,128]{3,1,2,0:T(8,128)S(1)} %bitcast_add_fusion.5) | copy-start | bytes 6291460 | tf_op jit(solution)/shard_map/vmap()/while
  156.2 4.8 %copy-start.1 = (bf16[1,32,128,128]{3,2,1,0:T(8,128)(2,1)S(1)}, bf16[1,32,128,128]{3,2,1,0:T(8,128)(2,1)}, u32[]{:S(2)}) copy-start(bf16[1,32,128,128]{3,2,1,0:T(8,128)(2,1)} %copy-done) | copy-start | bytes 3145732 | tf_op jit(solution)/shard_map/vmap()/while
  161.0 4.2 copy-start
  173.3 2.3 copy-start.14
  173.3 2.3 copy-start.2
  180.0 8.2 %copy-start.3 = (f32[1,32,128,128]{3,1,2,0:T(8,128)}, f32[1,32,128,128]{3,1,2,0:T(8,128)S(1)}, u32[]{:S(2)}) copy-start(f32[1,32,128,128]{3,1,2,0:T(8,128)S(1)} %bitcast_add_fusion.5) | copy-start | bytes 6291460 | tf_op jit(solution)/shard_map/vmap()/while
  181.8 6.5 %copy-start.1 = (bf16[1,32,128,128]{3,2,1,0:T(8,128)(2,1)S(1)}, bf16[1,32,128,128]{3,2,1,0:T(8,128)(2,1)}, u32[]{:S(2)}) copy-start(bf16[1,32,128,128]{3,2,1,0:T(8,128)(2,1)} %copy-done) | copy-start | bytes 3145732 | tf_op jit(solution)/shard_map/vmap()/while
  188.2 4.2 copy-start
  200.5 2.3 copy-start.2
  207.3 8.2 %copy-start.3 = (f32[1,32,128,128]{3,1,2,0:T(8,128)}, f32[1,32,128,128]{3,1,2,0:T(8,128)S(1)}, u32[]{:S(2)}) copy-start(f32[1,32,128,128]{3,1,2,0:T(8,128)S(1)} %bitcast_add_fusion.5) | copy-start | bytes 6291460 | tf_op jit(solution)/shard_map/vmap()/while
  209.1 6.5 %copy-start.1 = (bf16[1,32,128,128]{3,2,1,0:T(8,128)(2,1)S(1)}, bf16[1,32,128,128]{3,2,1,0:T(8,128)(2,1)}, u32[]{:S(2)}) copy-start(bf16[1,32,128,128]{3,2,1,0:T(8,128)(2,1)} %copy-done) | copy-start | bytes 3145732 | tf_op jit(solution)/shard_map/vmap()/while
  215.5 4.2 copy-start
  227.8 2.3 copy-start.2
  234.6 8.2 %copy-start.3 = (f32[1,32,128,128]{3,1,2,0:T(8,128)}, f32[1,32,128,128]{3,1,2,0:T(8,128)S(1)}, u32[]{:S(2)}) copy-start(f32[1,32,128,128]{3,1,2,0:T(8,128)S(1)} %bitcast_add_fusion.5) | copy-start | bytes 6291460 | tf_op jit(solution)/shard_map/vmap()/while
  236.3 6.5 %copy-start.1 = (bf16[1,32,128,128]{3,2,1,0:T(8,128)(2,1)S(1)}, bf16[1,32,128,128]{3,2,1,0:T(8,128)(2,1)}, u32[]{:S(2)}) copy-start(bf16[1,32,128,128]{3,2,1,0:T(8,128)(2,1)} %copy-done) | copy-start | bytes 3145732 | tf_op jit(solution)/shard_map/vmap()/while
  250.0 21.1 %all-to-all-start.4 = ((bf16[32,128,128]{1,2,0:T(8,128)(2,1)}), bf16[32,128,128]{1,2,0:T(8,128)(2,1)S(1)}, u32[]{:S(2)}, u32[]{:S(2)}) async-start(bf16[32,128,128]{1,2,0:T(8,128)(2,1)} %copy.138), calls=%async_computation.4 | async-start | bytes 2097152 | tf_op jit(solution)/shard_map/all_to_all | solution.py:187
  272.1 4.9 %copy-start.4 = (f32[1,32,128,128]{3,1,2,0:T(8,128)S(1)}, f32[1,32,128,128]{3,1,2,0:T(8,128)}, u32[]{:S(2)}) copy-start(f32[1,32,128,128]{3,1,2,0:T(8,128)} %get-tuple-element.66) | copy-start | bytes 6291460
  272.1 33.2 %all-to-all-start.5 = ((f32[32,128,128]{2,1,0:T(8,128)}), f32[32,128,128]{2,1,0:T(8,128)}, u32[]{:S(2)}, u32[]{:S(2)}) async-start(f32[32,128,128]{2,1,0:T(8,128)} %bitcast.258), calls=%async_computation.5 | async-start | bytes 4194304 | tf_op jit(solution)/shard_map/all_to_all | solution.py:189
  305.3 6.0 %copy-start.8 = (bf16[1,128,4096]{1,2,0:T(8,128)(2,1)S(1)}, bf16[1,128,4096]{1,2,0:T(8,128)(2,1)}, u32[]{:S(2)}) copy-start(bf16[1,128,4096]{1,2,0:T(8,128)(2,1)} %copy.127) | copy-start | bytes 3145732
  305.3 34.2 %all-to-all-start.6 = ((f32[32,128,128]{2,1,0:T(8,128)}), f32[32,128,128]{2,1,0:T(8,128)S(1)}, u32[]{:S(2)}, u32[]{:S(2)}) async-start(f32[32,128,128]{2,1,0:T(8,128)} %bitcast.265), calls=%async_computation.6 | async-start | bytes 4194304 | tf_op jit(solution)/shard_map/all_to_all | solution.py:190
  318.8 2.8 copy-start.10
  321.8 18.9 %copy-start.12 = (f32[128,8,128]{0,2,1:T(8,128)S(1)}, f32[128,8,128]{0,2,1:T(8,128)}, u32[]{:S(2)}) copy-start(f32[128,8,128]{0,2,1:T(8,128)} %copy.141) | copy-start | bytes 1572868
  (13 other events, 20.6 us)
where the time goes:
time: 446 us; the launch traced here: 444 us
  blocking collectives  131 us (29%)
  waiting for transfers between devices  113 us (25%)
  matrix products  83.9 us (19%)
  local copies, waits for them, and re-layouts  45.1 us (10%)
  starting transfers between devices  42.8 us (10%)
  other arithmetic  22.9 us (5%)
    psum x1, blocking collectives, shards(): q_total, k_total = lax.psum((q_part, k_part), ('seq', 'dp'))  101 us
    unnamed x1, blocking collectives  30.3 us
    dot_general x4, matrix products, one_group(): jnp.einsum('gsn,gskd->nkd', one_hot, key_pieces, precision=top_precision)  24.1 us
    all_to_all x1, waiting for transfers between devices, shards(): lax.all_to_all(dk_heads, 'seq', split_axis=0, concat_axis=1, tiled=True)  24 us
    dot_general x4, matrix products, one_group(): jnp.einsum('gsn,gskd->nkd', one_hot, value_pieces, precision=top_precision)  17.8 us
    all_to_all x1, waiting for transfers between devices, shards(): lax.all_to_all(dv_heads, 'seq', split_axis=0, concat_axis=1, tiled=True)  17.8 us
    all_to_all x1, waiting for transfers between devices, shards(): lax.all_to_all(d_context[0], 'seq', split_axis=1, concat_axis=0, tiled=True)  17 us
    all_to_all x1, waiting for transfers between devices, shards(): lax.all_to_all(k_wide, 'seq', split_axis=1, concat_axis=0, tiled=True)  16.9 us
  transfers between devices with their start and end apart: 7, of which 7 were waited for; matrix products, arithmetic and copies ran while one was open for 6% of the time, Pallas kernels for 0%

commit v1 on v0

v1 whole, which is shorter than its diff:
```python
import functools
import math

import jax
import jax.numpy as jnp
from jax import lax
from jax.experimental import pallas as pl
from jax.experimental.pallas import tpu as pltpu
from jax.sharding import PartitionSpec as P

BLK = 128
HD = 128
HALF = BLK // 2
SLOTS = 6
TAIL = 16
EPSILON = 1e-06

F32 = jnp.float32
BF16 = jnp.bfloat16
NT = (((1,), (1,)), ((), ()))
NN = (((1,), (0,)), ((), ()))

VMEM_SPEC = pl.BlockSpec(memory_space=pltpu.VMEM)
SMEM_SPEC = pl.BlockSpec(memory_space=pltpu.SMEM)
ANY_SPEC = pl.BlockSpec(memory_space=pl.ANY)


def run_copies(copies):
    for copy in copies:
        copy.start()
    for copy in copies:
        copy.wait()


def pack_kv_kernel(heads, k_ref, v_ref, out_ref, sems):
    copies = []
    for h in range(heads):
        rows = pl.ds((h % 2) * HALF, HALF)
        cols = pl.ds((h // 4) * HD, HD)
        copies.append(
            pltpu.make_async_copy(k_ref.at[0, rows, cols], out_ref.at[h, pl.ds(0, HALF)], sems.at[2 * h])
        )
        copies.append(
            pltpu.make_async_copy(
                v_ref.at[0, rows, cols], out_ref.at[h, pl.ds(HALF, HALF)], sems.at[2 * h + 1]
            )
        )
    run_copies(copies)


def pack_qd_kernel(heads, q_ref, d_ref, out_ref, sems):
    copies = []
    for h in range(heads):
        cols = pl.ds(h * HD, HD)
        copies.append(
            pltpu.make_async_copy(q_ref.at[0, :, cols], out_ref.at[h, pl.ds(0, BLK)], sems.at[2 * h])
        )
        copies.append(
            pltpu.make_async_copy(d_ref.at[0, :, cols], out_ref.at[h, pl.ds(BLK, BLK)], sems.at[2 * h + 1])
        )
    run_copies(copies)


def inverse_rms(values):
    return lax.rsqrt(jnp.mean(values * values, axis=-1, keepdims=True) + EPSILON)


def prep_kernel(blocks, own_ref, other_ref, gains_ref, kv_ref, kt_ref, khat_ref):
    core = lax.rem(lax.axis_index("seq"), 2)
    own = pl.multiple_of(core * HALF, HALF)
    other = pl.multiple_of((1 - core) * HALF, HALF)
    k_gain = gains_ref[1:2, :]

    def one_block(j, carry):
        for ref, start in ((own_ref, own), (other_ref, other)):
            values = ref[j, 0:HALF, :].astype(F32)
            hat = values * inverse_rms(values)
            khat_ref[j, pl.ds(start, HALF), :] = hat
            kv_ref[j, pl.ds(start, HALF), 0:HD] = (hat * k_gain).astype(BF16)
            kv_ref[j, pl.ds(start, HALF), HD : 2 * HD] = ref[j, HALF:BLK, :]
        kt_ref[j] = kv_ref[j, :, 0:HD].T
        return carry

    lax.fori_loop(0, blocks, one_block, 0, unroll=2)


def attend_kernel(
    blocks, dp_count, pat_ref, gains_ref, qd_ref, kv_ref, kt_ref, khat_ref,
    dq_ref, keep_ref, give_ref, gain_ref, acc_ref, lead_ref,
):
    core = lax.rem(lax.axis_index("seq"), 2)
    q_gain = gains_ref[0:1, :]
    scale = 1.0 / math.sqrt(HD)
    scale2 = scale * math.log2(math.e)
    zeros = jnp.zeros((BLK, HD), BF16)

    def load_query(b):
        q_raw = qd_ref[b, 0:BLK, :].astype(F32)
        d_low = qd_ref[b, BLK : 2 * BLK, :]
        q_inv = inverse_rms(q_raw)
        q_hat = q_raw * q_inv
        q_low = (q_hat * q_gain).astype(BF16)
        pair = jnp.concatenate(
            [jnp.concatenate([q_low, zeros], axis=1), jnp.concatenate([zeros, d_low], axis=1)], axis=0
        )
        return q_raw, q_inv, q_hat, pair

    def store_query(b, q_raw, q_inv, q_hat, dq_t):
        dq = dq_t.T.astype(BF16).astype(F32)
        scaled = q_gain * dq
        total = jnp.sum(scaled * q_raw, axis=-1, keepdims=True)
        grad = q_inv * scaled - q_inv * q_inv * q_inv * q_raw * total / HD
        dq_ref[b] = grad.astype(BF16)
        return jnp.sum((dq * q_hat).reshape(BLK // 8, 8, HD), axis=0)

    q_raw, q_inv, q_hat, pair = load_query(0)
    chunk = 8

    def lead_scores(i, peak):
        rows = kv_ref[pl.ds(i * chunk, chunk)].reshape(chunk * BLK, 2 * HD)
        both = lax.dot_general(rows, pair, NT, preferred_element_type=F32)
        scores = both[:, 0:BLK] * scale2
        start = pl.multiple_of(i * chunk * BLK, chunk * BLK)
        lead_ref[pl.ds(start, chunk * BLK), 0:BLK] = scores
        lead_ref[pl.ds(start, chunk * BLK), BLK : 2 * BLK] = both[:, BLK : 2 * BLK]
        return jnp.maximum(peak, jnp.max(scores.reshape(chunk * BLK // 8, 8, BLK), axis=0))

    peak = lax.fori_loop(0, blocks // chunk, lead_scores, jnp.full((8, BLK), -jnp.inf, F32))
    peak = jnp.max(peak, axis=0, keepdims=True)

    def lead_exp(i, sums):
        start = pl.multiple_of(i * chunk * BLK, chunk * BLK)
        raised = jnp.exp2(lead_ref[pl.ds(start, chunk * BLK), 0:BLK] - peak)
        lead_ref[pl.ds(start, chunk * BLK), 0:BLK] = raised
        product = raised * lead_ref[pl.ds(start, chunk * BLK), BLK : 2 * BLK]
        return (
            sums[0] + jnp.sum(raised.reshape(chunk * BLK // 8, 8, BLK), axis=0),
            sums[1] + jnp.sum(product.reshape(chunk * BLK // 8, 8, BLK), axis=0),
        )

    zero8 = jnp.zeros((8, BLK), F32)
    total, delta = lax.fori_loop(0, blocks // chunk, lead_exp, (zero8, zero8))
    inv_total = 1.0 / jnp.sum(total, axis=0, keepdims=True)
    delta = jnp.sum(delta, axis=0, keepdims=True) * inv_total

    def lead_grad(i, dq_t):
        start = pl.multiple_of(i * chunk * BLK, chunk * BLK)
        weights = lead_ref[pl.ds(start, chunk * BLK), 0:BLK] * inv_total
        d_weights = lead_ref[pl.ds(start, chunk * BLK), BLK : 2 * BLK]
        d_low = (weights * (d_weights - delta) * scale).astype(BF16)
        both = jnp.concatenate([d_low, weights.astype(BF16)], axis=1)
        terms = lax.dot_general(both, pair, NN, preferred_element_type=F32)
        acc_ref[pl.ds(i * chunk, chunk)] = terms.reshape(chunk, BLK, 2 * HD)
        keys = jnp.concatenate([kt_ref[i * chunk + t] for t in range(chunk)], axis=1)
        return dq_t + lax.dot_general(keys, d_low, NN, preferred_element_type=F32)

    dq_t = lax.fori_loop(0, blocks // chunk, lead_grad, jnp.zeros((HD, BLK), F32))
    q_part = store_query(0, q_raw, q_inv, q_hat, dq_t)

    def sparse_block(b, q_part):
        named = [pat_ref[0, b, s] for s in range(SLOTS)]
        index = [jnp.maximum(n, 0) for n in named]
        bias = []
        for s in range(SLOTS):
            kept = named[s] >= 0
            for t in range(s):
                kept = jnp.logical_and(kept, named[s] != named[t])
            bias.append(jnp.where(kept, 0.0, -jnp.inf).astype(F32))
        q_raw, q_inv, q_hat, pair = load_query(b)
        rows = jnp.concatenate([kv_ref[i] for i in index], axis=0)
        both = lax.dot_general(rows, pair, NT, preferred_element_type=F32)
        scores = [both[s * BLK : (s + 1) * BLK, 0:BLK] * scale2 + bias[s] for s in range(SLOTS)]
        d_weights = [both[s * BLK : (s + 1) * BLK, BLK : 2 * BLK] for s in range(SLOTS)]
        peak = functools.reduce(jnp.maximum, scores)
        peak = jnp.max(peak, axis=0, keepdims=True)
        raised = [jnp.exp2(x - peak) for x in scores]
        inv_total = 1.0 / jnp.sum(functools.reduce(jnp.add, raised), axis=0, keepdims=True)
        products = functools.reduce(jnp.add, [x * y for x, y in zip(raised, d_weights)])
        delta = jnp.sum(products, axis=0, keepdims=True) * inv_total
        weights = [x * inv_total for x in raised]
        d_low = [(x * (y - delta) * scale).astype(BF16) for x, y in zip(weights, d_weights)]
        stacked = jnp.concatenate(
            [jnp.concatenate([x, y.astype(BF16)], axis=1) for x, y in zip(d_low, weights)], axis=0
        )
        terms = lax.dot_general(stacked, pair, NN, preferred_element_type=F32)
        keys = jnp.concatenate([kt_ref[i] for i in index], axis=1)
        dq_t = lax.dot_general(keys, jnp.concatenate(d_low, axis=0), NN, preferred_element_type=F32)
        for s in range(SLOTS):
            acc_ref[index[s]] += terms[s * BLK : (s + 1) * BLK]
        return q_part + store_query(b, q_raw, q_inv, q_hat, dq_t)

    q_part = lax.fori_loop(1, blocks, sparse_block, q_part)

    own = pl.multiple_of(core * HALF, HALF)
    other = pl.multiple_of((1 - core) * HALF, HALF)

    def finish(j, k_part):
        keep_ref[j, 0:HALF, :] = acc_ref[j, pl.ds(own, HALF), 0:HD]
        keep_ref[j, HALF:BLK, :] = acc_ref[j, pl.ds(own, HALF), HD : 2 * HD]
        give_ref[j, 0:HALF, :] = acc_ref[j, pl.ds(other, HALF), 0:HD].astype(BF16)
        give_ref[j, HALF:BLK, :] = acc_ref[j, pl.ds(other, HALF), HD : 2 * HD].astype(BF16)
        product = acc_ref[j, :, 0:HD] * khat_ref[j]
        return k_part + jnp.sum(product.reshape(BLK // 8, 8, HD), axis=0)

    k_part = lax.fori_loop(0, blocks, finish, jnp.zeros((8, HD), F32), unroll=2)
    parts = jnp.concatenate(
        [
            jnp.sum(q_part, axis=0, keepdims=True),
            jnp.sum(k_part, axis=0, keepdims=True),
            jnp.zeros((6, HD), F32),
        ],
        axis=0,
    )
    for z in range(dp_count):
        gain_ref[z] = parts


def merge_kernel(blocks, keep_ref, got_ref, gain_ref, out_ref):
    parts = jnp.sum(gain_ref[...], axis=0)
    high = parts.astype(BF16).astype(F32)
    rest = parts - high
    middle = rest.astype(BF16).astype(F32)
    low = rest - middle
    tail = jnp.concatenate(
        [high[0:2], middle[0:2], low[0:2], jnp.zeros((TAIL - 6, HD), F32)], axis=0
    ).astype(BF16)

    def one_block(j, carry):
        out_ref[j, 0:BLK, :] = (keep_ref[j] + got_ref[j].astype(F32)).astype(BF16)
        out_ref[j, BLK : BLK + TAIL, :] = tail
        return carry

    lax.fori_loop(0, blocks, one_block, 0, unroll=4)


def unpack_q_kernel(heads, in_ref, out_ref, sems):
    run_copies(
        [
            pltpu.make_async_copy(in_ref.at[h], out_ref.at[0, :, pl.ds(h * HD, HD)], sems.at[h])
            for h in range(heads)
        ]
    )


def final_kernel(heads, in_ref, k_ref, gains_ref, k_grad_ref, v_grad_ref, gain_ref):
    k_gain = gains_ref[1:2, :]
    for g in range(heads // 4):
        for core in range(2):
            first, second = 4 * g + core, 4 * g + 2 + core
            rows = pl.ds(core * HALF, HALF)
            cols = pl.ds(g * HD, HD)
            d_k = in_ref[first, 0:HALF, :].astype(F32) + in_ref[second, 0:HALF, :].astype(F32)
            d_v = in_ref[first, HALF:BLK, :].astype(F32) + in_ref[second, HALF:BLK, :].astype(F32)
            v_grad_ref[0, rows, cols] = d_v.astype(BF16)
            values = k_ref[0, rows, cols].astype(F32)
            inverse = inverse_rms(values)
            scaled = k_gain * d_k.astype(BF16).astype(F32)
            total = jnp.sum(scaled * values, axis=-1, keepdims=True)
            grad = inverse * scaled - inverse * inverse * inverse * values * total / HD
            k_grad_ref[0, rows, cols] = grad.astype(BF16)
    tails = in_ref[0, BLK : BLK + TAIL, :].astype(F32)
    for s in range(1, heads):
        tails += in_ref[s, BLK : BLK + TAIL, :].astype(F32)
    sums = tails[0:2] + tails[2:4] + tails[4:6]
    shift = lax.rem(HD - 8 * lax.axis_index("dp"), HD)
    gain_ref[...] = pltpu.roll(jnp.concatenate([sums, jnp.zeros((6, HD), F32)], axis=0), shift, 1)


def struct(shape, dtype):
    return jax.ShapeDtypeStruct(shape, dtype)


def shards(heads, dp_count, q_raw, k_raw, v_raw, q_gain, k_gain, key_blocks, d_context):
    blocks = heads
    gain_slices = jnp.concatenate([q_gain[None], k_gain[None]], axis=0)
    gain_all = lax.all_to_all(
        jnp.broadcast_to(gain_slices[None], (dp_count,) + gain_slices.shape), "dp", 0, 0, tiled=True
    )
    gains = jnp.transpose(gain_all, (1, 0, 2)).reshape(2, HD)

    kv_send = pl.pallas_call(
        functools.partial(pack_kv_kernel, heads),
        out_shape=struct((heads, BLK, HD), BF16),
        in_specs=[ANY_SPEC] * 2,
        out_specs=VMEM_SPEC,
        scratch_shapes=[pltpu.SemaphoreType.DMA((2 * heads,))],
        name="pack_kv",
    )(k_raw, v_raw)
    kv_own = lax.all_to_all(kv_send, "seq", 0, 0, tiled=True)
    swap = [(s, s ^ 1) for s in range(heads)]
    kv_other = lax.ppermute(kv_own, "seq", swap)

    qd_send = pl.pallas_call(
        functools.partial(pack_qd_kernel, heads),
        out_shape=struct((heads, 2 * BLK, HD), BF16),
        in_specs=[ANY_SPEC] * 2,
        out_specs=VMEM_SPEC,
        scratch_shapes=[pltpu.SemaphoreType.DMA((2 * heads,))],
        name="pack_qd",
    )(q_raw, d_context)
    qd = lax.all_to_all(qd_send, "seq", 0, 0, tiled=True)

    kv, kt, khat = pl.pallas_call(
        functools.partial(prep_kernel, blocks),
        out_shape=(
            struct((blocks, BLK, 2 * HD), BF16),
            struct((blocks, HD, BLK), BF16),
            struct((blocks, BLK, HD), F32),
        ),
        in_specs=[VMEM_SPEC] * 3,
        out_specs=(VMEM_SPEC,) * 3,
        name="prep",
    )(kv_own, kv_other, gains)

    q_grad_heads, keep, give, gain_terms = pl.pallas_call(
        functools.partial(attend_kernel, blocks, dp_count),
        out_shape=(
            struct((blocks, BLK, HD), BF16),
            struct((blocks, BLK, HD), F32),
            struct((blocks, BLK, HD), BF16),
            struct((dp_count, 8, HD), F32),
        ),
        in_specs=[SMEM_SPEC] + [VMEM_SPEC] * 5,
        out_specs=(VMEM_SPEC,) * 4,
        scratch_shapes=[
            pltpu.VMEM((blocks, BLK, 2 * HD), F32),
            pltpu.VMEM((blocks * BLK, 2 * BLK), F32),
        ],
        name="attend",
    )(key_blocks, gains, qd, kv, kt, khat)

    got = lax.ppermute(give, "seq", swap)
    q_back = lax.all_to_all(q_grad_heads, "seq", 0, 0, tiled=True)
    gain_terms = lax.all_to_all(gain_terms, "dp", 0, 0, tiled=True)

    kv_terms = pl.pallas_call(
        functools.partial(merge_kernel, blocks),
        out_shape=struct((blocks, BLK + TAIL, HD), BF16),
        in_specs=[VMEM_SPEC] * 3,
        out_specs=VMEM_SPEC,
        name="merge",
    )(keep, got, gain_terms)
    kv_back = lax.all_to_all(kv_terms, "seq", 0, 0, tiled=True)

    q_grad = pl.pallas_call(
        functools.partial(unpack_q_kernel, heads),
        out_shape=struct((1, BLK, heads * HD), BF16),
        in_specs=[VMEM_SPEC],
        out_specs=ANY_SPEC,
        scratch_shapes=[pltpu.SemaphoreType.DMA((heads,))],
        name="unpack_q",
    )(q_back)

    k_grad, v_grad, totals = pl.pallas_call(
        functools.partial(final_kernel, heads),
        out_shape=(
            struct(k_raw.shape, BF16),
            struct(v_raw.shape, BF16),
            struct((8, HD), F32),
        ),
        in_specs=[VMEM_SPEC] * 3,
        out_specs=(VMEM_SPEC,) * 3,
        name="final",
    )(kv_back, k_raw, gains)
    width = q_gain.shape[0]
    return (q_grad, k_grad, v_grad, totals[0, :width], totals[1, :width])


def solution(mesh):
    placed = (
        P("dp", "seq", None),
        P("dp", "seq", None),
        P("dp", "seq", None),
        P("dp"),
        P("dp"),
        P("seq", None, None),
        P("dp", "seq", None),
    )
    return jax.shard_map(
        functools.partial(shards, mesh.shape["seq"], mesh.shape["dp"]),
        mesh=mesh,
        in_specs=placed,
        out_specs=(
            P("dp", "seq", None),
            P("dp", "seq", None),
            P("dp", "seq", None),
            P("dp"),
            P("dp"),
        ),
        check_vma=False,
    )
```

time: 446 us -> 203 us (0.46)
  blocking collectives: 131 us -> 0 us
  matrix products: 83.9 us -> 0 us
  Pallas kernels: 0 us -> 67.7 us
  local copies, waits for them, and re-layouts: 45.1 us -> 6.64 us
  waiting for transfers between devices: 113 us -> 76.6 us
  other arithmetic: 22.9 us -> 0.68 us
  starting transfers between devices: 42.8 us -> 49.6 us
    psum x1 -> x0, blocking collectives: 101 us -> none  [shards(): q_total, k_total = lax.psum((q_part, k_part), ('seq', 'dp'))]
    dot_general x33 -> x0, matrix products: 83.9 us -> none  [the longest x4 24.1 us: one_group(): jnp.einsum('gsn,gskd->nkd', one_hot, key_pieces, precision=top_precision)]
    pallas_call x0 -> x7, Pallas kernels: none -> 67.7 us  [the longest x1 46.4 us: shards(): pl.pallas_call(functools.partial(attend_kernel, blocks, dp_count), out_sh...]
    all_to_all x7 -> x6, waiting for transfers between devices: 113 us -> 75.5 us  [the longest x1 16.6 us: shards(): qd = lax.all_to_all(qd_send, 'seq', 0, 0, tiled=True)]
    unnamed x1 -> x0, blocking collectives: 30.3 us -> none
    gather x20 -> x0, local copies, waits for them, and re-layouts: 12.2 us -> none  [the longest x4 7.9 us: one_group(): selected_values = v_tiles[chosen]]
    unnamed x32 -> x15, local copies, waits for them, and re-layouts: 14 us -> 4.06 us
    reduce_sum x13 -> x0, other arithmetic: 9.45 us -> none  [the longest x5 3.7 us: softmax_rows(): return raised / jnp.sum(raised, axis=axes, keepdims=True)]
  transfers between devices with their start and end apart: 7 -> 8, of which waited for: 7 -> 7; matrix products, arithmetic and copies ran while one was open for 6% -> 1% of each run, Pallas kernels for 0% -> 9%
where the time goes in v1:
time: 203 us; the launch traced here: 202 us
  waiting for transfers between devices  76.6 us (38%)
  Pallas kernels  67.7 us (33%)
  starting transfers between devices  49.6 us (24%)
  local copies, waits for them, and re-layouts  6.64 us (3%)
    pallas_call x1, Pallas kernels, shards(): pl.pallas_call(functools.partial(attend_kernel, blocks, dp_count), out_sh...  46.4 us
    all_to_all x1, waiting for transfers between devices, shards(): qd = lax.all_to_all(qd_send, 'seq', 0, 0, tiled=True)  16.6 us
    all_to_all x1, waiting for transfers between devices, shards(): kv_back = lax.all_to_all(kv_terms, 'seq', 0, 0, tiled=True)  16.2 us
    all_to_all x1, starting transfers between devices, shards(): lax.all_to_all(jnp.broadcast_to(gain_slices[None], (dp_count,) + gain_sli...  15.7 us
    all_to_all x1, waiting for transfers between devices, shards(): kv_own = lax.all_to_all(kv_send, 'seq', 0, 0, tiled=True)  13.6 us
    all_to_all x1, waiting for transfers between devices, shards(): q_back = lax.all_to_all(q_grad_heads, 'seq', 0, 0, tiled=True)  13 us
    all_to_all x1, starting transfers between devices, shards(): kv_own = lax.all_to_all(kv_send, 'seq', 0, 0, tiled=True)  9.16 us
    all_to_all x1, waiting for transfers between devices, shards(): lax.all_to_all(jnp.broadcast_to(gain_slices[None], (dp_count,) + gain_sli...  8.65 us
  transfers between devices with their start and end apart: 8, of which 7 were waited for; matrix products, arithmetic and copies ran while one was open for 1% of the time, Pallas kernels for 9%

profile of v1, /device:TPU:1, one launch (start us, length us, event | category | flops | bytes accessed | tf_op | source)
XLA Modules:
  0.0 202.1 jit_solution(18397849431815049834)
XLA Ops:
  0.6 0.7 pad_maximum_fusion
  1.3 0.6 broadcast_in_dim.14
  1.9 15.7 %all-to-all-start = ((f32[16,2,8]{2,1,0:T(2,128)}), f32[16,2,8]{2,1,0:T(2,128)S(1)}, u32[]{:S(2)}, u32[]{:S(2)}) async-start(f32[16,2,8]{2,1,0:T(2,128)} %broadcast_in_dim.14), calls=%async_computation | async-start | bytes 32768 | tf_op jit(solution)/shard_map/all_to_all | solution.py:276
  17.7 2.7 %pack_kv.1 = bf16[32,128,128]{2,1,0:T(8,128)(2,1)} custom-call(bf16[1,128,1024]{2,1,0:T(8,128)(2,1)} %k_ref.3, bf16[1,128,1024]{2,1,0:T(8,128)(2,1)} %v_ref.1), custom_call_target="tpu_custom_call" | custom-call | tf_op jit(solution)/shard_map/pack_kv/pallas_call | solution.py:281
  20.4 8.7 %all-to-all-done = f32[16,2,8]{2,1,0:T(2,128)S(1)} async-done(((f32[16,2,8]{2,1,0:T(2,128)}), f32[16,2,8]{2,1,0:T(2,128)S(1)}, u32[]{:S(2)}, u32[]{:S(2)}) %all-to-all-start) | async-done | bytes 1056 | tf_op jit(solution)/shard_map/all_to_all | solution.py:276
  29.1 9.2 %all-to-all-start.2 = ((bf16[32,128,128]{2,1,0:T(8,128)(2,1)}), bf16[32,128,128]{2,1,0:T(8,128)(2,1)S(1)}, u32[]{:S(2)}, u32[]{:S(2)}) async-start(bf16[32,128,128]{2,1,0:T(8,128)(2,1)} %pack_kv.1), calls=%async_computation.2 | async-start | bytes 2097152 | tf_op jit(solution)/shard_map/all_to_all | solution.py:289
  38.2 3.4 %pack_qd.1 = bf16[32,256,128]{2,1,0:T(8,128)(2,1)} custom-call(bf16[1,128,4096]{2,1,0:T(8,128)(2,1)} %q_ref.1, bf16[1,128,4096]{2,1,0:T(8,128)(2,1)} %d_ref.1), custom_call_target="tpu_custom_call" | custom-call | tf_op jit(solution)/shard_map/pack_qd/pallas_call | solution.py:293
  41.7 0.0 copy-start.6
  41.7 13.6 %all-to-all-done.2.own_ref = bf16[32,128,128]{2,1,0:T(8,128)(2,1)S(1)} async-done(((bf16[32,128,128]{2,1,0:T(8,128)(2,1)}), bf16[32,128,128]{2,1,0:T(8,128)(2,1)S(1)}, u32[]{:S(2)}, u32[]{:S(2)}) %all-to-all-start.2) | async-done | bytes 1048608 | tf_op jit(solution)/shard_map/all_to_all | solution.py:289
  55.3 4.1 %all-to-all-start.1 = ((bf16[32,256,128]{2,1,0:T(8,128)(2,1)}), bf16[32,256,128]{2,1,0:T(8,128)(2,1)S(1)}, u32[]{:S(2)}, u32[]{:S(2)}) async-start(bf16[32,256,128]{2,1,0:T(8,128)(2,1)} %pack_qd.1), calls=%async_computation.1 | async-start | bytes 4194304 | tf_op jit(solution)/shard_map/all_to_all | solution.py:301
  59.3 2.3 %collective-permute-start = (bf16[32,128,128]{2,1,0:T(8,128)(2,1)S(1)}, bf16[32,128,128]{2,1,0:T(8,128)(2,1)}, u32[]{:S(2)}, u32[]{:S(2)}) collective-permute-start(bf16[32,128,128]{2,1,0:T(8,128)(2,1)S(1)} %all-to-all-done.2.own_ref), channel_id=1, source_target_pairs={{0,16},{16,0},{32,48},{48,32},{64,80},{80,64},{96,112},{112,96},{1... | collective-permute-start | bytes 3145736 | tf_op jit(solution)/shard_map/ppermute | solution.py:291
  61.6 0.7 copy.15.pat_ref
  62.3 0.7 reshape.14.gains_ref
  63.0 1.0 collective-permute-done.other_ref
  64.0 7.1 %prep.1 = (bf16[32,128,256]{2,1,0:T(8,128)(2,1)}, bf16[32,128,128]{2,1,0:T(8,128)(2,1)}, f32[32,128,128]{2,1,0:T(8,128)}) custom-call(bf16[32,128,128]{2,1,0:T(8,128)(2,1)} %copy-done.3, bf16[32,128,128]{2,1,0:T(8,128)(2,1)} %collective-permute-done.other_ref, f32[2,128]{1,0:T(2,128)} %reshape.14.gains_ref), custom_call_target="tpu_custom_call" | custom-call | tf_op jit(solution)/shard_map/prep/pallas_call | solution.py:303
  71.1 16.6 %all-to-all-done.1.qd_ref = bf16[32,256,128]{2,1,0:T(8,128)(2,1)S(1)} async-done(((bf16[32,256,128]{2,1,0:T(8,128)(2,1)}), bf16[32,256,128]{2,1,0:T(8,128)(2,1)S(1)}, u32[]{:S(2)}, u32[]{:S(2)}) %all-to-all-start.1) | async-done | bytes 2097184 | tf_op jit(solution)/shard_map/all_to_all | solution.py:301
  87.7 1.4 copy-done
  89.0 46.4 %attend.1 = (bf16[32,128,128]{2,1,0:T(8,128)(2,1)}, f32[32,128,128]{2,1,0:T(8,128)}, bf16[32,128,128]{2,1,0:T(8,128)(2,1)}, f32[16,8,128]{2,1,0:T(8,128)}) custom-call(s32[1,32,6]{2,1,0:T(8,128)} %copy.15.pat_ref, f32[2,128]{1,0:T(2,128)} %reshape.14.gains_ref, bf16[32,256,128]{2,1,0:T(8,128)(2,1)} %copy-done, ...), custom_call_target="tpu_custom_call" | custom-call | tf_op jit(solution)/shard_map/attend/pallas_call | solution.py:315
  135.4 3.5 %all-to-all-start.4 = ((f32[16,8,128]{2,1,0:T(8,128)}), f32[16,8,128]{2,1,0:T(8,128)S(1)}, u32[]{:S(2)}, u32[]{:S(2)}) async-start(f32[16,8,128]{2,1,0:T(8,128)} %get-tuple-element.21), calls=%async_computation.4 | async-start | bytes 131072 | tf_op jit(solution)/shard_map/all_to_all | solution.py:334
  138.9 4.0 %collective-permute-start.1 = (bf16[32,128,128]{2,1,0:T(8,128)(2,1)}, bf16[32,128,128]{2,1,0:T(8,128)(2,1)S(1)}, u32[]{:S(2)}, u32[]{:S(2)}) collective-permute-start(bf16[32,128,128]{2,1,0:T(8,128)(2,1)} %get-tuple-element.20), channel_id=1, source_target_pairs={{0,16},{16,0},{32,48},{48,32},{64,80},{80,64},{96,112},{112,96},{1... | collective-permute-start | bytes 3145736 | tf_op jit(solution)/shard_map/ppermute | solution.py:332
  143.0 7.6 %all-to-all-done.4.gain_ref = f32[16,8,128]{2,1,0:T(8,128)S(1)} async-done(((f32[16,8,128]{2,1,0:T(8,128)}), f32[16,8,128]{2,1,0:T(8,128)S(1)}, u32[]{:S(2)}, u32[]{:S(2)}) %all-to-all-start.4) | async-done | bytes 65568 | tf_op jit(solution)/shard_map/all_to_all | solution.py:334
  150.5 6.9 %all-to-all-start.3 = ((bf16[32,128,128]{2,1,0:T(8,128)(2,1)}), bf16[32,128,128]{2,1,0:T(8,128)(2,1)S(1)}, u32[]{:S(2)}, u32[]{:S(2)}) async-start(bf16[32,128,128]{2,1,0:T(8,128)(2,1)} %get-tuple-element.18), calls=%async_computation.3 | async-start | bytes 2097152 | tf_op jit(solution)/shard_map/all_to_all | solution.py:333
  157.4 0.0 collective-permute-done.1.got_ref
  157.5 1.0 copy-done.4
  158.4 3.2 %merge.1 = bf16[32,144,128]{2,1,0:T(8,128)(2,1)} custom-call(f32[32,128,128]{2,1,0:T(8,128)} %get-tuple-element.19.keep_ref, bf16[32,128,128]{2,1,0:T(8,128)(2,1)} %copy-done.4, f32[16,8,128]{2,1,0:T(8,128)} %copy-done.5), custom_call_target="tpu_custom_call" | custom-call | tf_op jit(solution)/shard_map/merge/pallas_call | solution.py:336
  161.6 13.0 %all-to-all-done.3.in_ref = bf16[32,128,128]{2,1,0:T(8,128)(2,1)S(1)} async-done(((bf16[32,128,128]{2,1,0:T(8,128)(2,1)}), bf16[32,128,128]{2,1,0:T(8,128)(2,1)S(1)}, u32[]{:S(2)}, u32[]{:S(2)}) %all-to-all-start.3) | async-done | bytes 1048608 | tf_op jit(solution)/shard_map/all_to_all | solution.py:333
  174.6 4.0 %all-to-all-start.5 = ((bf16[32,144,128]{2,1,0:T(8,128)(2,1)}), bf16[32,144,128]{2,1,0:T(8,128)(2,1)S(1)}, u32[]{:S(2)}, u32[]{:S(2)}) async-start(bf16[32,144,128]{2,1,0:T(8,128)(2,1)} %merge.1), calls=%async_computation.5 | async-start | bytes 2359296 | tf_op jit(solution)/shard_map/all_to_all | solution.py:343
  178.6 2.5 %unpack_q.1 = bf16[1,128,4096]{2,1,0:T(8,128)(2,1)} custom-call(bf16[32,128,128]{2,1,0:T(8,128)(2,1)} %copy-done.2), custom_call_target="tpu_custom_call" | custom-call | tf_op jit(solution)/shard_map/unpack_q/pallas_call | solution.py:345
  181.1 16.2 %all-to-all-done.5.in_ref = bf16[32,144,128]{2,1,0:T(8,128)(2,1)S(1)} async-done(((bf16[32,144,128]{2,1,0:T(8,128)(2,1)}), bf16[32,144,128]{2,1,0:T(8,128)(2,1)S(1)}, u32[]{:S(2)}, u32[]{:S(2)}) %all-to-all-start.5) | async-done | bytes 1179680 | tf_op jit(solution)/shard_map/all_to_all | solution.py:343
  197.2 1.0 copy-done.1
  198.3 2.5 %final.1 = (bf16[1,128,1024]{2,1,0:T(8,128)(2,1)}, bf16[1,128,1024]{2,1,0:T(8,128)(2,1)}, f32[8,128]{1,0:T(8,128)}) custom-call(bf16[32,144,128]{2,1,0:T(8,128)(2,1)} %copy-done.1, bf16[1,128,1024]{2,1,0:T(8,128)(2,1)} %k_ref.3, f32[2,128]{1,0:T(2,128)} %reshape.14.gains_ref), custom_call_target="tpu_custom_call" | custom-call | tf_op jit(solution)/shard_map/final/pallas_call | solution.py:354
  200.8 1.3 slice_bitcast_fusion
  (11 shorter events, 0.0 us)
Async XLA Ops:
  1.9 27.1 %all-to-all-start = ((f32[16,2,8]{2,1,0:T(2,128)}), f32[16,2,8]{2,1,0:T(2,128)S(1)}, u32[]{:S(2)}, u32[]{:S(2)}) async-start(f32[16,2,8]{2,1,0:T(2,128)} %broadcast_in_dim.14), calls=%async_computation | async-start | bytes 32768 | tf_op jit(solution)/shard_map/all_to_all | solution.py:276
  29.1 26.2 %all-to-all-start.2 = ((bf16[32,128,128]{2,1,0:T(8,128)(2,1)}), bf16[32,128,128]{2,1,0:T(8,128)(2,1)S(1)}, u32[]{:S(2)}, u32[]{:S(2)}) async-start(bf16[32,128,128]{2,1,0:T(8,128)(2,1)} %pack_kv.1), calls=%async_computation.2 | async-start | bytes 2097152 | tf_op jit(solution)/shard_map/all_to_all | solution.py:289
  41.7 19.9 %copy-start.6 = (s32[1,32,6]{1,0,2:T(1,128)S(1)}, s32[1,32,6]{1,0,2:T(1,128)}, u32[]{:S(2)}) copy-start(s32[1,32,6]{1,0,2:T(1,128)} %param.12) | copy-start | bytes 2308
  55.3 7.0 %copy-start.3 = (bf16[32,128,128]{2,1,0:T(8,128)(2,1)}, bf16[32,128,128]{2,1,0:T(8,128)(2,1)S(1)}, u32[]{:S(2)}) copy-start(bf16[32,128,128]{2,1,0:T(8,128)(2,1)S(1)} %all-to-all-done.2.own_ref) | copy-start | bytes 3145732
  55.3 32.4 %all-to-all-start.1 = ((bf16[32,256,128]{2,1,0:T(8,128)(2,1)}), bf16[32,256,128]{2,1,0:T(8,128)(2,1)S(1)}, u32[]{:S(2)}, u32[]{:S(2)}) async-start(bf16[32,256,128]{2,1,0:T(8,128)(2,1)} %pack_qd.1), calls=%async_computation.1 | async-start | bytes 4194304 | tf_op jit(solution)/shard_map/all_to_all | solution.py:301
  59.3 4.7 %collective-permute-start = (bf16[32,128,128]{2,1,0:T(8,128)(2,1)S(1)}, bf16[32,128,128]{2,1,0:T(8,128)(2,1)}, u32[]{:S(2)}, u32[]{:S(2)}) collective-permute-start(bf16[32,128,128]{2,1,0:T(8,128)(2,1)S(1)} %all-to-all-done.2.own_ref), channel_id=1, source_target_pairs={{0,16},{16,0},{32,48},{48,32},{64,80},{80,64},{96,112},{112,96},{1... | collective-permute-start | bytes 3145736 | tf_op jit(solution)/shard_map/ppermute | solution.py:291
  87.7 1.4 copy-start
  135.4 15.1 %all-to-all-start.4 = ((f32[16,8,128]{2,1,0:T(8,128)}), f32[16,8,128]{2,1,0:T(8,128)S(1)}, u32[]{:S(2)}, u32[]{:S(2)}) async-start(f32[16,8,128]{2,1,0:T(8,128)} %get-tuple-element.21), calls=%async_computation.4 | async-start | bytes 131072 | tf_op jit(solution)/shard_map/all_to_all | solution.py:334
  138.9 18.5 %collective-permute-start.1 = (bf16[32,128,128]{2,1,0:T(8,128)(2,1)}, bf16[32,128,128]{2,1,0:T(8,128)(2,1)S(1)}, u32[]{:S(2)}, u32[]{:S(2)}) collective-permute-start(bf16[32,128,128]{2,1,0:T(8,128)(2,1)} %get-tuple-element.20), channel_id=1, source_target_pairs={{0,16},{16,0},{32,48},{48,32},{64,80},{80,64},{96,112},{112,96},{1... | collective-permute-start | bytes 3145736 | tf_op jit(solution)/shard_map/ppermute | solution.py:332
  150.5 6.9 %copy-start.5 = (f32[16,8,128]{2,1,0:T(8,128)}, f32[16,8,128]{2,1,0:T(8,128)S(1)}, u32[]{:S(2)}) copy-start(f32[16,8,128]{2,1,0:T(8,128)S(1)} %all-to-all-done.4.gain_ref) | copy-start | bytes 196612
  150.5 24.1 %all-to-all-start.3 = ((bf16[32,128,128]{2,1,0:T(8,128)(2,1)}), bf16[32,128,128]{2,1,0:T(8,128)(2,1)S(1)}, u32[]{:S(2)}, u32[]{:S(2)}) async-start(bf16[32,128,128]{2,1,0:T(8,128)(2,1)} %get-tuple-element.18), calls=%async_computation.3 | async-start | bytes 2097152 | tf_op jit(solution)/shard_map/all_to_all | solution.py:333
  157.4 1.0 copy-start.4
  174.6 4.0 %copy-start.2 = (bf16[32,128,128]{2,1,0:T(8,128)(2,1)}, bf16[32,128,128]{2,1,0:T(8,128)(2,1)S(1)}, u32[]{:S(2)}) copy-start(bf16[32,128,128]{2,1,0:T(8,128)(2,1)S(1)} %all-to-all-done.3.in_ref) | copy-start | bytes 3145732
  174.6 22.6 %all-to-all-start.5 = ((bf16[32,144,128]{2,1,0:T(8,128)(2,1)}), bf16[32,144,128]{2,1,0:T(8,128)(2,1)S(1)}, u32[]{:S(2)}, u32[]{:S(2)}) async-start(bf16[32,144,128]{2,1,0:T(8,128)(2,1)} %merge.1), calls=%async_computation.5 | async-start | bytes 2359296 | tf_op jit(solution)/shard_map/all_to_all | solution.py:343
  197.2 1.0 copy-start.1

commit v2 on v0

v2 whole, which is shorter than its diff:
```python
import functools
import math

import jax
import jax.numpy as jnp
from jax import lax
from jax.experimental import pallas as pl
from jax.experimental.pallas import tpu as pltpu
from jax.sharding import PartitionSpec as P

BLK = 128
HD = 128
HALF = BLK // 2
SLOTS = 6
PARTS = 8
PACKS = 4
EPSILON = 1e-06

F32 = jnp.float32
BF16 = jnp.bfloat16
NT = (((1,), (1,)), ((), ()))
NN = (((1,), (0,)), ((), ()))

VMEM_SPEC = pl.BlockSpec(memory_space=pltpu.VMEM)
SMEM_SPEC = pl.BlockSpec(memory_space=pltpu.SMEM)
HBM_SPEC = pl.BlockSpec(memory_space=pltpu.HBM)


def run_copies(copies):
    for copy in copies:
        copy.start()
    for copy in copies:
        copy.wait()


def pack_kernel(heads, q_ref, d_ref, k_ref, v_ref, out_any, held_ref, sems, out_sems):
    copies = []
    for h in range(heads):
        rows = pl.ds((h % 2) * HALF, HALF)
        wide = pl.ds(h * HD, HD)
        cols = pl.ds((h // 4) * HD, HD)
        parts = (
            (q_ref.at[0, :, wide], 0, BLK),
            (d_ref.at[0, :, wide], BLK, BLK),
            (k_ref.at[0, rows, cols], 2 * BLK, HALF),
            (v_ref.at[0, rows, cols], 2 * BLK + HALF, HALF),
        )
        copies.append(
            [
                pltpu.make_async_copy(source, held_ref.at[h, pl.ds(first, count)], sems.at[4 * h + n])
                for n, (source, first, count) in enumerate(parts)
            ]
        )
    for group in copies:
        for copy in group:
            copy.start()
    step = heads // PACKS
    outs = []
    for n in range(PACKS):
        for group in copies[n * step : (n + 1) * step]:
            for copy in group:
                copy.wait()
        chunk = pl.ds(n * step, step)
        outs.append(pltpu.make_async_copy(held_ref.at[chunk], out_any.at[chunk], out_sems.at[n]))
        outs[-1].start()
    for copy in outs:
        copy.wait()


def inverse_rms(values):
    return lax.rsqrt(jnp.mean(values * values, axis=-1, keepdims=True) + EPSILON)


def rows_sum(values):
    return jnp.sum(values.reshape(values.shape[0] // 8, 8, values.shape[1]), axis=0)


def named_blocks(pat_ref, b):
    named = [pat_ref[0, b, s] for s in range(SLOTS)]
    return named, [jnp.maximum(n, 0) for n in named]


SCALE = 1.0 / math.sqrt(HD)
SCALE2 = SCALE * math.log2(math.e)
CHUNK = 8
GROUPS = [list(range(s, s + 2)) for s in range(0, SLOTS, 2)]


def attend_kernel(
    blocks, pat_ref, gains_ref, got_ref, other_ref,
    send_any, keep_ref, give_ref, parts_ref,
    dq_ref, acc_ref, lead_ref, lead_dq_ref, kv_ref, kt_ref, khat_ref, qn_ref,
    s0, s1, g0, g1, x0, x1, peak_ref, sem,
):
    s_refs, g_refs, x_refs = (s0, s1), (g0, g1), (x0, x1)
    q_gain = gains_ref[0:1, :]
    k_gain = gains_ref[1:2, :]
    zeros = jnp.zeros((BLK, HD), BF16)
    own_k, own_v = pl.ds(2 * BLK, HALF), pl.ds(2 * BLK + HALF, HALF)

    def normalise(j, carry):
        k_raw = jnp.concatenate([got_ref[j, own_k, :], other_ref[j, 0:HALF, :]], axis=0).astype(F32)
        k_hat = k_raw * inverse_rms(k_raw)
        k_low = (k_hat * k_gain).astype(BF16)
        q_raw = got_ref[j, 0:BLK, :].astype(F32)
        q_low = (q_raw * inverse_rms(q_raw) * q_gain).astype(BF16)
        khat_ref[j] = k_hat
        kv_ref[j, :, 0:HD] = k_low
        kv_ref[j, :, HD : 2 * HD] = jnp.concatenate([got_ref[j, own_v, :], other_ref[j, HALF:BLK, :]], axis=0)
        kt_ref[j] = k_low.T
        qn_ref[j] = q_low
        return carry

    lax.fori_loop(0, blocks, normalise, 0, unroll=4)

    def pair_of(b):
        d_low = got_ref[b, BLK : 2 * BLK, :]
        return jnp.concatenate(
            [jnp.concatenate([qn_ref[b], zeros], axis=1), jnp.concatenate([zeros, d_low], axis=1)], axis=0
        )

    def slot_rows(s):
        return pl.ds(s * BLK, BLK)

    pair = pair_of(0)

    def chunk_rows(i):
        return pl.ds(pl.multiple_of(i * CHUNK * BLK, CHUNK * BLK), CHUNK * BLK)

    def lead_scores(i, peak):
        rows = kv_ref[pl.ds(i * CHUNK, CHUNK)].reshape(CHUNK * BLK, 2 * HD)
        both = lax.dot_general(rows, pair, NT, preferred_element_type=F32)
        lead_ref[chunk_rows(i), :] = both
        return jnp.maximum(peak, jnp.max(both[:, 0:BLK].reshape(CHUNK * BLK // 8, 8, BLK), axis=0))

    peak = lax.fori_loop(0, blocks // CHUNK, lead_scores, jnp.full((8, BLK), -jnp.inf, F32))
    peak = jnp.max(peak, axis=0, keepdims=True) * SCALE2

    def lead_exp(i, sums):
        raised = jnp.exp2(lead_ref[chunk_rows(i), 0:BLK] * SCALE2 - peak)
        lead_ref[chunk_rows(i), 0:BLK] = raised
        product = raised * lead_ref[chunk_rows(i), BLK : 2 * BLK]
        return sums[0] + rows_sum(raised), sums[1] + rows_sum(product)

    zero8 = jnp.zeros((8, BLK), F32)
    total, delta = lax.fori_loop(0, blocks // CHUNK, lead_exp, (zero8, zero8))
    lead_inv = 1.0 / jnp.sum(total, axis=0, keepdims=True)
    lead_delta = jnp.sum(delta, axis=0, keepdims=True) * lead_inv

    def lead_grad(i, dq_t):
        weights = lead_ref[chunk_rows(i), 0:BLK] * lead_inv
        d_weights = lead_ref[chunk_rows(i), BLK : 2 * BLK]
        d_low = (weights * (d_weights - lead_delta) * SCALE).astype(BF16)
        both = jnp.concatenate([d_low, weights.astype(BF16)], axis=1)
        terms = lax.dot_general(both, pair, NN, preferred_element_type=F32)
        acc_ref[pl.ds(i * CHUNK, CHUNK)] = terms.reshape(CHUNK, BLK, 2 * HD)
        keys = jnp.concatenate([kt_ref[i * CHUNK + t] for t in range(CHUNK)], axis=1)
        return dq_t + lax.dot_general(keys, d_low, NN, preferred_element_type=F32)

    lead_dq_ref[...] = lax.fori_loop(0, blocks // CHUNK, lead_grad, jnp.zeros((HD, BLK), F32))

    def scores_slots(b, side, slots, pair, peak):
        index = named_blocks(pat_ref, b)[1]
        rows = jnp.concatenate([kv_ref[index[s]] for s in slots], axis=0)
        both = lax.dot_general(rows, pair, NT, preferred_element_type=F32)
        span = pl.ds(slots[0] * BLK, len(slots) * BLK)
        s_refs[side][span, :] = both[:, 0:BLK]
        g_refs[side][span, :] = both[:, BLK : 2 * BLK]
        top = jnp.max(both[:, 0:BLK].reshape(len(slots) * BLK // 8, 8, BLK), axis=0)
        return top if peak is None else jnp.maximum(peak, top)

    def exp_slot(b, side, s, peak, sums):
        named = named_blocks(pat_ref, b)[0]
        kept = named[s] >= 0
        for t in range(s):
            kept = jnp.logical_and(kept, named[s] != named[t])
        floor = peak + jnp.where(kept, 0.0, jnp.inf).astype(F32)
        raised = jnp.exp2(s_refs[side][slot_rows(s), :] * SCALE2 - floor)
        s_refs[side][slot_rows(s), :] = raised
        product = raised * g_refs[side][slot_rows(s), :]
        return sums[0] + rows_sum(raised), sums[1] + rows_sum(product)

    def grads_slots(side, slots, pair, inv_total, inv_scaled, delta):
        span = pl.ds(slots[0] * BLK, len(slots) * BLK)
        raised = s_refs[side][span, :]
        d_low = (raised * inv_scaled * (g_refs[side][span, :] - delta)).astype(BF16)
        x_refs[side][span, :] = d_low
        both = jnp.concatenate([d_low, (raised * inv_total).astype(BF16)], axis=1)
        return lax.dot_general(both, pair, NN, preferred_element_type=F32)

    def query_product(b, side):
        index = named_blocks(pat_ref, b)[1]
        keys = jnp.concatenate([kt_ref[i] for i in index], axis=1)
        return lax.dot_general(keys, x_refs[side][...], NN, preferred_element_type=F32)

    def query_grad(b, dq_t, q_part):
        dq = dq_t.T.astype(BF16).astype(F32)
        q_raw = got_ref[b, 0:BLK, :].astype(F32)
        q_inv = inverse_rms(q_raw)
        q_hat = q_raw * q_inv
        scaled = q_gain * dq
        mean = jnp.mean(scaled * q_hat, axis=-1, keepdims=True)
        dq_ref[b] = (q_inv * (scaled - q_hat * mean)).astype(BF16)
        return q_part + rows_sum(dq * q_hat)

    def step(b, side, q_part, ahead=True, behind=True):
        peak = peak_ref[side, 0:1, :] * SCALE2
        sums = (zero8, zero8)
        pair = pair_of(b + 1) if ahead else None
        top = None
        dq_t = query_product(b - 1, 1 - side) if behind else None
        for slots in GROUPS:
            if ahead:
                top = scores_slots(b + 1, 1 - side, slots, pair, top)
            for s in slots:
                sums = exp_slot(b, side, s, peak, sums)
        if ahead:
            peak_ref[1 - side, 0:1, :] = jnp.max(top, axis=0, keepdims=True)
        inv_total = 1.0 / jnp.sum(sums[0], axis=0, keepdims=True)
        delta = jnp.sum(sums[1], axis=0, keepdims=True) * inv_total
        pair = pair_of(b)
        index = named_blocks(pat_ref, b)[1]
        for slots in GROUPS:
            terms = grads_slots(side, slots, pair, inv_total, inv_total * SCALE, delta)
            for n, s in enumerate(slots):
                acc_ref[index[s]] += terms[n * BLK : (n + 1) * BLK]
        return query_grad(b - 1, dq_t, q_part) if behind else q_part

    x0[...] = jnp.zeros_like(x0)
    pair = pair_of(1)
    top = None
    for slots in GROUPS:
        top = scores_slots(1, 1, slots, pair, top)
    peak_ref[1, 0:1, :] = jnp.max(top, axis=0, keepdims=True)

    def two_steps(i, q_part):
        q_part = step(2 * i + 1, 1, q_part)
        return step(2 * i + 2, 0, q_part)

    q_part = lax.fori_loop(0, blocks // 2 - 1, two_steps, zero8)
    q_part = step(blocks - 1, 1, q_part, ahead=False)
    q_part = query_grad(blocks - 1, query_product(blocks - 1, 1), q_part)
    q_part = query_grad(0, lead_dq_ref[...], q_part)
    dq_copy = pltpu.make_async_copy(dq_ref, send_any.at[:, pl.ds(0, BLK)], sem)
    dq_copy.start()

    def finish(j, k_part):
        keep_ref[j, 0:HALF, :] = acc_ref[j, 0:HALF, 0:HD]
        keep_ref[j, HALF:BLK, :] = acc_ref[j, 0:HALF, HD : 2 * HD]
        give_ref[j, 0:HALF, :] = acc_ref[j, HALF:BLK, 0:HD].astype(BF16)
        give_ref[j, HALF:BLK, :] = acc_ref[j, HALF:BLK, HD : 2 * HD].astype(BF16)
        return k_part + rows_sum(acc_ref[j, :, 0:HD] * khat_ref[j])

    k_part = lax.fori_loop(0, blocks, finish, zero8, unroll=2)
    parts = jnp.concatenate(
        [
            jnp.sum(q_part, axis=0, keepdims=True),
            jnp.sum(k_part, axis=0, keepdims=True),
            jnp.zeros((PARTS - 2, HD), F32),
        ],
        axis=0,
    )
    for j in range(blocks):
        parts_ref[j] = parts
    dq_copy.wait()


def merge_kernel(blocks, keep_ref, got_ref, send_any, out_any, sum_ref, sem):
    def one_block(j, carry):
        sum_ref[j] = (keep_ref[j] + got_ref[j].astype(F32)).astype(BF16)
        return carry

    lax.fori_loop(0, blocks, one_block, 0, unroll=4)
    run_copies([pltpu.make_async_copy(sum_ref, out_any.at[:, pl.ds(BLK, BLK)], sem)])


def parts_sum_kernel(in_ref, out_ref):
    out_ref[...] = jnp.sum(in_ref[...], axis=0)[0:2]


def final_kernel(heads, in_ref, k_ref, gains_ref, q_grad_any, k_grad_ref, v_grad_ref, sems):
    copies = [
        pltpu.make_async_copy(in_ref.at[h, pl.ds(0, BLK)], q_grad_any.at[0, :, pl.ds(h * HD, HD)], sems.at[h])
        for h in range(heads)
    ]
    for copy in copies:
        copy.start()
    k_gain = gains_ref[1:2, :]
    for g in range(heads // 4):
        for core in range(2):
            first, second = 4 * g + core, 4 * g + 2 + core
            rows = pl.ds(core * HALF, HALF)
            cols = pl.ds(g * HD, HD)
            both = in_ref[first, BLK : 2 * BLK, :].astype(F32) + in_ref[second, BLK : 2 * BLK, :].astype(F32)
            v_grad_ref[0, rows, cols] = both[HALF:BLK].astype(BF16)
            values = k_ref[0, rows, cols].astype(F32)
            inverse = inverse_rms(values)
            scaled = k_gain * both[0:HALF].astype(BF16).astype(F32)
            total = jnp.sum(scaled * values, axis=-1, keepdims=True)
            grad = inverse * scaled - inverse * inverse * inverse * values * total / HD
            k_grad_ref[0, rows, cols] = grad.astype(BF16)
    for copy in copies:
        copy.wait()


def dp_step(values, step, dp_count):
    if step >= dp_count:
        return values
    return values + lax.ppermute(values, "dp", [(z, z ^ step) for z in range(dp_count)])


def struct(shape, dtype):
    return jax.ShapeDtypeStruct(shape, dtype)


def call(kernel, name, ins, outs, scratch=(), mib=12, aliases={}):
    return pl.pallas_call(
        kernel,
        out_shape=tuple(array for array, spec in outs),
        in_specs=list(ins),
        out_specs=tuple(spec for array, spec in outs),
        scratch_shapes=list(scratch),
        input_output_aliases=aliases,
        compiler_params=pltpu.CompilerParams(vmem_limit_bytes=mib << 20),
        name=name,
    )


def shards(heads, dp_count, q_raw, k_raw, v_raw, q_gain, k_gain, key_blocks, d_context):
    blocks = heads
    swap = [(s, s ^ 1) for s in range(heads)]
    mine = lax.broadcasted_iota(jnp.int32, (2, HD), 1) // (HD // dp_count) == lax.axis_index("dp")
    spread = jnp.concatenate([jnp.tile(q_gain, dp_count)[None], jnp.tile(k_gain, dp_count)[None]], axis=0)
    gains = jnp.where(mine, spread, 0.0)

    (sent,) = call(
        functools.partial(pack_kernel, heads),
        "pack",
        [HBM_SPEC] * 4,
        [(pltpu.HBM((heads, 3 * BLK, HD), BF16), HBM_SPEC)],
        [
            pltpu.VMEM((heads, 3 * BLK, HD), BF16),
            pltpu.SemaphoreType.DMA((4 * heads,)),
            pltpu.SemaphoreType.DMA((PACKS,)),
        ],
    )(*[pltpu.with_memory_space_constraint(x, pltpu.HBM) for x in (q_raw, d_context, k_raw, v_raw)])
    arrived = lax.all_to_all(sent, "seq", 0, 0, tiled=True)
    for step in (8, 4, 2, 1):
        gains = dp_step(gains, step, dp_count)
    arrived, gains = lax.optimization_barrier((arrived, gains))
    other = lax.ppermute(arrived[:, 2 * BLK :], "seq", swap)

    send, keep, give, parts = call(
        functools.partial(attend_kernel, blocks),
        "attend",
        [SMEM_SPEC] + [VMEM_SPEC] * 3,
        [
            (pltpu.HBM((blocks, 2 * BLK, HD), BF16), HBM_SPEC),
            (pltpu.HBM((blocks, BLK, HD), F32), VMEM_SPEC),
            (pltpu.HBM((blocks, BLK, HD), BF16), VMEM_SPEC),
            (struct((blocks, PARTS, HD), F32), VMEM_SPEC),
        ],
        [
            pltpu.VMEM((blocks, BLK, HD), BF16),
            pltpu.VMEM((blocks, BLK, 2 * HD), F32),
            pltpu.VMEM((blocks * BLK, 2 * BLK), F32),
            pltpu.VMEM((HD, BLK), F32),
            pltpu.VMEM((blocks, BLK, 2 * HD), BF16),
            pltpu.VMEM((blocks, HD, BLK), BF16),
            pltpu.VMEM((blocks, BLK, HD), F32),
            pltpu.VMEM((blocks, BLK, HD), BF16),
        ]
        + [pltpu.VMEM((SLOTS * BLK, BLK), F32)] * 4
        + [pltpu.VMEM((SLOTS * BLK, BLK), BF16)] * 2
        + [pltpu.VMEM((2, 8, BLK), F32), pltpu.SemaphoreType.DMA],
        mib=40,
    )(key_blocks, gains, arrived, other)

    parts = lax.all_to_all(parts, "seq", 0, 0, tiled=True)
    got = lax.ppermute(give, "seq", swap)
    (send,) = call(
        functools.partial(merge_kernel, blocks),
        "merge",
        [VMEM_SPEC] * 2 + [HBM_SPEC],
        [(pltpu.HBM(send.shape, BF16), HBM_SPEC)],
        [pltpu.VMEM((blocks, BLK, HD), BF16), pltpu.SemaphoreType.DMA],
        aliases={2: 0},
    )(keep, got, send)
    back = lax.all_to_all(send, "seq", 0, 0, tiled=True)

    (totals,) = call(parts_sum_kernel, "parts_sum", [VMEM_SPEC], [(struct((2, HD), F32), VMEM_SPEC)])(parts)
    for step in (1, 2, 4, 8):
        totals = dp_step(totals, step, dp_count)
    width = q_gain.shape[0]
    totals = lax.dynamic_slice_in_dim(totals, lax.axis_index("dp") * width, width, axis=1)

    q_grad, k_grad, v_grad = call(
        functools.partial(final_kernel, heads),
        "final",
        [VMEM_SPEC] * 3,
        [
            (struct(q_raw.shape, BF16), HBM_SPEC),
            (struct(k_raw.shape, BF16), VMEM_SPEC),
            (struct(v_raw.shape, BF16), VMEM_SPEC),
        ],
        [pltpu.SemaphoreType.DMA((heads,))],
    )(back, k_raw, gains)
    return (q_grad, k_grad, v_grad, totals[0], totals[1])


def solution(mesh):
    placed = (
        P("dp", "seq", None),
        P("dp", "seq", None),
        P("dp", "seq", None),
        P("dp"),
        P("dp"),
        P("seq", None, None),
        P("dp", "seq", None),
    )
    return jax.shard_map(
        functools.partial(shards, mesh.shape["seq"], mesh.shape["dp"]),
        mesh=mesh,
        in_specs=placed,
        out_specs=(
            P("dp", "seq", None),
            P("dp", "seq", None),
            P("dp", "seq", None),
            P("dp"),
            P("dp"),
        ),
        check_vma=False,
    )
```

time: 446 us -> 144 us (0.32)
  the two profiles are of different devices: /device:TPU:1 before, /device:TPU:2 now
where the time goes in v2:
time: 144 us
  starting transfers between devices  76.6 us (53%)
  Pallas kernels  32.1 us (22%)
  waiting for transfers between devices  30.6 us (21%)
  local copies, waits for them, and re-layouts  3.51 us (2%)
    ppermute x8, starting transfers between devices, dp_step(): lax.ppermute(values, 'dp', [(z, z ^ step) for z in range(dp_count)])  52 us
    pallas_call x1, Pallas kernels, shards(): call(functools.partial(attend_kernel, blocks), 'attend', [SMEM_SPEC] + [V...  24.6 us
    ppermute x8, waiting for transfers between devices, dp_step(): lax.ppermute(values, 'dp', [(z, z ^ step) for z in range(dp_count)])  20.8 us
    all_to_all x1, starting transfers between devices, shards(): arrived = lax.all_to_all(sent, 'seq', 0, 0, tiled=True)  9.62 us
    all_to_all x1, starting transfers between devices, shards(): parts = lax.all_to_all(parts, 'seq', 0, 0, tiled=True)  5.93 us
    all_to_all x1, starting transfers between devices, shards(): back = lax.all_to_all(send, 'seq', 0, 0, tiled=True)  5.08 us
    pallas_call x1, Pallas kernels, shards(): call(functools.partial(pack_kernel, heads), 'pack', [HBM_SPEC] * 4, [(plt...  3.98 us
    all_to_all x1, waiting for transfers between devices, shards(): parts = lax.all_to_all(parts, 'seq', 0, 0, tiled=True)  3.84 us
  transfers between devices with their start and end apart: 13, of which 11 were waited for; matrix products, arithmetic and copies ran while one was open for 1% of the time, Pallas kernels for 1%

profile of v2, /device:TPU:2, one launch (start us, length us, event | category | flops | bytes accessed | tf_op | source)
XLA Modules:
  0.0 143.7 jit_solution(14012683908018754009)
XLA Ops:
  0.6 4.0 %pack.1 = bf16[32,384,128]{2,1,0:T(8,128)(2,1)} custom-call(bf16[1,128,4096]{2,1,0:T(8,128)(2,1)} %q_ref.1, bf16[1,128,4096]{2,1,0:T(8,128)(2,1)} %d_ref.1, bf16[1,128,1024]{2,1,0:T(8,128)(2,1)} %k_ref.3, bf16[1,128,1024]{2,1,0:T(8,128)(2,1)} %v_ref.1), custom_call_target="tpu_custom_call" | custom-call | tf_op jit(solution)/shard_map/pack/pallas_call | solution.py:336
  4.6 9.6 %all-to-all-start = ((bf16[32,384,128]{2,1,0:T(8,128)(2,1)}), bf16[32,384,128]{2,1,0:T(8,128)(2,1)S(1)}, u32[]{:S(2)}, u32[]{:S(2)}) async-start(bf16[32,384,128]{2,1,0:T(8,128)(2,1)} %pack.1), calls=%async_computation | async-start | bytes 6291456 | tf_op jit(solution)/shard_map/all_to_all | solution.py:347
  14.5 13.7 %collective-permute-start = (f32[2,128]{1,0:T(2,128)S(1)}, f32[2,128]{1,0:T(2,128)S(1)}, u32[]{:S(2)}, u32[]{:S(2)}) collective-permute-start(f32[2,128]{1,0:T(2,128)S(1)} %compare_select_fusion), channel_id=1, source_target_pairs={{0,8},{1,9},{2,10},{3,11},{4,12},{5,13},{6,14},{7,15},{8,0},{9,1},... | collective-permute-start | bytes 3080 | tf_op jit(solution)/shard_map/ppermute | solution.py:309
  28.3 1.5 %collective-permute-done = f32[2,128]{1,0:T(2,128)S(1)} collective-permute-done((f32[2,128]{1,0:T(2,128)S(1)}, f32[2,128]{1,0:T(2,128)S(1)}, u32[]{:S(2)}, u32[]{:S(2)}) %collective-permute-start) | collective-permute-done | bytes 1056 | tf_op jit(solution)/shard_map/ppermute | solution.py:309
  29.8 6.0 %collective-permute-start.1 = (f32[2,128]{1,0:T(2,128)S(1)}, f32[2,128]{1,0:T(2,128)S(1)}, u32[]{:S(2)}, u32[]{:S(2)}) collective-permute-start(f32[2,128]{1,0:T(2,128)S(1)} %fusion), channel_id=1, source_target_pairs={{0,4},{1,5},{2,6},{3,7},{4,0},{5,1},{6,2},{7,3},{8,12},{9,13},{10,... | collective-permute-start | bytes 3080 | tf_op jit(solution)/shard_map/ppermute | solution.py:309
  35.9 3.4 %collective-permute-done.1 = f32[2,128]{1,0:T(2,128)S(1)} collective-permute-done((f32[2,128]{1,0:T(2,128)S(1)}, f32[2,128]{1,0:T(2,128)S(1)}, u32[]{:S(2)}, u32[]{:S(2)}) %collective-permute-start.1) | collective-permute-done | bytes 1056 | tf_op jit(solution)/shard_map/ppermute | solution.py:309
  39.2 3.4 %collective-permute-start.2 = (f32[2,128]{1,0:T(2,128)S(1)}, f32[2,128]{1,0:T(2,128)S(1)}, u32[]{:S(2)}, u32[]{:S(2)}) collective-permute-start(f32[2,128]{1,0:T(2,128)S(1)} %fusion.1), channel_id=1, source_target_pairs={{0,2},{1,3},{2,0},{3,1},{4,6},{5,7},{6,4},{7,5},{8,10},{9,11},{10,... | collective-permute-start | bytes 3080 | tf_op jit(solution)/shard_map/ppermute | solution.py:309
  42.6 3.0 %collective-permute-done.2 = f32[2,128]{1,0:T(2,128)S(1)} collective-permute-done((f32[2,128]{1,0:T(2,128)S(1)}, f32[2,128]{1,0:T(2,128)S(1)}, u32[]{:S(2)}, u32[]{:S(2)}) %collective-permute-start.2) | collective-permute-done | bytes 1056 | tf_op jit(solution)/shard_map/ppermute | solution.py:309
  45.6 2.9 %collective-permute-start.3 = (f32[2,128]{1,0:T(2,128)S(1)}, f32[2,128]{1,0:T(2,128)S(1)}, u32[]{:S(2)}, u32[]{:S(2)}) collective-permute-start(f32[2,128]{1,0:T(2,128)S(1)} %add.31), channel_id=1, source_target_pairs={{0,1},{1,0},{2,3},{3,2},{4,5},{5,4},{6,7},{7,6},{8,9},{9,8},{10,11... | collective-permute-start | bytes 3080 | tf_op jit(solution)/shard_map/ppermute | solution.py:309
  48.5 2.5 %collective-permute-done.3 = f32[2,128]{1,0:T(2,128)S(1)} collective-permute-done((f32[2,128]{1,0:T(2,128)S(1)}, f32[2,128]{1,0:T(2,128)S(1)}, u32[]{:S(2)}, u32[]{:S(2)}) %collective-permute-start.3) | collective-permute-done | bytes 1056 | tf_op jit(solution)/shard_map/ppermute | solution.py:309
  51.1 3.1 %all-to-all-done.got_ref = bf16[32,384,128]{2,1,0:T(8,128)(2,1)S(1)} async-done(((bf16[32,384,128]{2,1,0:T(8,128)(2,1)}), bf16[32,384,128]{2,1,0:T(8,128)(2,1)S(1)}, u32[]{:S(2)}, u32[]{:S(2)}) %all-to-all-start) | async-done | bytes 3145760 | tf_op jit(solution)/shard_map/all_to_all | solution.py:347
  54.2 1.0 slice.9
  55.2 1.9 %collective-permute-start.4 = (bf16[32,128,128]{2,1,0:T(8,128)(2,1)}, bf16[32,128,128]{2,1,0:T(8,128)(2,1)}, u32[]{:S(2)}, u32[]{:S(2)}) collective-permute-start(bf16[32,128,128]{2,1,0:T(8,128)(2,1)} %slice.9), channel_id=1, source_target_pairs={{0,16},{16,0},{32,48},{48,32},{64,80},{80,64},{96,112},{112,96},{1... | collective-permute-start | bytes 3145736 | tf_op jit(solution)/shard_map/ppermute | solution.py:351
  57.2 0.1 copy.14.pat_ref
  57.3 2.9 %collective-permute-done.4.other_ref = bf16[32,128,128]{2,1,0:T(8,128)(2,1)} collective-permute-done((bf16[32,128,128]{2,1,0:T(8,128)(2,1)}, bf16[32,128,128]{2,1,0:T(8,128)(2,1)}, u32[]{:S(2)}, u32[]{:S(2)}) %collective-permute-start.4) | collective-permute-done | bytes 1048608 | tf_op jit(solution)/shard_map/ppermute | solution.py:351
  60.1 24.6 %attend.1 = (bf16[32,256,128]{2,1,0:T(8,128)(2,1)}, f32[32,128,128]{2,1,0:T(8,128)}, bf16[32,128,128]{2,1,0:T(8,128)(2,1)}, f32[32,8,128]{2,1,0:T(8,128)}) custom-call(s32[1,32,6]{2,1,0:T(8,128)S(1)} %copy.14.pat_ref, f32[2,128]{1,0:T(2,128)S(1)} %add.32.gains_ref, bf16[32,384,128]{2,1,0:T(8,128)(2,1)S(1)} %all-to-all-done.got_ref, ...), custom_call_target="tpu_custom_call" | custom-call | tf_op jit(solution)/shard_map/attend/pallas_call | solution.py:353
  84.7 2.0 %collective-permute-start.5 = (bf16[32,128,128]{2,1,0:T(8,128)(2,1)}, bf16[32,128,128]{2,1,0:T(8,128)(2,1)S(1)}, u32[]{:S(2)}, u32[]{:S(2)}) collective-permute-start(bf16[32,128,128]{2,1,0:T(8,128)(2,1)} %get-tuple-element.17), channel_id=1, source_target_pairs={{0,16},{16,0},{32,48},{48,32},{64,80},{80,64},{96,112},{112,96},{1... | collective-permute-start | bytes 3145736 | tf_op jit(solution)/shard_map/ppermute | solution.py:380
  86.8 5.9 %all-to-all-start.2 = ((f32[32,8,128]{2,1,0:T(8,128)}), f32[32,8,128]{2,1,0:T(8,128)S(1)}, u32[]{:S(2)}, u32[]{:S(2)}) async-start(f32[32,8,128]{2,1,0:T(8,128)} %get-tuple-element.22), calls=%async_computation.2 | async-start | bytes 262144 | tf_op jit(solution)/shard_map/all_to_all | solution.py:379
  92.7 1.6 %copy-done = f32[32,128,128]{2,1,0:T(8,128)S(1)} copy-done((f32[32,128,128]{2,1,0:T(8,128)S(1)}, f32[32,128,128]{2,1,0:T(8,128)}, u32[]{:S(2)}) %copy-start) | copy-done | bytes 2097176
  94.3 1.2 merge.1
  95.6 3.8 %all-to-all-done.2.in_ref = f32[32,8,128]{2,1,0:T(8,128)S(1)} async-done(((f32[32,8,128]{2,1,0:T(8,128)}), f32[32,8,128]{2,1,0:T(8,128)S(1)}, u32[]{:S(2)}, u32[]{:S(2)}) %all-to-all-start.2) | async-done | bytes 131104 | tf_op jit(solution)/shard_map/all_to_all | solution.py:379
  99.4 5.1 %all-to-all-start.1 = ((bf16[32,256,128]{2,1,0:T(8,128)(2,1)}), bf16[32,256,128]{2,1,0:T(8,128)(2,1)S(1)}, u32[]{:S(2)}, u32[]{:S(2)}) async-start(bf16[32,256,128]{2,1,0:T(8,128)(2,1)} %merge.1), calls=%async_computation.1 | async-start | bytes 4194304 | tf_op jit(solution)/shard_map/all_to_all | solution.py:389
  104.5 1.9 %collective-permute-start.6 = (f32[2,128]{1,0:T(2,128)S(1)}, f32[2,128]{1,0:T(2,128)S(1)}, u32[]{:S(2)}, u32[]{:S(2)}) collective-permute-start(f32[2,128]{1,0:T(2,128)S(1)} %parts_sum.1), channel_id=1, source_target_pairs={{0,1},{1,0},{2,3},{3,2},{4,5},{5,4},{6,7},{7,6},{8,9},{9,8},{10,11... | collective-permute-start | bytes 3080 | tf_op jit(solution)/shard_map/ppermute | solution.py:309
  106.4 3.5 %collective-permute-done.6 = f32[2,128]{1,0:T(2,128)S(1)} collective-permute-done((f32[2,128]{1,0:T(2,128)S(1)}, f32[2,128]{1,0:T(2,128)S(1)}, u32[]{:S(2)}, u32[]{:S(2)}) %collective-permute-start.6) | collective-permute-done | bytes 1056 | tf_op jit(solution)/shard_map/ppermute | solution.py:309
  110.0 3.1 %collective-permute-start.7 = (f32[2,128]{1,0:T(2,128)S(1)}, f32[2,128]{1,0:T(2,128)S(1)}, u32[]{:S(2)}, u32[]{:S(2)}) collective-permute-start(f32[2,128]{1,0:T(2,128)S(1)} %add.33), channel_id=1, source_target_pairs={{0,2},{1,3},{2,0},{3,1},{4,6},{5,7},{6,4},{7,5},{8,10},{9,11},{10,... | collective-permute-start | bytes 3080 | tf_op jit(solution)/shard_map/ppermute | solution.py:309
  113.1 3.3 %collective-permute-done.7 = f32[2,128]{1,0:T(2,128)S(1)} collective-permute-done((f32[2,128]{1,0:T(2,128)S(1)}, f32[2,128]{1,0:T(2,128)S(1)}, u32[]{:S(2)}, u32[]{:S(2)}) %collective-permute-start.7) | collective-permute-done | bytes 1056 | tf_op jit(solution)/shard_map/ppermute | solution.py:309
  116.3 7.4 %collective-permute-start.8 = (f32[2,128]{1,0:T(2,128)S(1)}, f32[2,128]{1,0:T(2,128)S(1)}, u32[]{:S(2)}, u32[]{:S(2)}) collective-permute-start(f32[2,128]{1,0:T(2,128)S(1)} %add.34), channel_id=1, source_target_pairs={{0,4},{1,5},{2,6},{3,7},{4,0},{5,1},{6,2},{7,3},{8,12},{9,13},{10,... | collective-permute-start | bytes 3080 | tf_op jit(solution)/shard_map/ppermute | solution.py:309
  123.7 2.0 %collective-permute-done.8 = f32[2,128]{1,0:T(2,128)S(1)} collective-permute-done((f32[2,128]{1,0:T(2,128)S(1)}, f32[2,128]{1,0:T(2,128)S(1)}, u32[]{:S(2)}, u32[]{:S(2)}) %collective-permute-start.8) | collective-permute-done | bytes 1056 | tf_op jit(solution)/shard_map/ppermute | solution.py:309
  125.7 13.6 %collective-permute-start.9 = (f32[2,128]{1,0:T(2,128)S(1)}, f32[2,128]{1,0:T(2,128)S(1)}, u32[]{:S(2)}, u32[]{:S(2)}) collective-permute-start(f32[2,128]{1,0:T(2,128)S(1)} %add.35), channel_id=1, source_target_pairs={{0,8},{1,9},{2,10},{3,11},{4,12},{5,13},{6,14},{7,15},{8,0},{9,1},... | collective-permute-start | bytes 3080 | tf_op jit(solution)/shard_map/ppermute | solution.py:309
  139.3 1.5 %collective-permute-done.9 = f32[2,128]{1,0:T(2,128)S(1)} collective-permute-done((f32[2,128]{1,0:T(2,128)S(1)}, f32[2,128]{1,0:T(2,128)S(1)}, u32[]{:S(2)}, u32[]{:S(2)}) %collective-permute-start.9) | collective-permute-done | bytes 1056 | tf_op jit(solution)/shard_map/ppermute | solution.py:309
  140.9 0.5 slice_bitcast_fusion
  141.5 2.2 %final.1 = (bf16[1,128,4096]{2,1,0:T(8,128)(2,1)}, bf16[1,128,1024]{2,1,0:T(8,128)(2,1)}, bf16[1,128,1024]{2,1,0:T(8,128)(2,1)}) custom-call(bf16[32,256,128]{2,1,0:T(8,128)(2,1)S(1)} %all-to-all-done.1.in_ref, bf16[1,128,1024]{2,1,0:T(8,128)(2,1)S(1)} %copy-done.1, f32[2,128]{1,0:T(2,128)S(1)} %add.32.gains_ref), custom_call_target="tpu_custom_call" | custom-call | tf_op jit(solution)/shard_map/final/pallas_call | solution.py:397
  (28 shorter events, 0.4 us)
Async XLA Ops:
  4.6 9.7 %copy-start.3 = (f32[8]{0:T(128)S(1)}, f32[8]{0:T(128)}, u32[]{:S(2)}) copy-start(f32[8]{0:T(128)} %param.10) | copy-start | bytes 100
  4.6 9.8 %copy-start.4 = (f32[8]{0:T(128)S(1)}, f32[8]{0:T(128)}, u32[]{:S(2)}) copy-start(f32[8]{0:T(128)} %param.11) | copy-start | bytes 100
  4.6 49.6 %all-to-all-start = ((bf16[32,384,128]{2,1,0:T(8,128)(2,1)}), bf16[32,384,128]{2,1,0:T(8,128)(2,1)S(1)}, u32[]{:S(2)}, u32[]{:S(2)}) async-start(bf16[32,384,128]{2,1,0:T(8,128)(2,1)} %pack.1), calls=%async_computation | async-start | bytes 6291456 | tf_op jit(solution)/shard_map/all_to_all | solution.py:347
  14.3 42.9 %copy-start.2 = (s32[1,32,6]{1,0,2:T(1,128)S(1)}, s32[1,32,6]{1,0,2:T(1,128)}, u32[]{:S(2)}) copy-start(s32[1,32,6]{1,0,2:T(1,128)} %param.12) | copy-start | bytes 2308
  14.5 15.3 %collective-permute-start = (f32[2,128]{1,0:T(2,128)S(1)}, f32[2,128]{1,0:T(2,128)S(1)}, u32[]{:S(2)}, u32[]{:S(2)}) collective-permute-start(f32[2,128]{1,0:T(2,128)S(1)} %compare_select_fusion), channel_id=1, source_target_pairs={{0,8},{1,9},{2,10},{3,11},{4,12},{5,13},{6,14},{7,15},{8,0},{9,1},... | collective-permute-start | bytes 3080 | tf_op jit(solution)/shard_map/ppermute | solution.py:309
  29.8 9.4 %collective-permute-start.1 = (f32[2,128]{1,0:T(2,128)S(1)}, f32[2,128]{1,0:T(2,128)S(1)}, u32[]{:S(2)}, u32[]{:S(2)}) collective-permute-start(f32[2,128]{1,0:T(2,128)S(1)} %fusion), channel_id=1, source_target_pairs={{0,4},{1,5},{2,6},{3,7},{4,0},{5,1},{6,2},{7,3},{8,12},{9,13},{10,... | collective-permute-start | bytes 3080 | tf_op jit(solution)/shard_map/ppermute | solution.py:309
  39.2 6.4 %collective-permute-start.2 = (f32[2,128]{1,0:T(2,128)S(1)}, f32[2,128]{1,0:T(2,128)S(1)}, u32[]{:S(2)}, u32[]{:S(2)}) collective-permute-start(f32[2,128]{1,0:T(2,128)S(1)} %fusion.1), channel_id=1, source_target_pairs={{0,2},{1,3},{2,0},{3,1},{4,6},{5,7},{6,4},{7,5},{8,10},{9,11},{10,... | collective-permute-start | bytes 3080 | tf_op jit(solution)/shard_map/ppermute | solution.py:309
  45.6 5.5 %collective-permute-start.3 = (f32[2,128]{1,0:T(2,128)S(1)}, f32[2,128]{1,0:T(2,128)S(1)}, u32[]{:S(2)}, u32[]{:S(2)}) collective-permute-start(f32[2,128]{1,0:T(2,128)S(1)} %add.31), channel_id=1, source_target_pairs={{0,1},{1,0},{2,3},{3,2},{4,5},{5,4},{6,7},{7,6},{8,9},{9,8},{10,11... | collective-permute-start | bytes 3080 | tf_op jit(solution)/shard_map/ppermute | solution.py:309
  55.2 4.9 %collective-permute-start.4 = (bf16[32,128,128]{2,1,0:T(8,128)(2,1)}, bf16[32,128,128]{2,1,0:T(8,128)(2,1)}, u32[]{:S(2)}, u32[]{:S(2)}) collective-permute-start(bf16[32,128,128]{2,1,0:T(8,128)(2,1)} %slice.9), channel_id=1, source_target_pairs={{0,16},{16,0},{32,48},{48,32},{64,80},{80,64},{96,112},{112,96},{1... | collective-permute-start | bytes 3145736 | tf_op jit(solution)/shard_map/ppermute | solution.py:351
  84.7 8.0 %collective-permute-start.5 = (bf16[32,128,128]{2,1,0:T(8,128)(2,1)}, bf16[32,128,128]{2,1,0:T(8,128)(2,1)S(1)}, u32[]{:S(2)}, u32[]{:S(2)}) collective-permute-start(bf16[32,128,128]{2,1,0:T(8,128)(2,1)} %get-tuple-element.17), channel_id=1, source_target_pairs={{0,16},{16,0},{32,48},{48,32},{64,80},{80,64},{96,112},{112,96},{1... | collective-permute-start | bytes 3145736 | tf_op jit(solution)/shard_map/ppermute | solution.py:380
  86.8 12.6 %all-to-all-start.2 = ((f32[32,8,128]{2,1,0:T(8,128)}), f32[32,8,128]{2,1,0:T(8,128)S(1)}, u32[]{:S(2)}, u32[]{:S(2)}) async-start(f32[32,8,128]{2,1,0:T(8,128)} %get-tuple-element.22), calls=%async_computation.2 | async-start | bytes 262144 | tf_op jit(solution)/shard_map/all_to_all | solution.py:379
  92.7 1.6 %copy-start = (f32[32,128,128]{2,1,0:T(8,128)S(1)}, f32[32,128,128]{2,1,0:T(8,128)}, u32[]{:S(2)}) copy-start(f32[32,128,128]{2,1,0:T(8,128)} %get-tuple-element.16.keep_ref) | copy-start | bytes 6291460
  95.5 45.9 %copy-start.1 = (bf16[1,128,1024]{2,1,0:T(8,128)(2,1)S(1)}, bf16[1,128,1024]{2,1,0:T(8,128)(2,1)}, u32[]{:S(2)}) copy-start(bf16[1,128,1024]{2,1,0:T(8,128)(2,1)} %k_ref.3) | copy-start | bytes 786436
  99.4 42.1 %all-to-all-start.1 = ((bf16[32,256,128]{2,1,0:T(8,128)(2,1)}), bf16[32,256,128]{2,1,0:T(8,128)(2,1)S(1)}, u32[]{:S(2)}, u32[]{:S(2)}) async-start(bf16[32,256,128]{2,1,0:T(8,128)(2,1)} %merge.1), calls=%async_computation.1 | async-start | bytes 4194304 | tf_op jit(solution)/shard_map/all_to_all | solution.py:389
  104.5 5.5 %collective-permute-start.6 = (f32[2,128]{1,0:T(2,128)S(1)}, f32[2,128]{1,0:T(2,128)S(1)}, u32[]{:S(2)}, u32[]{:S(2)}) collective-permute-start(f32[2,128]{1,0:T(2,128)S(1)} %parts_sum.1), channel_id=1, source_target_pairs={{0,1},{1,0},{2,3},{3,2},{4,5},{5,4},{6,7},{7,6},{8,9},{9,8},{10,11... | collective-permute-start | bytes 3080 | tf_op jit(solution)/shard_map/ppermute | solution.py:309
  110.0 6.4 %collective-permute-start.7 = (f32[2,128]{1,0:T(2,128)S(1)}, f32[2,128]{1,0:T(2,128)S(1)}, u32[]{:S(2)}, u32[]{:S(2)}) collective-permute-start(f32[2,128]{1,0:T(2,128)S(1)} %add.33), channel_id=1, source_target_pairs={{0,2},{1,3},{2,0},{3,1},{4,6},{5,7},{6,4},{7,5},{8,10},{9,11},{10,... | collective-permute-start | bytes 3080 | tf_op jit(solution)/shard_map/ppermute | solution.py:309
  116.3 9.4 %collective-permute-start.8 = (f32[2,128]{1,0:T(2,128)S(1)}, f32[2,128]{1,0:T(2,128)S(1)}, u32[]{:S(2)}, u32[]{:S(2)}) collective-permute-start(f32[2,128]{1,0:T(2,128)S(1)} %add.34), channel_id=1, source_target_pairs={{0,4},{1,5},{2,6},{3,7},{4,0},{5,1},{6,2},{7,3},{8,12},{9,13},{10,... | collective-permute-start | bytes 3080 | tf_op jit(solution)/shard_map/ppermute | solution.py:309
  125.7 15.2 %collective-permute-start.9 = (f32[2,128]{1,0:T(2,128)S(1)}, f32[2,128]{1,0:T(2,128)S(1)}, u32[]{:S(2)}, u32[]{:S(2)}) collective-permute-start(f32[2,128]{1,0:T(2,128)S(1)} %add.35), channel_id=1, source_target_pairs={{0,8},{1,9},{2,10},{3,11},{4,12},{5,13},{6,14},{7,15},{8,0},{9,1},... | collective-permute-start | bytes 3080 | tf_op jit(solution)/shard_map/ppermute | solution.py:309

commit v3 on v2

--- a/solution.py
+++ b/solution.py
@@ -14,6 +14,7 @@
 SLOTS = 6
 PARTS = 8
 PACKS = 4
+OUTS = 4
 EPSILON = 1e-06
 
 F32 = jnp.float32
@@ -33,35 +34,37 @@
         copy.wait()
 
 
-def pack_kernel(heads, q_ref, d_ref, k_ref, v_ref, out_any, held_ref, sems, out_sems):
-    copies = []
-    for h in range(heads):
-        rows = pl.ds((h % 2) * HALF, HALF)
-        wide = pl.ds(h * HD, HD)
-        cols = pl.ds((h // 4) * HD, HD)
-        parts = (
-            (q_ref.at[0, :, wide], 0, BLK),
-            (d_ref.at[0, :, wide], BLK, BLK),
-            (k_ref.at[0, rows, cols], 2 * BLK, HALF),
-            (v_ref.at[0, rows, cols], 2 * BLK + HALF, HALF),
-        )
-        copies.append(
+def pack_kernel(heads, q_any, d_any, k_any, v_any, out_any, q_ref, d_ref, k_ref, v_ref, out_ref, sems, out_sems):
+    step = heads // PACKS
+    loads = []
+    for n in range(PACKS):
+        wide = pl.ds(n * step * HD, step * HD)
+        cols = pl.ds(n * (step // 4) * HD, (step // 4) * HD)
+        arrays = ((q_any, q_ref, wide), (d_any, d_ref, wide), (k_any, k_ref, cols), (v_any, v_ref, cols))
+        loads.append(
             [
-                pltpu.make_async_copy(source, held_ref.at[h, pl.ds(first, count)], sems.at[4 * h + n])
-                for n, (source, first, count) in enumerate(parts)
+                pltpu.make_async_copy(source.at[0, :, span], held.at[:, span], sems.at[4 * n + i])
+                for i, (source, held, span) in enumerate(arrays)
             ]
         )
-    for group in copies:
+    for group in loads:
         for copy in group:
             copy.start()
-    step = heads // PACKS
     outs = []
     for n in range(PACKS):
-        for group in copies[n * step : (n + 1) * step]:
-            for copy in group:
-                copy.wait()
+        for copy in loads[n]:
+            copy.wait()
+        for h in range(n * step, (n + 1) * step):
+            half = (h % 2) * HALF
+            rows = slice(half, half + HALF)
+            wide = slice(h * HD, (h + 1) * HD)
+            cols = slice((h // 4) * HD, (h // 4 + 1) * HD)
+            out_ref[h, 0:BLK, :] = q_ref[:, wide]
+            out_ref[h, BLK : 2 * BLK, :] = d_ref[:, wide]
+            out_ref[h, 2 * BLK : 2 * BLK + HALF, :] = k_ref[rows, cols]
+            out_ref[h, 2 * BLK + HALF : 3 * BLK, :] = v_ref[rows, cols]
         chunk = pl.ds(n * step, step)
-        outs.append(pltpu.make_async_copy(held_ref.at[chunk], out_any.at[chunk], out_sems.at[n]))
+        outs.append(pltpu.make_async_copy(out_ref.at[chunk], out_any.at[chunk], out_sems.at[n]))
         outs[-1].start()
     for copy in outs:
         copy.wait()
@@ -88,9 +91,9 @@
 
 def attend_kernel(
     blocks, pat_ref, gains_ref, got_ref, other_ref,
-    send_any, keep_ref, give_ref, parts_ref,
-    dq_ref, acc_ref, lead_ref, lead_dq_ref, kv_ref, kt_ref, khat_ref, qn_ref,
-    s0, s1, g0, g1, x0, x1, peak_ref, sem,
+    send_any, keep_any, give_any, parts_ref,
+    dq_ref, keep_ref, give_ref, acc_ref, lead_ref, lead_dq_ref, kv_ref, kt_ref, khat_ref, qn_ref,
+    s0, s1, g0, g1, x0, x1, peak_ref, sem, give_sems, keep_sems,
 ):
     s_refs, g_refs, x_refs = (s0, s1), (g0, g1), (x0, x1)
     q_gain = gains_ref[0:1, :]
@@ -245,13 +248,21 @@
     dq_copy.start()
 
     def finish(j, k_part):
-        keep_ref[j, 0:HALF, :] = acc_ref[j, 0:HALF, 0:HD]
-        keep_ref[j, HALF:BLK, :] = acc_ref[j, 0:HALF, HD : 2 * HD]
-        give_ref[j, 0:HALF, :] = acc_ref[j, HALF:BLK, 0:HD].astype(BF16)
-        give_ref[j, HALF:BLK, :] = acc_ref[j, HALF:BLK, HD : 2 * HD].astype(BF16)
+        for half, ref in ((0, keep_ref), (HALF, give_ref)):
+            rows = pl.ds(half, HALF)
+            ref[j, 0:HALF, :] = acc_ref[j, rows, 0:HD].astype(BF16)
+            ref[j, HALF:BLK, :] = acc_ref[j, rows, HD : 2 * HD].astype(BF16)
         return k_part + rows_sum(acc_ref[j, :, 0:HD] * khat_ref[j])
 
-    k_part = lax.fori_loop(0, blocks, finish, zero8, unroll=2)
+    k_part = zero8
+    step_blocks = blocks // OUTS
+    out_copies = []
+    for n in range(OUTS):
+        k_part = lax.fori_loop(n * step_blocks, (n + 1) * step_blocks, finish, k_part, unroll=2)
+        chunk = pl.ds(n * step_blocks, step_blocks)
+        for ref, out, copy_sems in ((give_ref, give_any, give_sems), (keep_ref, keep_any, keep_sems)):
+            out_copies.append(pltpu.make_async_copy(ref.at[chunk], out.at[chunk], copy_sems.at[n]))
+            out_copies[-1].start()
     parts = jnp.concatenate(
         [
             jnp.sum(q_part, axis=0, keepdims=True),
@@ -263,11 +274,13 @@
     for j in range(blocks):
         parts_ref[j] = parts
     dq_copy.wait()
+    for copy in out_copies:
+        copy.wait()
 
 
 def merge_kernel(blocks, keep_ref, got_ref, send_any, out_any, sum_ref, sem):
     def one_block(j, carry):
-        sum_ref[j] = (keep_ref[j] + got_ref[j].astype(F32)).astype(BF16)
+        sum_ref[j] = (keep_ref[j].astype(F32) + got_ref[j].astype(F32)).astype(BF16)
         return carry
 
     lax.fori_loop(0, blocks, one_block, 0, unroll=4)
@@ -313,7 +326,7 @@
     return jax.ShapeDtypeStruct(shape, dtype)
 
 
-def call(kernel, name, ins, outs, scratch=(), mib=12, aliases={}):
+def call(kernel, ins, outs, scratch=(), mib=12, aliases={}):
     return pl.pallas_call(
         kernel,
         out_shape=tuple(array for array, spec in outs),
@@ -322,7 +335,6 @@
         scratch_shapes=list(scratch),
         input_output_aliases=aliases,
         compiler_params=pltpu.CompilerParams(vmem_limit_bytes=mib << 20),
-        name=name,
     )
 
 
@@ -335,12 +347,15 @@
 
     (sent,) = call(
         functools.partial(pack_kernel, heads),
-        "pack",
         [HBM_SPEC] * 4,
         [(pltpu.HBM((heads, 3 * BLK, HD), BF16), HBM_SPEC)],
         [
+            pltpu.VMEM(q_raw.shape[1:], BF16),
+            pltpu.VMEM(d_context.shape[1:], BF16),
+            pltpu.VMEM(k_raw.shape[1:], BF16),
+            pltpu.VMEM(v_raw.shape[1:], BF16),
             pltpu.VMEM((heads, 3 * BLK, HD), BF16),
-            pltpu.SemaphoreType.DMA((4 * heads,)),
+            pltpu.SemaphoreType.DMA((4 * PACKS,)),
             pltpu.SemaphoreType.DMA((PACKS,)),
         ],
     )(*[pltpu.with_memory_space_constraint(x, pltpu.HBM) for x in (q_raw, d_context, k_raw, v_raw)])
@@ -352,15 +367,16 @@
 
     send, keep, give, parts = call(
         functools.partial(attend_kernel, blocks),
-        "attend",
         [SMEM_SPEC] + [VMEM_SPEC] * 3,
         [
             (pltpu.HBM((blocks, 2 * BLK, HD), BF16), HBM_SPEC),
-            (pltpu.HBM((blocks, BLK, HD), F32), VMEM_SPEC),
-            (pltpu.HBM((blocks, BLK, HD), BF16), VMEM_SPEC),
+            (pltpu.HBM((blocks, BLK, HD), BF16), HBM_SPEC),
+            (pltpu.HBM((blocks, BLK, HD), BF16), HBM_SPEC),
             (struct((blocks, PARTS, HD), F32), VMEM_SPEC),
         ],
         [
+            pltpu.VMEM((blocks, BLK, HD), BF16),
+            pltpu.VMEM((blocks, BLK, HD), BF16),
             pltpu.VMEM((blocks, BLK, HD), BF16),
             pltpu.VMEM((blocks, BLK, 2 * HD), F32),
             pltpu.VMEM((blocks * BLK, 2 * BLK), F32),
@@ -372,7 +388,8 @@
         ]
         + [pltpu.VMEM((SLOTS * BLK, BLK), F32)] * 4
         + [pltpu.VMEM((SLOTS * BLK, BLK), BF16)] * 2
-        + [pltpu.VMEM((2, 8, BLK), F32), pltpu.SemaphoreType.DMA],
+        + [pltpu.VMEM((2, 8, BLK), F32), pltpu.SemaphoreType.DMA]
+        + [pltpu.SemaphoreType.DMA((OUTS,))] * 2,
         mib=40,
     )(key_blocks, gains, arrived, other)
 
@@ -380,7 +397,6 @@
     got = lax.ppermute(give, "seq", swap)
     (send,) = call(
         functools.partial(merge_kernel, blocks),
-        "merge",
         [VMEM_SPEC] * 2 + [HBM_SPEC],
         [(pltpu.HBM(send.shape, BF16), HBM_SPEC)],
         [pltpu.VMEM((blocks, BLK, HD), BF16), pltpu.SemaphoreType.DMA],
@@ -388,15 +404,15 @@
     )(keep, got, send)
     back = lax.all_to_all(send, "seq", 0, 0, tiled=True)
 
-    (totals,) = call(parts_sum_kernel, "parts_sum", [VMEM_SPEC], [(struct((2, HD), F32), VMEM_SPEC)])(parts)
-    for step in (1, 2, 4, 8):
+    (totals,) = call(parts_sum_kernel, [VMEM_SPEC], [(struct((2, HD), F32), VMEM_SPEC)])(parts)
+    for step in (8, 4, 2):
         totals = dp_step(totals, step, dp_count)
+    totals = dp_step(totals, 1, dp_count)
     width = q_gain.shape[0]
     totals = lax.dynamic_slice_in_dim(totals, lax.axis_index("dp") * width, width, axis=1)
 
     q_grad, k_grad, v_grad = call(
         functools.partial(final_kernel, heads),
-        "final",
         [VMEM_SPEC] * 3,
         [
             (struct(q_raw.shape, BF16), HBM_SPEC),

time: 144 us -> 143 us (level)
  no operation moved by 1% of the time
where the time goes in v3:
time: 143 us; the launch traced here: 142 us
  starting transfers between devices  76.6 us (54%)
  waiting for transfers between devices  31 us (22%)
  Pallas kernels  30.7 us (21%)
  local copies, waits for them, and re-layouts  3.14 us (2%)
    ppermute x8, starting transfers between devices, dp_step(): lax.ppermute(values, 'dp', [(z, z ^ step) for z in range(dp_count)])  52 us
    pallas_call x1, Pallas kernels, shards(): call(functools.partial(attend_kernel, blocks), [SMEM_SPEC] + [VMEM_SPEC]...  24.2 us
    ppermute x8, waiting for transfers between devices, dp_step(): lax.ppermute(values, 'dp', [(z, z ^ step) for z in range(dp_count)])  20.8 us
    all_to_all x1, starting transfers between devices, shards(): arrived = lax.all_to_all(sent, 'seq', 0, 0, tiled=True)  9.62 us
    all_to_all x1, starting transfers between devices, shards(): parts = lax.all_to_all(parts, 'seq', 0, 0, tiled=True)  5.95 us
    all_to_all x1, starting transfers between devices, shards(): back = lax.all_to_all(send, 'seq', 0, 0, tiled=True)  5.08 us
    all_to_all x1, waiting for transfers between devices, shards(): parts = lax.all_to_all(parts, 'seq', 0, 0, tiled=True)  4.14 us
    all_to_all x1, waiting for transfers between devices, shards(): arrived = lax.all_to_all(sent, 'seq', 0, 0, tiled=True)  3.15 us
  transfers between devices with their start and end apart: 13, of which 11 were waited for; matrix products, arithmetic and copies ran while one was open for 1% of the time, Pallas kernels for 1%

profile of v3, /device:TPU:2, one launch (start us, length us, event | category | flops | bytes accessed | tf_op | source)
XLA Modules:
  0.0 142.3 jit_solution(2907013295313127630)
XLA Ops:
  0.6 3.0 %shard_map.110 = bf16[32,384,128]{2,1,0:T(8,128)(2,1)} custom-call(bf16[1,128,4096]{2,1,0:T(8,128)(2,1)} %q_any.1, bf16[1,128,4096]{2,1,0:T(8,128)(2,1)} %d_any.1, bf16[1,128,1024]{2,1,0:T(8,128)(2,1)} %k_ref.1, bf16[1,128,1024]{2,1,0:T(8,128)(2,1)} %v_any.1), custom_call_target="tpu_custom_call" | custom-call | tf_op jit(solution)/shard_map/pallas_call | solution.py:348
  3.6 9.6 %all-to-all-start = ((bf16[32,384,128]{2,1,0:T(8,128)(2,1)}), bf16[32,384,128]{2,1,0:T(8,128)(2,1)S(1)}, u32[]{:S(2)}, u32[]{:S(2)}) async-start(bf16[32,384,128]{2,1,0:T(8,128)(2,1)} %shard_map.110), calls=%async_computation | async-start | bytes 6291456 | tf_op jit(solution)/shard_map/all_to_all | solution.py:362
  13.5 13.7 %collective-permute-start = (f32[2,128]{1,0:T(2,128)S(1)}, f32[2,128]{1,0:T(2,128)S(1)}, u32[]{:S(2)}, u32[]{:S(2)}) collective-permute-start(f32[2,128]{1,0:T(2,128)S(1)} %compare_select_fusion), channel_id=1, source_target_pairs={{0,8},{1,9},{2,10},{3,11},{4,12},{5,13},{6,14},{7,15},{8,0},{9,1},... | collective-permute-start | bytes 3080 | tf_op jit(solution)/shard_map/ppermute | solution.py:322
  27.3 1.5 %collective-permute-done = f32[2,128]{1,0:T(2,128)S(1)} collective-permute-done((f32[2,128]{1,0:T(2,128)S(1)}, f32[2,128]{1,0:T(2,128)S(1)}, u32[]{:S(2)}, u32[]{:S(2)}) %collective-permute-start) | collective-permute-done | bytes 1056 | tf_op jit(solution)/shard_map/ppermute | solution.py:322
  28.8 6.0 %collective-permute-start.1 = (f32[2,128]{1,0:T(2,128)S(1)}, f32[2,128]{1,0:T(2,128)S(1)}, u32[]{:S(2)}, u32[]{:S(2)}) collective-permute-start(f32[2,128]{1,0:T(2,128)S(1)} %fusion), channel_id=1, source_target_pairs={{0,4},{1,5},{2,6},{3,7},{4,0},{5,1},{6,2},{7,3},{8,12},{9,13},{10,... | collective-permute-start | bytes 3080 | tf_op jit(solution)/shard_map/ppermute | solution.py:322
  34.8 3.4 %collective-permute-done.1 = f32[2,128]{1,0:T(2,128)S(1)} collective-permute-done((f32[2,128]{1,0:T(2,128)S(1)}, f32[2,128]{1,0:T(2,128)S(1)}, u32[]{:S(2)}, u32[]{:S(2)}) %collective-permute-start.1) | collective-permute-done | bytes 1056 | tf_op jit(solution)/shard_map/ppermute | solution.py:322
  38.2 3.4 %collective-permute-start.2 = (f32[2,128]{1,0:T(2,128)S(1)}, f32[2,128]{1,0:T(2,128)S(1)}, u32[]{:S(2)}, u32[]{:S(2)}) collective-permute-start(f32[2,128]{1,0:T(2,128)S(1)} %fusion.1), channel_id=1, source_target_pairs={{0,2},{1,3},{2,0},{3,1},{4,6},{5,7},{6,4},{7,5},{8,10},{9,11},{10,... | collective-permute-start | bytes 3080 | tf_op jit(solution)/shard_map/ppermute | solution.py:322
  41.6 3.0 %collective-permute-done.2 = f32[2,128]{1,0:T(2,128)S(1)} collective-permute-done((f32[2,128]{1,0:T(2,128)S(1)}, f32[2,128]{1,0:T(2,128)S(1)}, u32[]{:S(2)}, u32[]{:S(2)}) %collective-permute-start.2) | collective-permute-done | bytes 1056 | tf_op jit(solution)/shard_map/ppermute | solution.py:322
  44.6 2.9 %collective-permute-start.3 = (f32[2,128]{1,0:T(2,128)S(1)}, f32[2,128]{1,0:T(2,128)S(1)}, u32[]{:S(2)}, u32[]{:S(2)}) collective-permute-start(f32[2,128]{1,0:T(2,128)S(1)} %add.31), channel_id=1, source_target_pairs={{0,1},{1,0},{2,3},{3,2},{4,5},{5,4},{6,7},{7,6},{8,9},{9,8},{10,11... | collective-permute-start | bytes 3080 | tf_op jit(solution)/shard_map/ppermute | solution.py:322
  47.5 2.5 %collective-permute-done.3 = f32[2,128]{1,0:T(2,128)S(1)} collective-permute-done((f32[2,128]{1,0:T(2,128)S(1)}, f32[2,128]{1,0:T(2,128)S(1)}, u32[]{:S(2)}, u32[]{:S(2)}) %collective-permute-start.3) | collective-permute-done | bytes 1056 | tf_op jit(solution)/shard_map/ppermute | solution.py:322
  50.0 3.1 %all-to-all-done.got_ref = bf16[32,384,128]{2,1,0:T(8,128)(2,1)S(1)} async-done(((bf16[32,384,128]{2,1,0:T(8,128)(2,1)}), bf16[32,384,128]{2,1,0:T(8,128)(2,1)S(1)}, u32[]{:S(2)}, u32[]{:S(2)}) %all-to-all-start) | async-done | bytes 3145760 | tf_op jit(solution)/shard_map/all_to_all | solution.py:362
  53.2 1.0 slice.9
  54.2 1.9 %collective-permute-start.4 = (bf16[32,128,128]{2,1,0:T(8,128)(2,1)}, bf16[32,128,128]{2,1,0:T(8,128)(2,1)}, u32[]{:S(2)}, u32[]{:S(2)}) collective-permute-start(bf16[32,128,128]{2,1,0:T(8,128)(2,1)} %slice.9), channel_id=1, source_target_pairs={{0,16},{16,0},{32,48},{48,32},{64,80},{80,64},{96,112},{112,96},{1... | collective-permute-start | bytes 3145736 | tf_op jit(solution)/shard_map/ppermute | solution.py:366
  56.2 0.1 copy.14.pat_ref
  56.3 2.9 %collective-permute-done.4.other_ref = bf16[32,128,128]{2,1,0:T(8,128)(2,1)} collective-permute-done((bf16[32,128,128]{2,1,0:T(8,128)(2,1)}, bf16[32,128,128]{2,1,0:T(8,128)(2,1)}, u32[]{:S(2)}, u32[]{:S(2)}) %collective-permute-start.4) | collective-permute-done | bytes 1048608 | tf_op jit(solution)/shard_map/ppermute | solution.py:366
  59.1 24.2 %shard_map.111 = (bf16[32,256,128]{2,1,0:T(8,128)(2,1)}, bf16[32,128,128]{2,1,0:T(8,128)(2,1)}, bf16[32,128,128]{2,1,0:T(8,128)(2,1)}, f32[32,8,128]{2,1,0:T(8,128)}) custom-call(s32[1,32,6]{2,1,0:T(8,128)S(1)} %copy.14.pat_ref, f32[2,128]{1,0:T(2,128)S(1)} %add.32.gains_ref, bf16[32,384,128]{2,1,0:T(8,128)(2,1)S(1)} %all-to-all-done.got_ref, ...), custom_call_target="tpu_custom_call" | custom-call | tf_op jit(solution)/shard_map/pallas_call | solution.py:368
  83.3 2.0 %collective-permute-start.5 = (bf16[32,128,128]{2,1,0:T(8,128)(2,1)}, bf16[32,128,128]{2,1,0:T(8,128)(2,1)S(1)}, u32[]{:S(2)}, u32[]{:S(2)}) collective-permute-start(bf16[32,128,128]{2,1,0:T(8,128)(2,1)} %get-tuple-element.17), channel_id=1, source_target_pairs={{0,16},{16,0},{32,48},{48,32},{64,80},{80,64},{96,112},{112,96},{1... | collective-permute-start | bytes 3145736 | tf_op jit(solution)/shard_map/ppermute | solution.py:397
  85.4 6.0 %all-to-all-start.2 = ((f32[32,8,128]{2,1,0:T(8,128)}), f32[32,8,128]{2,1,0:T(8,128)S(1)}, u32[]{:S(2)}, u32[]{:S(2)}) async-start(f32[32,8,128]{2,1,0:T(8,128)} %get-tuple-element.22), calls=%async_computation.2 | async-start | bytes 262144 | tf_op jit(solution)/shard_map/all_to_all | solution.py:396
  91.3 1.2 copy-done.1
  92.6 1.3 shard_map.112
  93.9 4.1 %all-to-all-done.2.in_ref = f32[32,8,128]{2,1,0:T(8,128)S(1)} async-done(((f32[32,8,128]{2,1,0:T(8,128)}), f32[32,8,128]{2,1,0:T(8,128)S(1)}, u32[]{:S(2)}, u32[]{:S(2)}) %all-to-all-start.2) | async-done | bytes 131104 | tf_op jit(solution)/shard_map/all_to_all | solution.py:396
  98.0 5.1 %all-to-all-start.1 = ((bf16[32,256,128]{2,1,0:T(8,128)(2,1)}), bf16[32,256,128]{2,1,0:T(8,128)(2,1)S(1)}, u32[]{:S(2)}, u32[]{:S(2)}) async-start(bf16[32,256,128]{2,1,0:T(8,128)(2,1)} %shard_map.112), calls=%async_computation.1 | async-start | bytes 4194304 | tf_op jit(solution)/shard_map/all_to_all | solution.py:405
  103.2 13.6 %collective-permute-start.6 = (f32[2,128]{1,0:T(2,128)S(1)}, f32[2,128]{1,0:T(2,128)S(1)}, u32[]{:S(2)}, u32[]{:S(2)}) collective-permute-start(f32[2,128]{1,0:T(2,128)S(1)} %shard_map.114), channel_id=1, source_target_pairs={{0,8},{1,9},{2,10},{3,11},{4,12},{5,13},{6,14},{7,15},{8,0},{9,1},... | collective-permute-start | bytes 3080 | tf_op jit(solution)/shard_map/ppermute | solution.py:322
  116.8 1.5 %collective-permute-done.6 = f32[2,128]{1,0:T(2,128)S(1)} collective-permute-done((f32[2,128]{1,0:T(2,128)S(1)}, f32[2,128]{1,0:T(2,128)S(1)}, u32[]{:S(2)}, u32[]{:S(2)}) %collective-permute-start.6) | collective-permute-done | bytes 1056 | tf_op jit(solution)/shard_map/ppermute | solution.py:322
  118.3 6.0 %collective-permute-start.7 = (f32[2,128]{1,0:T(2,128)S(1)}, f32[2,128]{1,0:T(2,128)S(1)}, u32[]{:S(2)}, u32[]{:S(2)}) collective-permute-start(f32[2,128]{1,0:T(2,128)S(1)} %add.33), channel_id=1, source_target_pairs={{0,4},{1,5},{2,6},{3,7},{4,0},{5,1},{6,2},{7,3},{8,12},{9,13},{10,... | collective-permute-start | bytes 3080 | tf_op jit(solution)/shard_map/ppermute | solution.py:322
  124.3 3.3 %collective-permute-done.7 = f32[2,128]{1,0:T(2,128)S(1)} collective-permute-done((f32[2,128]{1,0:T(2,128)S(1)}, f32[2,128]{1,0:T(2,128)S(1)}, u32[]{:S(2)}, u32[]{:S(2)}) %collective-permute-start.7) | collective-permute-done | bytes 1056 | tf_op jit(solution)/shard_map/ppermute | solution.py:322
  127.7 3.4 %collective-permute-start.8 = (f32[2,128]{1,0:T(2,128)S(1)}, f32[2,128]{1,0:T(2,128)S(1)}, u32[]{:S(2)}, u32[]{:S(2)}) collective-permute-start(f32[2,128]{1,0:T(2,128)S(1)} %add.34), channel_id=1, source_target_pairs={{0,2},{1,3},{2,0},{3,1},{4,6},{5,7},{6,4},{7,5},{8,10},{9,11},{10,... | collective-permute-start | bytes 3080 | tf_op jit(solution)/shard_map/ppermute | solution.py:322
  131.1 3.0 %collective-permute-done.8 = f32[2,128]{1,0:T(2,128)S(1)} collective-permute-done((f32[2,128]{1,0:T(2,128)S(1)}, f32[2,128]{1,0:T(2,128)S(1)}, u32[]{:S(2)}, u32[]{:S(2)}) %collective-permute-start.8) | collective-permute-done | bytes 1056 | tf_op jit(solution)/shard_map/ppermute | solution.py:322
  134.1 2.9 %collective-permute-start.9 = (f32[2,128]{1,0:T(2,128)S(1)}, f32[2,128]{1,0:T(2,128)S(1)}, u32[]{:S(2)}, u32[]{:S(2)}) collective-permute-start(f32[2,128]{1,0:T(2,128)S(1)} %add.35), channel_id=1, source_target_pairs={{0,1},{1,0},{2,3},{3,2},{4,5},{5,4},{6,7},{7,6},{8,9},{9,8},{10,11... | collective-permute-start | bytes 3080 | tf_op jit(solution)/shard_map/ppermute | solution.py:322
  137.0 2.5 %collective-permute-done.9 = f32[2,128]{1,0:T(2,128)S(1)} collective-permute-done((f32[2,128]{1,0:T(2,128)S(1)}, f32[2,128]{1,0:T(2,128)S(1)}, u32[]{:S(2)}, u32[]{:S(2)}) %collective-permute-start.9) | collective-permute-done | bytes 1056 | tf_op jit(solution)/shard_map/ppermute | solution.py:322
  139.6 0.5 slice_bitcast_fusion
  140.1 2.2 %shard_map.113 = (bf16[1,128,4096]{2,1,0:T(8,128)(2,1)}, bf16[1,128,1024]{2,1,0:T(8,128)(2,1)}, bf16[1,128,1024]{2,1,0:T(8,128)(2,1)}) custom-call(bf16[32,256,128]{2,1,0:T(8,128)(2,1)S(1)} %all-to-all-done.1.in_ref, bf16[1,128,1024]{2,1,0:T(8,128)(2,1)S(1)} %copy-done, f32[2,128]{1,0:T(2,128)S(1)} %add.32.gains_ref), custom_call_target="tpu_custom_call" | custom-call | tf_op jit(solution)/shard_map/pallas_call | solution.py:414
  (28 shorter events, 0.4 us)
Async XLA Ops:
  3.6 9.7 %copy-start.3 = (f32[8]{0:T(128)S(1)}, f32[8]{0:T(128)}, u32[]{:S(2)}) copy-start(f32[8]{0:T(128)} %param.10) | copy-start | bytes 100
  3.6 9.8 %copy-start.4 = (f32[8]{0:T(128)S(1)}, f32[8]{0:T(128)}, u32[]{:S(2)}) copy-start(f32[8]{0:T(128)} %param.11) | copy-start | bytes 100
  3.6 49.6 %all-to-all-start = ((bf16[32,384,128]{2,1,0:T(8,128)(2,1)}), bf16[32,384,128]{2,1,0:T(8,128)(2,1)S(1)}, u32[]{:S(2)}, u32[]{:S(2)}) async-start(bf16[32,384,128]{2,1,0:T(8,128)(2,1)} %shard_map.110), calls=%async_computation | async-start | bytes 6291456 | tf_op jit(solution)/shard_map/all_to_all | solution.py:362
  13.3 42.9 %copy-start.2 = (s32[1,32,6]{1,0,2:T(1,128)S(1)}, s32[1,32,6]{1,0,2:T(1,128)}, u32[]{:S(2)}) copy-start(s32[1,32,6]{1,0,2:T(1,128)} %param.12) | copy-start | bytes 2308
  13.5 15.3 %collective-permute-start = (f32[2,128]{1,0:T(2,128)S(1)}, f32[2,128]{1,0:T(2,128)S(1)}, u32[]{:S(2)}, u32[]{:S(2)}) collective-permute-start(f32[2,128]{1,0:T(2,128)S(1)} %compare_select_fusion), channel_id=1, source_target_pairs={{0,8},{1,9},{2,10},{3,11},{4,12},{5,13},{6,14},{7,15},{8,0},{9,1},... | collective-permute-start | bytes 3080 | tf_op jit(solution)/shard_map/ppermute | solution.py:322
  28.8 9.4 %collective-permute-start.1 = (f32[2,128]{1,0:T(2,128)S(1)}, f32[2,128]{1,0:T(2,128)S(1)}, u32[]{:S(2)}, u32[]{:S(2)}) collective-permute-start(f32[2,128]{1,0:T(2,128)S(1)} %fusion), channel_id=1, source_target_pairs={{0,4},{1,5},{2,6},{3,7},{4,0},{5,1},{6,2},{7,3},{8,12},{9,13},{10,... | collective-permute-start | bytes 3080 | tf_op jit(solution)/shard_map/ppermute | solution.py:322
  38.2 6.4 %collective-permute-start.2 = (f32[2,128]{1,0:T(2,128)S(1)}, f32[2,128]{1,0:T(2,128)S(1)}, u32[]{:S(2)}, u32[]{:S(2)}) collective-permute-start(f32[2,128]{1,0:T(2,128)S(1)} %fusion.1), channel_id=1, source_target_pairs={{0,2},{1,3},{2,0},{3,1},{4,6},{5,7},{6,4},{7,5},{8,10},{9,11},{10,... | collective-permute-start | bytes 3080 | tf_op jit(solution)/shard_map/ppermute | solution.py:322
  44.6 5.5 %collective-permute-start.3 = (f32[2,128]{1,0:T(2,128)S(1)}, f32[2,128]{1,0:T(2,128)S(1)}, u32[]{:S(2)}, u32[]{:S(2)}) collective-permute-start(f32[2,128]{1,0:T(2,128)S(1)} %add.31), channel_id=1, source_target_pairs={{0,1},{1,0},{2,3},{3,2},{4,5},{5,4},{6,7},{7,6},{8,9},{9,8},{10,11... | collective-permute-start | bytes 3080 | tf_op jit(solution)/shard_map/ppermute | solution.py:322
  54.2 4.9 %collective-permute-start.4 = (bf16[32,128,128]{2,1,0:T(8,128)(2,1)}, bf16[32,128,128]{2,1,0:T(8,128)(2,1)}, u32[]{:S(2)}, u32[]{:S(2)}) collective-permute-start(bf16[32,128,128]{2,1,0:T(8,128)(2,1)} %slice.9), channel_id=1, source_target_pairs={{0,16},{16,0},{32,48},{48,32},{64,80},{80,64},{96,112},{112,96},{1... | collective-permute-start | bytes 3145736 | tf_op jit(solution)/shard_map/ppermute | solution.py:366
  83.3 8.0 %collective-permute-start.5 = (bf16[32,128,128]{2,1,0:T(8,128)(2,1)}, bf16[32,128,128]{2,1,0:T(8,128)(2,1)S(1)}, u32[]{:S(2)}, u32[]{:S(2)}) collective-permute-start(bf16[32,128,128]{2,1,0:T(8,128)(2,1)} %get-tuple-element.17), channel_id=1, source_target_pairs={{0,16},{16,0},{32,48},{48,32},{64,80},{80,64},{96,112},{112,96},{1... | collective-permute-start | bytes 3145736 | tf_op jit(solution)/shard_map/ppermute | solution.py:397
  85.4 12.7 %all-to-all-start.2 = ((f32[32,8,128]{2,1,0:T(8,128)}), f32[32,8,128]{2,1,0:T(8,128)S(1)}, u32[]{:S(2)}, u32[]{:S(2)}) async-start(f32[32,8,128]{2,1,0:T(8,128)} %get-tuple-element.22), calls=%async_computation.2 | async-start | bytes 262144 | tf_op jit(solution)/shard_map/all_to_all | solution.py:396
  91.3 1.2 copy-start.1
  93.9 46.2 %copy-start = (bf16[1,128,1024]{2,1,0:T(8,128)(2,1)S(1)}, bf16[1,128,1024]{2,1,0:T(8,128)(2,1)}, u32[]{:S(2)}) copy-start(bf16[1,128,1024]{2,1,0:T(8,128)(2,1)} %k_ref.1) | copy-start | bytes 786436
  98.0 42.1 %all-to-all-start.1 = ((bf16[32,256,128]{2,1,0:T(8,128)(2,1)}), bf16[32,256,128]{2,1,0:T(8,128)(2,1)S(1)}, u32[]{:S(2)}, u32[]{:S(2)}) async-start(bf16[32,256,128]{2,1,0:T(8,128)(2,1)} %shard_map.112), calls=%async_computation.1 | async-start | bytes 4194304 | tf_op jit(solution)/shard_map/all_to_all | solution.py:405
  103.2 15.2 %collective-permute-start.6 = (f32[2,128]{1,0:T(2,128)S(1)}, f32[2,128]{1,0:T(2,128)S(1)}, u32[]{:S(2)}, u32[]{:S(2)}) collective-permute-start(f32[2,128]{1,0:T(2,128)S(1)} %shard_map.114), channel_id=1, source_target_pairs={{0,8},{1,9},{2,10},{3,11},{4,12},{5,13},{6,14},{7,15},{8,0},{9,1},... | collective-permute-start | bytes 3080 | tf_op jit(solution)/shard_map/ppermute | solution.py:322
  118.3 9.4 %collective-permute-start.7 = (f32[2,128]{1,0:T(2,128)S(1)}, f32[2,128]{1,0:T(2,128)S(1)}, u32[]{:S(2)}, u32[]{:S(2)}) collective-permute-start(f32[2,128]{1,0:T(2,128)S(1)} %add.33), channel_id=1, source_target_pairs={{0,4},{1,5},{2,6},{3,7},{4,0},{5,1},{6,2},{7,3},{8,12},{9,13},{10,... | collective-permute-start | bytes 3080 | tf_op jit(solution)/shard_map/ppermute | solution.py:322
  127.7 6.4 %collective-permute-start.8 = (f32[2,128]{1,0:T(2,128)S(1)}, f32[2,128]{1,0:T(2,128)S(1)}, u32[]{:S(2)}, u32[]{:S(2)}) collective-permute-start(f32[2,128]{1,0:T(2,128)S(1)} %add.34), channel_id=1, source_target_pairs={{0,2},{1,3},{2,0},{3,1},{4,6},{5,7},{6,4},{7,5},{8,10},{9,11},{10,... | collective-permute-start | bytes 3080 | tf_op jit(solution)/shard_map/ppermute | solution.py:322
  134.1 5.5 %collective-permute-start.9 = (f32[2,128]{1,0:T(2,128)S(1)}, f32[2,128]{1,0:T(2,128)S(1)}, u32[]{:S(2)}, u32[]{:S(2)}) collective-permute-start(f32[2,128]{1,0:T(2,128)S(1)} %add.35), channel_id=1, source_target_pairs={{0,1},{1,0},{2,3},{3,2},{4,5},{5,4},{6,7},{7,6},{8,9},{9,8},{10,11... | collective-permute-start | bytes 3080 | tf_op jit(solution)/shard_map/ppermute | solution.py:322

commit v4 on v3

--- a/solution.py
+++ b/solution.py
@@ -25,13 +25,6 @@
 VMEM_SPEC = pl.BlockSpec(memory_space=pltpu.VMEM)
 SMEM_SPEC = pl.BlockSpec(memory_space=pltpu.SMEM)
 HBM_SPEC = pl.BlockSpec(memory_space=pltpu.HBM)
-
-
-def run_copies(copies):
-    for copy in copies:
-        copy.start()
-    for copy in copies:
-        copy.wait()
 
 
 def pack_kernel(heads, q_any, d_any, k_any, v_any, out_any, q_ref, d_ref, k_ref, v_ref, out_ref, sems, out_sems):
@@ -278,13 +271,29 @@
         copy.wait()
 
 
-def merge_kernel(blocks, keep_ref, got_ref, send_any, out_any, sum_ref, sem):
+def merge_kernel(blocks, keep_any, got_ref, send_any, out_any, keep_ref, sum_ref, sems, out_sems):
+    step = blocks // OUTS
+    loads = []
+    for n in range(OUTS):
+        chunk = pl.ds(n * step, step)
+        loads.append(pltpu.make_async_copy(keep_any.at[chunk], keep_ref.at[chunk], sems.at[n]))
+        loads[-1].start()
+
     def one_block(j, carry):
         sum_ref[j] = (keep_ref[j].astype(F32) + got_ref[j].astype(F32)).astype(BF16)
         return carry
 
-    lax.fori_loop(0, blocks, one_block, 0, unroll=4)
-    run_copies([pltpu.make_async_copy(sum_ref, out_any.at[:, pl.ds(BLK, BLK)], sem)])
+    outs = []
+    for n in range(OUTS):
+        loads[n].wait()
+        lax.fori_loop(n * step, (n + 1) * step, one_block, 0, unroll=4)
+        chunk = pl.ds(n * step, step)
+        outs.append(
+            pltpu.make_async_copy(sum_ref.at[chunk], out_any.at[chunk, pl.ds(BLK, BLK)], out_sems.at[n])
+        )
+        outs[-1].start()
+    for copy in outs:
+        copy.wait()
 
 
 def parts_sum_kernel(in_ref, out_ref):
@@ -397,17 +406,18 @@
     got = lax.ppermute(give, "seq", swap)
     (send,) = call(
         functools.partial(merge_kernel, blocks),
-        [VMEM_SPEC] * 2 + [HBM_SPEC],
+        [HBM_SPEC, VMEM_SPEC, HBM_SPEC],
         [(pltpu.HBM(send.shape, BF16), HBM_SPEC)],
-        [pltpu.VMEM((blocks, BLK, HD), BF16), pltpu.SemaphoreType.DMA],
+        [pltpu.VMEM((blocks, BLK, HD), BF16)] * 2 + [pltpu.SemaphoreType.DMA((OUTS,))] * 2,
         aliases={2: 0},
-    )(keep, got, send)
+    )(pltpu.with_memory_space_constraint(keep, pltpu.HBM), got, send)
     back = lax.all_to_all(send, "seq", 0, 0, tiled=True)
 
     (totals,) = call(parts_sum_kernel, [VMEM_SPEC], [(struct((2, HD), F32), VMEM_SPEC)])(parts)
-    for step in (8, 4, 2):
+    totals = dp_step(totals, 1, dp_count)
+    for step in (8, 4):
         totals = dp_step(totals, step, dp_count)
-    totals = dp_step(totals, 1, dp_count)
+    totals = dp_step(totals, 2, dp_count)
     width = q_gain.shape[0]
     totals = lax.dynamic_slice_in_dim(totals, lax.axis_index("dp") * width, width, axis=1)
 

time: 143 us -> 143 us (level)
  no operation moved by 1% of the time
where the time goes in v4:
time: 143 us; the launch traced here: 142 us
  starting transfers between devices  75.6 us (53%)
  waiting for transfers between devices  32.4 us (23%)
  Pallas kernels  31.5 us (22%)
  local copies, waits for them, and re-layouts  1.92 us (1%)
    ppermute x8, starting transfers between devices, dp_step(): lax.ppermute(values, 'dp', [(z, z ^ step) for z in range(dp_count)])  51 us
    pallas_call x1, Pallas kernels, shards(): call(functools.partial(attend_kernel, blocks), [SMEM_SPEC] + [VMEM_SPEC]...  24.2 us
    ppermute x8, waiting for transfers between devices, dp_step(): lax.ppermute(values, 'dp', [(z, z ^ step) for z in range(dp_count)])  21.8 us
    all_to_all x1, starting transfers between devices, shards(): arrived = lax.all_to_all(sent, 'seq', 0, 0, tiled=True)  9.62 us
    all_to_all x1, starting transfers between devices, shards(): parts = lax.all_to_all(parts, 'seq', 0, 0, tiled=True)  5.92 us
    all_to_all x1, starting transfers between devices, shards(): back = lax.all_to_all(send, 'seq', 0, 0, tiled=True)  5.08 us
    all_to_all x1, waiting for transfers between devices, shards(): parts = lax.all_to_all(parts, 'seq', 0, 0, tiled=True)  4.59 us
    all_to_all x1, waiting for transfers between devices, shards(): arrived = lax.all_to_all(sent, 'seq', 0, 0, tiled=True)  3.15 us
  transfers between devices with their start and end apart: 13, of which 11 were waited for; matrix products, arithmetic and copies ran while one was open for 1% of the time, Pallas kernels for 1%

profile of v4, /device:TPU:2, one launch (start us, length us, event | category | flops | bytes accessed | tf_op | source)
XLA Modules:
  0.0 142.4 jit_solution(2419812484549334675)
XLA Ops:
  0.6 3.0 %shard_map.110 = bf16[32,384,128]{2,1,0:T(8,128)(2,1)} custom-call(bf16[1,128,4096]{2,1,0:T(8,128)(2,1)} %q_any.1, bf16[1,128,4096]{2,1,0:T(8,128)(2,1)} %d_any.1, bf16[1,128,1024]{2,1,0:T(8,128)(2,1)} %k_ref.1, bf16[1,128,1024]{2,1,0:T(8,128)(2,1)} %v_any.1), custom_call_target="tpu_custom_call" | custom-call | tf_op jit(solution)/shard_map/pallas_call | solution.py:357
  3.6 9.6 %all-to-all-start = ((bf16[32,384,128]{2,1,0:T(8,128)(2,1)}), bf16[32,384,128]{2,1,0:T(8,128)(2,1)S(1)}, u32[]{:S(2)}, u32[]{:S(2)}) async-start(bf16[32,384,128]{2,1,0:T(8,128)(2,1)} %shard_map.110), calls=%async_computation | async-start | bytes 6291456 | tf_op jit(solution)/shard_map/all_to_all | solution.py:371
  13.4 0.1 broadcast_in_dim_tile.7
  13.5 13.7 %collective-permute-start = (f32[2,128]{1,0:T(2,128)S(1)}, f32[2,128]{1,0:T(2,128)S(1)}, u32[]{:S(2)}, u32[]{:S(2)}) collective-permute-start(f32[2,128]{1,0:T(2,128)S(1)} %compare_select_fusion), channel_id=1, source_target_pairs={{0,8},{1,9},{2,10},{3,11},{4,12},{5,13},{6,14},{7,15},{8,0},{9,1},... | collective-permute-start | bytes 3080 | tf_op jit(solution)/shard_map/ppermute | solution.py:331
  27.3 1.5 %collective-permute-done = f32[2,128]{1,0:T(2,128)S(1)} collective-permute-done((f32[2,128]{1,0:T(2,128)S(1)}, f32[2,128]{1,0:T(2,128)S(1)}, u32[]{:S(2)}, u32[]{:S(2)}) %collective-permute-start) | collective-permute-done | bytes 1056 | tf_op jit(solution)/shard_map/ppermute | solution.py:331
  28.8 6.0 %collective-permute-start.1 = (f32[2,128]{1,0:T(2,128)S(1)}, f32[2,128]{1,0:T(2,128)S(1)}, u32[]{:S(2)}, u32[]{:S(2)}) collective-permute-start(f32[2,128]{1,0:T(2,128)S(1)} %fusion), channel_id=1, source_target_pairs={{0,4},{1,5},{2,6},{3,7},{4,0},{5,1},{6,2},{7,3},{8,12},{9,13},{10,... | collective-permute-start | bytes 3080 | tf_op jit(solution)/shard_map/ppermute | solution.py:331
  34.9 3.4 %collective-permute-done.1 = f32[2,128]{1,0:T(2,128)S(1)} collective-permute-done((f32[2,128]{1,0:T(2,128)S(1)}, f32[2,128]{1,0:T(2,128)S(1)}, u32[]{:S(2)}, u32[]{:S(2)}) %collective-permute-start.1) | collective-permute-done | bytes 1056 | tf_op jit(solution)/shard_map/ppermute | solution.py:331
  38.2 3.4 %collective-permute-start.2 = (f32[2,128]{1,0:T(2,128)S(1)}, f32[2,128]{1,0:T(2,128)S(1)}, u32[]{:S(2)}, u32[]{:S(2)}) collective-permute-start(f32[2,128]{1,0:T(2,128)S(1)} %fusion.1), channel_id=1, source_target_pairs={{0,2},{1,3},{2,0},{3,1},{4,6},{5,7},{6,4},{7,5},{8,10},{9,11},{10,... | collective-permute-start | bytes 3080 | tf_op jit(solution)/shard_map/ppermute | solution.py:331
  41.6 3.0 %collective-permute-done.2 = f32[2,128]{1,0:T(2,128)S(1)} collective-permute-done((f32[2,128]{1,0:T(2,128)S(1)}, f32[2,128]{1,0:T(2,128)S(1)}, u32[]{:S(2)}, u32[]{:S(2)}) %collective-permute-start.2) | collective-permute-done | bytes 1056 | tf_op jit(solution)/shard_map/ppermute | solution.py:331
  44.6 2.9 %collective-permute-start.3 = (f32[2,128]{1,0:T(2,128)S(1)}, f32[2,128]{1,0:T(2,128)S(1)}, u32[]{:S(2)}, u32[]{:S(2)}) collective-permute-start(f32[2,128]{1,0:T(2,128)S(1)} %add.31), channel_id=1, source_target_pairs={{0,1},{1,0},{2,3},{3,2},{4,5},{5,4},{6,7},{7,6},{8,9},{9,8},{10,11... | collective-permute-start | bytes 3080 | tf_op jit(solution)/shard_map/ppermute | solution.py:331
  47.5 2.5 %collective-permute-done.3 = f32[2,128]{1,0:T(2,128)S(1)} collective-permute-done((f32[2,128]{1,0:T(2,128)S(1)}, f32[2,128]{1,0:T(2,128)S(1)}, u32[]{:S(2)}, u32[]{:S(2)}) %collective-permute-start.3) | collective-permute-done | bytes 1056 | tf_op jit(solution)/shard_map/ppermute | solution.py:331
  50.1 3.1 %all-to-all-done.got_ref = bf16[32,384,128]{2,1,0:T(8,128)(2,1)S(1)} async-done(((bf16[32,384,128]{2,1,0:T(8,128)(2,1)}), bf16[32,384,128]{2,1,0:T(8,128)(2,1)S(1)}, u32[]{:S(2)}, u32[]{:S(2)}) %all-to-all-start) | async-done | bytes 3145760 | tf_op jit(solution)/shard_map/all_to_all | solution.py:371
  53.2 1.0 slice.9
  54.2 1.9 %collective-permute-start.4 = (bf16[32,128,128]{2,1,0:T(8,128)(2,1)}, bf16[32,128,128]{2,1,0:T(8,128)(2,1)}, u32[]{:S(2)}, u32[]{:S(2)}) collective-permute-start(bf16[32,128,128]{2,1,0:T(8,128)(2,1)} %slice.9), channel_id=1, source_target_pairs={{0,16},{16,0},{32,48},{48,32},{64,80},{80,64},{96,112},{112,96},{1... | collective-permute-start | bytes 3145736 | tf_op jit(solution)/shard_map/ppermute | solution.py:375
  56.2 0.1 copy.14.pat_ref
  56.3 2.9 %collective-permute-done.4.other_ref = bf16[32,128,128]{2,1,0:T(8,128)(2,1)} collective-permute-done((bf16[32,128,128]{2,1,0:T(8,128)(2,1)}, bf16[32,128,128]{2,1,0:T(8,128)(2,1)}, u32[]{:S(2)}, u32[]{:S(2)}) %collective-permute-start.4) | collective-permute-done | bytes 1048608 | tf_op jit(solution)/shard_map/ppermute | solution.py:375
  59.1 24.2 %shard_map.111 = (bf16[32,256,128]{2,1,0:T(8,128)(2,1)}, bf16[32,128,128]{2,1,0:T(8,128)(2,1)}, bf16[32,128,128]{2,1,0:T(8,128)(2,1)}, f32[32,8,128]{2,1,0:T(8,128)}) custom-call(s32[1,32,6]{2,1,0:T(8,128)S(1)} %copy.14.pat_ref, f32[2,128]{1,0:T(2,128)S(1)} %add.32.gains_ref, bf16[32,384,128]{2,1,0:T(8,128)(2,1)S(1)} %all-to-all-done.got_ref, ...), custom_call_target="tpu_custom_call" | custom-call | tf_op jit(solution)/shard_map/pallas_call | solution.py:377
  83.3 2.1 %collective-permute-start.5 = (bf16[32,128,128]{2,1,0:T(8,128)(2,1)}, bf16[32,128,128]{2,1,0:T(8,128)(2,1)S(1)}, u32[]{:S(2)}, u32[]{:S(2)}) collective-permute-start(bf16[32,128,128]{2,1,0:T(8,128)(2,1)} %get-tuple-element.17), channel_id=1, source_target_pairs={{0,16},{16,0},{32,48},{48,32},{64,80},{80,64},{96,112},{112,96},{1... | collective-permute-start | bytes 3145736 | tf_op jit(solution)/shard_map/ppermute | solution.py:406
  85.4 5.9 %all-to-all-start.2 = ((f32[32,8,128]{2,1,0:T(8,128)}), f32[32,8,128]{2,1,0:T(8,128)S(1)}, u32[]{:S(2)}, u32[]{:S(2)}) async-start(f32[32,8,128]{2,1,0:T(8,128)} %get-tuple-element.22), calls=%async_computation.2 | async-start | bytes 262144 | tf_op jit(solution)/shard_map/all_to_all | solution.py:405
  91.3 2.1 %shard_map.112 = bf16[32,256,128]{2,1,0:T(8,128)(2,1)} custom-call(bf16[32,128,128]{2,1,0:T(8,128)(2,1)} %get-tuple-element.16.keep_any, bf16[32,128,128]{2,1,0:T(8,128)(2,1)S(1)} %collective-permute-done.5.got_ref, bf16[32,256,128]{2,1,0:T(8,128)(2,1)} %get-tuple-element.18.send_any), custom_call_target="tpu_custom_call", output_to_operand_aliasing={{}: (2, {})} | custom-call | tf_op jit(solution)/shard_map/pallas_call | solution.py:407
  93.4 4.6 %all-to-all-done.2.in_ref = f32[32,8,128]{2,1,0:T(8,128)S(1)} async-done(((f32[32,8,128]{2,1,0:T(8,128)}), f32[32,8,128]{2,1,0:T(8,128)S(1)}, u32[]{:S(2)}, u32[]{:S(2)}) %all-to-all-start.2) | async-done | bytes 131104 | tf_op jit(solution)/shard_map/all_to_all | solution.py:405
  98.0 5.1 %all-to-all-start.1 = ((bf16[32,256,128]{2,1,0:T(8,128)(2,1)}), bf16[32,256,128]{2,1,0:T(8,128)(2,1)S(1)}, u32[]{:S(2)}, u32[]{:S(2)}) async-start(bf16[32,256,128]{2,1,0:T(8,128)(2,1)} %shard_map.112), calls=%async_computation.1 | async-start | bytes 4194304 | tf_op jit(solution)/shard_map/all_to_all | solution.py:414
  103.2 1.9 %collective-permute-start.6 = (f32[2,128]{1,0:T(2,128)S(1)}, f32[2,128]{1,0:T(2,128)S(1)}, u32[]{:S(2)}, u32[]{:S(2)}) collective-permute-start(f32[2,128]{1,0:T(2,128)S(1)} %shard_map.114), channel_id=1, source_target_pairs={{0,1},{1,0},{2,3},{3,2},{4,5},{5,4},{6,7},{7,6},{8,9},{9,8},{10,11... | collective-permute-start | bytes 3080 | tf_op jit(solution)/shard_map/ppermute | solution.py:331
  105.1 3.5 %collective-permute-done.6 = f32[2,128]{1,0:T(2,128)S(1)} collective-permute-done((f32[2,128]{1,0:T(2,128)S(1)}, f32[2,128]{1,0:T(2,128)S(1)}, u32[]{:S(2)}, u32[]{:S(2)}) %collective-permute-start.6) | collective-permute-done | bytes 1056 | tf_op jit(solution)/shard_map/ppermute | solution.py:331
  108.6 13.6 %collective-permute-start.7 = (f32[2,128]{1,0:T(2,128)S(1)}, f32[2,128]{1,0:T(2,128)S(1)}, u32[]{:S(2)}, u32[]{:S(2)}) collective-permute-start(f32[2,128]{1,0:T(2,128)S(1)} %add.33), channel_id=1, source_target_pairs={{0,8},{1,9},{2,10},{3,11},{4,12},{5,13},{6,14},{7,15},{8,0},{9,1},... | collective-permute-start | bytes 3080 | tf_op jit(solution)/shard_map/ppermute | solution.py:331
  122.3 1.5 %collective-permute-done.7 = f32[2,128]{1,0:T(2,128)S(1)} collective-permute-done((f32[2,128]{1,0:T(2,128)S(1)}, f32[2,128]{1,0:T(2,128)S(1)}, u32[]{:S(2)}, u32[]{:S(2)}) %collective-permute-start.7) | collective-permute-done | bytes 1056 | tf_op jit(solution)/shard_map/ppermute | solution.py:331
  123.8 6.0 %collective-permute-start.8 = (f32[2,128]{1,0:T(2,128)S(1)}, f32[2,128]{1,0:T(2,128)S(1)}, u32[]{:S(2)}, u32[]{:S(2)}) collective-permute-start(f32[2,128]{1,0:T(2,128)S(1)} %add.34), channel_id=1, source_target_pairs={{0,4},{1,5},{2,6},{3,7},{4,0},{5,1},{6,2},{7,3},{8,12},{9,13},{10,... | collective-permute-start | bytes 3080 | tf_op jit(solution)/shard_map/ppermute | solution.py:331
  129.8 3.4 %collective-permute-done.8 = f32[2,128]{1,0:T(2,128)S(1)} collective-permute-done((f32[2,128]{1,0:T(2,128)S(1)}, f32[2,128]{1,0:T(2,128)S(1)}, u32[]{:S(2)}, u32[]{:S(2)}) %collective-permute-start.8) | collective-permute-done | bytes 1056 | tf_op jit(solution)/shard_map/ppermute | solution.py:331
  133.2 3.4 %collective-permute-start.9 = (f32[2,128]{1,0:T(2,128)S(1)}, f32[2,128]{1,0:T(2,128)S(1)}, u32[]{:S(2)}, u32[]{:S(2)}) collective-permute-start(f32[2,128]{1,0:T(2,128)S(1)} %add.35), channel_id=1, source_target_pairs={{0,2},{1,3},{2,0},{3,1},{4,6},{5,7},{6,4},{7,5},{8,10},{9,11},{10,... | collective-permute-start | bytes 3080 | tf_op jit(solution)/shard_map/ppermute | solution.py:331
  136.6 3.0 %collective-permute-done.9 = f32[2,128]{1,0:T(2,128)S(1)} collective-permute-done((f32[2,128]{1,0:T(2,128)S(1)}, f32[2,128]{1,0:T(2,128)S(1)}, u32[]{:S(2)}, u32[]{:S(2)}) %collective-permute-start.9) | collective-permute-done | bytes 1056 | tf_op jit(solution)/shard_map/ppermute | solution.py:331
  139.6 0.5 slice_bitcast_fusion
  140.1 2.2 %shard_map.113 = (bf16[1,128,4096]{2,1,0:T(8,128)(2,1)}, bf16[1,128,1024]{2,1,0:T(8,128)(2,1)}, bf16[1,128,1024]{2,1,0:T(8,128)(2,1)}) custom-call(bf16[32,256,128]{2,1,0:T(8,128)(2,1)S(1)} %all-to-all-done.1.in_ref, bf16[1,128,1024]{2,1,0:T(8,128)(2,1)S(1)} %copy-done, f32[2,128]{1,0:T(2,128)S(1)} %add.32.gains_ref), custom_call_target="tpu_custom_call" | custom-call | tf_op jit(solution)/shard_map/pallas_call | solution.py:424
  (26 shorter events, 0.3 us)
Async XLA Ops:
  3.6 9.7 %copy-start.2 = (f32[8]{0:T(128)S(1)}, f32[8]{0:T(128)}, u32[]{:S(2)}) copy-start(f32[8]{0:T(128)} %param.10) | copy-start | bytes 100
  3.6 9.8 %copy-start.3 = (f32[8]{0:T(128)S(1)}, f32[8]{0:T(128)}, u32[]{:S(2)}) copy-start(f32[8]{0:T(128)} %param.11) | copy-start | bytes 100
  3.6 49.6 %all-to-all-start = ((bf16[32,384,128]{2,1,0:T(8,128)(2,1)}), bf16[32,384,128]{2,1,0:T(8,128)(2,1)S(1)}, u32[]{:S(2)}, u32[]{:S(2)}) async-start(bf16[32,384,128]{2,1,0:T(8,128)(2,1)} %shard_map.110), calls=%async_computation | async-start | bytes 6291456 | tf_op jit(solution)/shard_map/all_to_all | solution.py:371
  13.3 42.9 %copy-start.1 = (s32[1,32,6]{1,0,2:T(1,128)S(1)}, s32[1,32,6]{1,0,2:T(1,128)}, u32[]{:S(2)}) copy-start(s32[1,32,6]{1,0,2:T(1,128)} %param.12) | copy-start | bytes 2308
  13.5 15.3 %collective-permute-start = (f32[2,128]{1,0:T(2,128)S(1)}, f32[2,128]{1,0:T(2,128)S(1)}, u32[]{:S(2)}, u32[]{:S(2)}) collective-permute-start(f32[2,128]{1,0:T(2,128)S(1)} %compare_select_fusion), channel_id=1, source_target_pairs={{0,8},{1,9},{2,10},{3,11},{4,12},{5,13},{6,14},{7,15},{8,0},{9,1},... | collective-permute-start | bytes 3080 | tf_op jit(solution)/shard_map/ppermute | solution.py:331
  28.8 9.4 %collective-permute-start.1 = (f32[2,128]{1,0:T(2,128)S(1)}, f32[2,128]{1,0:T(2,128)S(1)}, u32[]{:S(2)}, u32[]{:S(2)}) collective-permute-start(f32[2,128]{1,0:T(2,128)S(1)} %fusion), channel_id=1, source_target_pairs={{0,4},{1,5},{2,6},{3,7},{4,0},{5,1},{6,2},{7,3},{8,12},{9,13},{10,... | collective-permute-start | bytes 3080 | tf_op jit(solution)/shard_map/ppermute | solution.py:331
  38.2 6.4 %collective-permute-start.2 = (f32[2,128]{1,0:T(2,128)S(1)}, f32[2,128]{1,0:T(2,128)S(1)}, u32[]{:S(2)}, u32[]{:S(2)}) collective-permute-start(f32[2,128]{1,0:T(2,128)S(1)} %fusion.1), channel_id=1, source_target_pairs={{0,2},{1,3},{2,0},{3,1},{4,6},{5,7},{6,4},{7,5},{8,10},{9,11},{10,... | collective-permute-start | bytes 3080 | tf_op jit(solution)/shard_map/ppermute | solution.py:331
  44.6 5.5 %collective-permute-start.3 = (f32[2,128]{1,0:T(2,128)S(1)}, f32[2,128]{1,0:T(2,128)S(1)}, u32[]{:S(2)}, u32[]{:S(2)}) collective-permute-start(f32[2,128]{1,0:T(2,128)S(1)} %add.31), channel_id=1, source_target_pairs={{0,1},{1,0},{2,3},{3,2},{4,5},{5,4},{6,7},{7,6},{8,9},{9,8},{10,11... | collective-permute-start | bytes 3080 | tf_op jit(solution)/shard_map/ppermute | solution.py:331
  54.2 4.9 %collective-permute-start.4 = (bf16[32,128,128]{2,1,0:T(8,128)(2,1)}, bf16[32,128,128]{2,1,0:T(8,128)(2,1)}, u32[]{:S(2)}, u32[]{:S(2)}) collective-permute-start(bf16[32,128,128]{2,1,0:T(8,128)(2,1)} %slice.9), channel_id=1, source_target_pairs={{0,16},{16,0},{32,48},{48,32},{64,80},{80,64},{96,112},{112,96},{1... | collective-permute-start | bytes 3145736 | tf_op jit(solution)/shard_map/ppermute | solution.py:375
  83.3 8.0 %collective-permute-start.5 = (bf16[32,128,128]{2,1,0:T(8,128)(2,1)}, bf16[32,128,128]{2,1,0:T(8,128)(2,1)S(1)}, u32[]{:S(2)}, u32[]{:S(2)}) collective-permute-start(bf16[32,128,128]{2,1,0:T(8,128)(2,1)} %get-tuple-element.17), channel_id=1, source_target_pairs={{0,16},{16,0},{32,48},{48,32},{64,80},{80,64},{96,112},{112,96},{1... | collective-permute-start | bytes 3145736 | tf_op jit(solution)/shard_map/ppermute | solution.py:406
  85.4 12.6 %all-to-all-start.2 = ((f32[32,8,128]{2,1,0:T(8,128)}), f32[32,8,128]{2,1,0:T(8,128)S(1)}, u32[]{:S(2)}, u32[]{:S(2)}) async-start(f32[32,8,128]{2,1,0:T(8,128)} %get-tuple-element.22), calls=%async_computation.2 | async-start | bytes 262144 | tf_op jit(solution)/shard_map/all_to_all | solution.py:405
  93.4 46.7 %copy-start = (bf16[1,128,1024]{2,1,0:T(8,128)(2,1)S(1)}, bf16[1,128,1024]{2,1,0:T(8,128)(2,1)}, u32[]{:S(2)}) copy-start(bf16[1,128,1024]{2,1,0:T(8,128)(2,1)} %k_ref.1) | copy-start | bytes 786436
  98.0 42.1 %all-to-all-start.1 = ((bf16[32,256,128]{2,1,0:T(8,128)(2,1)}), bf16[32,256,128]{2,1,0:T(8,128)(2,1)S(1)}, u32[]{:S(2)}, u32[]{:S(2)}) async-start(bf16[32,256,128]{2,1,0:T(8,128)(2,1)} %shard_map.112), calls=%async_computation.1 | async-start | bytes 4194304 | tf_op jit(solution)/shard_map/all_to_all | solution.py:414
  103.2 5.5 %collective-permute-start.6 = (f32[2,128]{1,0:T(2,128)S(1)}, f32[2,128]{1,0:T(2,128)S(1)}, u32[]{:S(2)}, u32[]{:S(2)}) collective-permute-start(f32[2,128]{1,0:T(2,128)S(1)} %shard_map.114), channel_id=1, source_target_pairs={{0,1},{1,0},{2,3},{3,2},{4,5},{5,4},{6,7},{7,6},{8,9},{9,8},{10,11... | collective-permute-start | bytes 3080 | tf_op jit(solution)/shard_map/ppermute | solution.py:331
  108.6 15.2 %collective-permute-start.7 = (f32[2,128]{1,0:T(2,128)S(1)}, f32[2,128]{1,0:T(2,128)S(1)}, u32[]{:S(2)}, u32[]{:S(2)}) collective-permute-start(f32[2,128]{1,0:T(2,128)S(1)} %add.33), channel_id=1, source_target_pairs={{0,8},{1,9},{2,10},{3,11},{4,12},{5,13},{6,14},{7,15},{8,0},{9,1},... | collective-permute-start | bytes 3080 | tf_op jit(solution)/shard_map/ppermute | solution.py:331
  123.8 9.4 %collective-permute-start.8 = (f32[2,128]{1,0:T(2,128)S(1)}, f32[2,128]{1,0:T(2,128)S(1)}, u32[]{:S(2)}, u32[]{:S(2)}) collective-permute-start(f32[2,128]{1,0:T(2,128)S(1)} %add.34), channel_id=1, source_target_pairs={{0,4},{1,5},{2,6},{3,7},{4,0},{5,1},{6,2},{7,3},{8,12},{9,13},{10,... | collective-permute-start | bytes 3080 | tf_op jit(solution)/shard_map/ppermute | solution.py:331
  133.2 6.4 %collective-permute-start.9 = (f32[2,128]{1,0:T(2,128)S(1)}, f32[2,128]{1,0:T(2,128)S(1)}, u32[]{:S(2)}, u32[]{:S(2)}) collective-permute-start(f32[2,128]{1,0:T(2,128)S(1)} %add.35), channel_id=1, source_target_pairs={{0,2},{1,3},{2,0},{3,1},{4,6},{5,7},{6,4},{7,5},{8,10},{9,11},{10,... | collective-permute-start | bytes 3080 | tf_op jit(solution)/shard_map/ppermute | solution.py:331

commit v5 on v4

--- a/solution.py
+++ b/solution.py
@@ -78,15 +78,15 @@
 
 SCALE = 1.0 / math.sqrt(HD)
 SCALE2 = SCALE * math.log2(math.e)
-CHUNK = 8
+CHUNK = 16
 GROUPS = [list(range(s, s + 2)) for s in range(0, SLOTS, 2)]
 
 
 def attend_kernel(
-    blocks, pat_ref, gains_ref, got_ref, other_ref,
+    blocks, pat_ref, gains_ref, got_ref, other_any,
     send_any, keep_any, give_any, parts_ref,
-    dq_ref, keep_ref, give_ref, acc_ref, lead_ref, lead_dq_ref, kv_ref, kt_ref, khat_ref, qn_ref,
-    s0, s1, g0, g1, x0, x1, peak_ref, sem, give_sems, keep_sems,
+    other_ref, dq_ref, keep_ref, give_ref, acc_ref, lead_ref, lead_dq_ref, kv_ref, kt_ref, khat_ref, qn_ref,
+    s0, s1, g0, g1, x0, x1, peak_ref, sem, other_sem, give_sems, keep_sems,
 ):
     s_refs, g_refs, x_refs = (s0, s1), (g0, g1), (x0, x1)
     q_gain = gains_ref[0:1, :]
@@ -94,20 +94,26 @@
     zeros = jnp.zeros((BLK, HD), BF16)
     own_k, own_v = pl.ds(2 * BLK, HALF), pl.ds(2 * BLK + HALF, HALF)
 
-    def normalise(j, carry):
+    def normalise_queries(j, carry):
+        q_raw = got_ref[j, 0:BLK, :].astype(F32)
+        qn_ref[j] = (q_raw * inverse_rms(q_raw) * q_gain).astype(BF16)
+        return carry
+
+    def normalise_keys(j, carry):
         k_raw = jnp.concatenate([got_ref[j, own_k, :], other_ref[j, 0:HALF, :]], axis=0).astype(F32)
         k_hat = k_raw * inverse_rms(k_raw)
         k_low = (k_hat * k_gain).astype(BF16)
-        q_raw = got_ref[j, 0:BLK, :].astype(F32)
-        q_low = (q_raw * inverse_rms(q_raw) * q_gain).astype(BF16)
         khat_ref[j] = k_hat
         kv_ref[j, :, 0:HD] = k_low
         kv_ref[j, :, HD : 2 * HD] = jnp.concatenate([got_ref[j, own_v, :], other_ref[j, HALF:BLK, :]], axis=0)
         kt_ref[j] = k_low.T
-        qn_ref[j] = q_low
         return carry
 
-    lax.fori_loop(0, blocks, normalise, 0, unroll=4)
+    other_copy = pltpu.make_async_copy(other_any, other_ref, other_sem)
+    other_copy.start()
+    lax.fori_loop(0, blocks, normalise_queries, 0, unroll=8)
+    other_copy.wait()
+    lax.fori_loop(0, blocks, normalise_keys, 0, unroll=4)
 
     def pair_of(b):
         d_low = got_ref[b, BLK : 2 * BLK, :]
@@ -376,7 +382,7 @@
 
     send, keep, give, parts = call(
         functools.partial(attend_kernel, blocks),
-        [SMEM_SPEC] + [VMEM_SPEC] * 3,
+        [SMEM_SPEC] + [VMEM_SPEC] * 2 + [HBM_SPEC],
         [
             (pltpu.HBM((blocks, 2 * BLK, HD), BF16), HBM_SPEC),
             (pltpu.HBM((blocks, BLK, HD), BF16), HBM_SPEC),
@@ -384,6 +390,7 @@
             (struct((blocks, PARTS, HD), F32), VMEM_SPEC),
         ],
         [
+            pltpu.VMEM((blocks, BLK, HD), BF16),
             pltpu.VMEM((blocks, BLK, HD), BF16),
             pltpu.VMEM((blocks, BLK, HD), BF16),
             pltpu.VMEM((blocks, BLK, HD), BF16),
@@ -397,10 +404,11 @@
         ]
         + [pltpu.VMEM((SLOTS * BLK, BLK), F32)] * 4
         + [pltpu.VMEM((SLOTS * BLK, BLK), BF16)] * 2
-        + [pltpu.VMEM((2, 8, BLK), F32), pltpu.SemaphoreType.DMA]
+        + [pltpu.VMEM((2, 8, BLK), F32)]
+        + [pltpu.SemaphoreType.DMA] * 2
         + [pltpu.SemaphoreType.DMA((OUTS,))] * 2,
         mib=40,
-    )(key_blocks, gains, arrived, other)
+    )(key_blocks, gains, arrived, pltpu.with_memory_space_constraint(other, pltpu.HBM))
 
     parts = lax.all_to_all(parts, "seq", 0, 0, tiled=True)
     got = lax.ppermute(give, "seq", swap)

time: 143 us -> 143 us (level)
  no operation moved by 1% of the time
where the time goes in v5:
time: 143 us; the launch traced here: 142 us
  starting transfers between devices  75.5 us (53%)
  waiting for transfers between devices  32.4 us (23%)
  Pallas kernels  31 us (22%)
  local copies, waits for them, and re-layouts  1.92 us (1%)
    ppermute x8, starting transfers between devices, dp_step(): lax.ppermute(values, 'dp', [(z, z ^ step) for z in range(dp_count)])  51 us
    pallas_call x1, Pallas kernels, shards(): call(functools.partial(attend_kernel, blocks), [SMEM_SPEC] + [VMEM_SPEC]...  23.7 us
    ppermute x8, waiting for transfers between devices, dp_step(): lax.ppermute(values, 'dp', [(z, z ^ step) for z in range(dp_count)])  21.8 us
    all_to_all x1, starting transfers between devices, shards(): arrived = lax.all_to_all(sent, 'seq', 0, 0, tiled=True)  9.62 us
    all_to_all x1, starting transfers between devices, shards(): parts = lax.all_to_all(parts, 'seq', 0, 0, tiled=True)  5.94 us
    all_to_all x1, starting transfers between devices, shards(): back = lax.all_to_all(send, 'seq', 0, 0, tiled=True)  5.08 us
    all_to_all x1, waiting for transfers between devices, shards(): parts = lax.all_to_all(parts, 'seq', 0, 0, tiled=True)  4.59 us
    all_to_all x1, waiting for transfers between devices, shards(): arrived = lax.all_to_all(sent, 'seq', 0, 0, tiled=True)  3.15 us
  transfers between devices with their start and end apart: 13, of which 11 were waited for; matrix products, arithmetic and copies ran while one was open for 1% of the time, Pallas kernels for 1%

profile of v5, /device:TPU:2, one launch (start us, length us, event | category | flops | bytes accessed | tf_op | source)
XLA Modules:
  0.0 141.9 jit_solution(1783996612978889833)
XLA Ops:
  0.6 3.0 %shard_map.110 = bf16[32,384,128]{2,1,0:T(8,128)(2,1)} custom-call(bf16[1,128,4096]{2,1,0:T(8,128)(2,1)} %q_any.1, bf16[1,128,4096]{2,1,0:T(8,128)(2,1)} %d_any.1, bf16[1,128,1024]{2,1,0:T(8,128)(2,1)} %k_ref.1, bf16[1,128,1024]{2,1,0:T(8,128)(2,1)} %v_any.1), custom_call_target="tpu_custom_call" | custom-call | tf_op jit(solution)/shard_map/pallas_call | solution.py:363
  3.6 9.6 %all-to-all-start = ((bf16[32,384,128]{2,1,0:T(8,128)(2,1)}), bf16[32,384,128]{2,1,0:T(8,128)(2,1)S(1)}, u32[]{:S(2)}, u32[]{:S(2)}) async-start(bf16[32,384,128]{2,1,0:T(8,128)(2,1)} %shard_map.110), calls=%async_computation | async-start | bytes 6291456 | tf_op jit(solution)/shard_map/all_to_all | solution.py:377
  13.4 0.1 broadcast_in_dim_tile.7
  13.5 13.7 %collective-permute-start = (f32[2,128]{1,0:T(2,128)S(1)}, f32[2,128]{1,0:T(2,128)S(1)}, u32[]{:S(2)}, u32[]{:S(2)}) collective-permute-start(f32[2,128]{1,0:T(2,128)S(1)} %compare_select_fusion), channel_id=1, source_target_pairs={{0,8},{1,9},{2,10},{3,11},{4,12},{5,13},{6,14},{7,15},{8,0},{9,1},... | collective-permute-start | bytes 3080 | tf_op jit(solution)/shard_map/ppermute | solution.py:337
  27.3 1.5 %collective-permute-done = f32[2,128]{1,0:T(2,128)S(1)} collective-permute-done((f32[2,128]{1,0:T(2,128)S(1)}, f32[2,128]{1,0:T(2,128)S(1)}, u32[]{:S(2)}, u32[]{:S(2)}) %collective-permute-start) | collective-permute-done | bytes 1056 | tf_op jit(solution)/shard_map/ppermute | solution.py:337
  28.8 6.0 %collective-permute-start.1 = (f32[2,128]{1,0:T(2,128)S(1)}, f32[2,128]{1,0:T(2,128)S(1)}, u32[]{:S(2)}, u32[]{:S(2)}) collective-permute-start(f32[2,128]{1,0:T(2,128)S(1)} %fusion), channel_id=1, source_target_pairs={{0,4},{1,5},{2,6},{3,7},{4,0},{5,1},{6,2},{7,3},{8,12},{9,13},{10,... | collective-permute-start | bytes 3080 | tf_op jit(solution)/shard_map/ppermute | solution.py:337
  34.9 3.4 %collective-permute-done.1 = f32[2,128]{1,0:T(2,128)S(1)} collective-permute-done((f32[2,128]{1,0:T(2,128)S(1)}, f32[2,128]{1,0:T(2,128)S(1)}, u32[]{:S(2)}, u32[]{:S(2)}) %collective-permute-start.1) | collective-permute-done | bytes 1056 | tf_op jit(solution)/shard_map/ppermute | solution.py:337
  38.2 3.4 %collective-permute-start.2 = (f32[2,128]{1,0:T(2,128)S(1)}, f32[2,128]{1,0:T(2,128)S(1)}, u32[]{:S(2)}, u32[]{:S(2)}) collective-permute-start(f32[2,128]{1,0:T(2,128)S(1)} %fusion.1), channel_id=1, source_target_pairs={{0,2},{1,3},{2,0},{3,1},{4,6},{5,7},{6,4},{7,5},{8,10},{9,11},{10,... | collective-permute-start | bytes 3080 | tf_op jit(solution)/shard_map/ppermute | solution.py:337
  41.6 3.0 %collective-permute-done.2 = f32[2,128]{1,0:T(2,128)S(1)} collective-permute-done((f32[2,128]{1,0:T(2,128)S(1)}, f32[2,128]{1,0:T(2,128)S(1)}, u32[]{:S(2)}, u32[]{:S(2)}) %collective-permute-start.2) | collective-permute-done | bytes 1056 | tf_op jit(solution)/shard_map/ppermute | solution.py:337
  44.6 2.9 %collective-permute-start.3 = (f32[2,128]{1,0:T(2,128)S(1)}, f32[2,128]{1,0:T(2,128)S(1)}, u32[]{:S(2)}, u32[]{:S(2)}) collective-permute-start(f32[2,128]{1,0:T(2,128)S(1)} %add.31), channel_id=1, source_target_pairs={{0,1},{1,0},{2,3},{3,2},{4,5},{5,4},{6,7},{7,6},{8,9},{9,8},{10,11... | collective-permute-start | bytes 3080 | tf_op jit(solution)/shard_map/ppermute | solution.py:337
  47.5 2.5 %collective-permute-done.3 = f32[2,128]{1,0:T(2,128)S(1)} collective-permute-done((f32[2,128]{1,0:T(2,128)S(1)}, f32[2,128]{1,0:T(2,128)S(1)}, u32[]{:S(2)}, u32[]{:S(2)}) %collective-permute-start.3) | collective-permute-done | bytes 1056 | tf_op jit(solution)/shard_map/ppermute | solution.py:337
  50.1 3.1 %all-to-all-done.got_ref = bf16[32,384,128]{2,1,0:T(8,128)(2,1)S(1)} async-done(((bf16[32,384,128]{2,1,0:T(8,128)(2,1)}), bf16[32,384,128]{2,1,0:T(8,128)(2,1)S(1)}, u32[]{:S(2)}, u32[]{:S(2)}) %all-to-all-start) | async-done | bytes 3145760 | tf_op jit(solution)/shard_map/all_to_all | solution.py:377
  53.2 1.0 slice.9
  54.2 1.9 %collective-permute-start.4 = (bf16[32,128,128]{2,1,0:T(8,128)(2,1)}, bf16[32,128,128]{2,1,0:T(8,128)(2,1)}, u32[]{:S(2)}, u32[]{:S(2)}) collective-permute-start(bf16[32,128,128]{2,1,0:T(8,128)(2,1)} %slice.9), channel_id=1, source_target_pairs={{0,16},{16,0},{32,48},{48,32},{64,80},{80,64},{96,112},{112,96},{1... | collective-permute-start | bytes 3145736 | tf_op jit(solution)/shard_map/ppermute | solution.py:381
  56.2 0.1 copy.14.pat_ref
  56.3 2.9 %collective-permute-done.4.other_any = bf16[32,128,128]{2,1,0:T(8,128)(2,1)} collective-permute-done((bf16[32,128,128]{2,1,0:T(8,128)(2,1)}, bf16[32,128,128]{2,1,0:T(8,128)(2,1)}, u32[]{:S(2)}, u32[]{:S(2)}) %collective-permute-start.4) | collective-permute-done | bytes 1048608 | tf_op jit(solution)/shard_map/ppermute | solution.py:381
  59.1 23.7 %shard_map.111 = (bf16[32,256,128]{2,1,0:T(8,128)(2,1)}, bf16[32,128,128]{2,1,0:T(8,128)(2,1)}, bf16[32,128,128]{2,1,0:T(8,128)(2,1)}, f32[32,8,128]{2,1,0:T(8,128)}) custom-call(s32[1,32,6]{2,1,0:T(8,128)S(1)} %copy.14.pat_ref, f32[2,128]{1,0:T(2,128)S(1)} %add.32.gains_ref, bf16[32,384,128]{2,1,0:T(8,128)(2,1)S(1)} %all-to-all-done.got_ref, ...), custom_call_target="tpu_custom_call" | custom-call | tf_op jit(solution)/shard_map/pallas_call | solution.py:383
  82.8 2.0 %collective-permute-start.5 = (bf16[32,128,128]{2,1,0:T(8,128)(2,1)}, bf16[32,128,128]{2,1,0:T(8,128)(2,1)S(1)}, u32[]{:S(2)}, u32[]{:S(2)}) collective-permute-start(bf16[32,128,128]{2,1,0:T(8,128)(2,1)} %get-tuple-element.17), channel_id=1, source_target_pairs={{0,16},{16,0},{32,48},{48,32},{64,80},{80,64},{96,112},{112,96},{1... | collective-permute-start | bytes 3145736 | tf_op jit(solution)/shard_map/ppermute | solution.py:414
  84.9 5.9 %all-to-all-start.2 = ((f32[32,8,128]{2,1,0:T(8,128)}), f32[32,8,128]{2,1,0:T(8,128)S(1)}, u32[]{:S(2)}, u32[]{:S(2)}) async-start(f32[32,8,128]{2,1,0:T(8,128)} %get-tuple-element.22), calls=%async_computation.2 | async-start | bytes 262144 | tf_op jit(solution)/shard_map/all_to_all | solution.py:413
  90.9 2.1 %shard_map.112 = bf16[32,256,128]{2,1,0:T(8,128)(2,1)} custom-call(bf16[32,128,128]{2,1,0:T(8,128)(2,1)} %get-tuple-element.16.keep_any, bf16[32,128,128]{2,1,0:T(8,128)(2,1)S(1)} %collective-permute-done.5.got_ref, bf16[32,256,128]{2,1,0:T(8,128)(2,1)} %get-tuple-element.18.send_any), custom_call_target="tpu_custom_call", output_to_operand_aliasing={{}: (2, {})} | custom-call | tf_op jit(solution)/shard_map/pallas_call | solution.py:415
  93.0 4.6 %all-to-all-done.2.in_ref = f32[32,8,128]{2,1,0:T(8,128)S(1)} async-done(((f32[32,8,128]{2,1,0:T(8,128)}), f32[32,8,128]{2,1,0:T(8,128)S(1)}, u32[]{:S(2)}, u32[]{:S(2)}) %all-to-all-start.2) | async-done | bytes 131104 | tf_op jit(solution)/shard_map/all_to_all | solution.py:413
  97.5 5.1 %all-to-all-start.1 = ((bf16[32,256,128]{2,1,0:T(8,128)(2,1)}), bf16[32,256,128]{2,1,0:T(8,128)(2,1)S(1)}, u32[]{:S(2)}, u32[]{:S(2)}) async-start(bf16[32,256,128]{2,1,0:T(8,128)(2,1)} %shard_map.112), calls=%async_computation.1 | async-start | bytes 4194304 | tf_op jit(solution)/shard_map/all_to_all | solution.py:422
  102.7 1.9 %collective-permute-start.6 = (f32[2,128]{1,0:T(2,128)S(1)}, f32[2,128]{1,0:T(2,128)S(1)}, u32[]{:S(2)}, u32[]{:S(2)}) collective-permute-start(f32[2,128]{1,0:T(2,128)S(1)} %shard_map.114), channel_id=1, source_target_pairs={{0,1},{1,0},{2,3},{3,2},{4,5},{5,4},{6,7},{7,6},{8,9},{9,8},{10,11... | collective-permute-start | bytes 3080 | tf_op jit(solution)/shard_map/ppermute | solution.py:337
  104.6 3.5 %collective-permute-done.6 = f32[2,128]{1,0:T(2,128)S(1)} collective-permute-done((f32[2,128]{1,0:T(2,128)S(1)}, f32[2,128]{1,0:T(2,128)S(1)}, u32[]{:S(2)}, u32[]{:S(2)}) %collective-permute-start.6) | collective-permute-done | bytes 1056 | tf_op jit(solution)/shard_map/ppermute | solution.py:337
  108.1 13.6 %collective-permute-start.7 = (f32[2,128]{1,0:T(2,128)S(1)}, f32[2,128]{1,0:T(2,128)S(1)}, u32[]{:S(2)}, u32[]{:S(2)}) collective-permute-start(f32[2,128]{1,0:T(2,128)S(1)} %add.33), channel_id=1, source_target_pairs={{0,8},{1,9},{2,10},{3,11},{4,12},{5,13},{6,14},{7,15},{8,0},{9,1},... | collective-permute-start | bytes 3080 | tf_op jit(solution)/shard_map/ppermute | solution.py:337
  121.8 1.5 %collective-permute-done.7 = f32[2,128]{1,0:T(2,128)S(1)} collective-permute-done((f32[2,128]{1,0:T(2,128)S(1)}, f32[2,128]{1,0:T(2,128)S(1)}, u32[]{:S(2)}, u32[]{:S(2)}) %collective-permute-start.7) | collective-permute-done | bytes 1056 | tf_op jit(solution)/shard_map/ppermute | solution.py:337
  123.3 6.0 %collective-permute-start.8 = (f32[2,128]{1,0:T(2,128)S(1)}, f32[2,128]{1,0:T(2,128)S(1)}, u32[]{:S(2)}, u32[]{:S(2)}) collective-permute-start(f32[2,128]{1,0:T(2,128)S(1)} %add.34), channel_id=1, source_target_pairs={{0,4},{1,5},{2,6},{3,7},{4,0},{5,1},{6,2},{7,3},{8,12},{9,13},{10,... | collective-permute-start | bytes 3080 | tf_op jit(solution)/shard_map/ppermute | solution.py:337
  129.3 3.4 %collective-permute-done.8 = f32[2,128]{1,0:T(2,128)S(1)} collective-permute-done((f32[2,128]{1,0:T(2,128)S(1)}, f32[2,128]{1,0:T(2,128)S(1)}, u32[]{:S(2)}, u32[]{:S(2)}) %collective-permute-start.8) | collective-permute-done | bytes 1056 | tf_op jit(solution)/shard_map/ppermute | solution.py:337
  132.7 3.4 %collective-permute-start.9 = (f32[2,128]{1,0:T(2,128)S(1)}, f32[2,128]{1,0:T(2,128)S(1)}, u32[]{:S(2)}, u32[]{:S(2)}) collective-permute-start(f32[2,128]{1,0:T(2,128)S(1)} %add.35), channel_id=1, source_target_pairs={{0,2},{1,3},{2,0},{3,1},{4,6},{5,7},{6,4},{7,5},{8,10},{9,11},{10,... | collective-permute-start | bytes 3080 | tf_op jit(solution)/shard_map/ppermute | solution.py:337
  136.1 3.0 %collective-permute-done.9 = f32[2,128]{1,0:T(2,128)S(1)} collective-permute-done((f32[2,128]{1,0:T(2,128)S(1)}, f32[2,128]{1,0:T(2,128)S(1)}, u32[]{:S(2)}, u32[]{:S(2)}) %collective-permute-start.9) | collective-permute-done | bytes 1056 | tf_op jit(solution)/shard_map/ppermute | solution.py:337
  139.1 0.5 slice_bitcast_fusion
  139.6 2.2 %shard_map.113 = (bf16[1,128,4096]{2,1,0:T(8,128)(2,1)}, bf16[1,128,1024]{2,1,0:T(8,128)(2,1)}, bf16[1,128,1024]{2,1,0:T(8,128)(2,1)}) custom-call(bf16[32,256,128]{2,1,0:T(8,128)(2,1)S(1)} %all-to-all-done.1.in_ref, bf16[1,128,1024]{2,1,0:T(8,128)(2,1)S(1)} %copy-done, f32[2,128]{1,0:T(2,128)S(1)} %add.32.gains_ref), custom_call_target="tpu_custom_call" | custom-call | tf_op jit(solution)/shard_map/pallas_call | solution.py:432
  (26 shorter events, 0.3 us)
Async XLA Ops:
  3.6 9.7 %copy-start.2 = (f32[8]{0:T(128)S(1)}, f32[8]{0:T(128)}, u32[]{:S(2)}) copy-start(f32[8]{0:T(128)} %param.10) | copy-start | bytes 100
  3.6 9.8 %copy-start.3 = (f32[8]{0:T(128)S(1)}, f32[8]{0:T(128)}, u32[]{:S(2)}) copy-start(f32[8]{0:T(128)} %param.11) | copy-start | bytes 100
  3.6 49.6 %all-to-all-start = ((bf16[32,384,128]{2,1,0:T(8,128)(2,1)}), bf16[32,384,128]{2,1,0:T(8,128)(2,1)S(1)}, u32[]{:S(2)}, u32[]{:S(2)}) async-start(bf16[32,384,128]{2,1,0:T(8,128)(2,1)} %shard_map.110), calls=%async_computation | async-start | bytes 6291456 | tf_op jit(solution)/shard_map/all_to_all | solution.py:377
  13.3 42.9 %copy-start.1 = (s32[1,32,6]{1,0,2:T(1,128)S(1)}, s32[1,32,6]{1,0,2:T(1,128)}, u32[]{:S(2)}) copy-start(s32[1,32,6]{1,0,2:T(1,128)} %param.12) | copy-start | bytes 2308
  13.5 15.3 %collective-permute-start = (f32[2,128]{1,0:T(2,128)S(1)}, f32[2,128]{1,0:T(2,128)S(1)}, u32[]{:S(2)}, u32[]{:S(2)}) collective-permute-start(f32[2,128]{1,0:T(2,128)S(1)} %compare_select_fusion), channel_id=1, source_target_pairs={{0,8},{1,9},{2,10},{3,11},{4,12},{5,13},{6,14},{7,15},{8,0},{9,1},... | collective-permute-start | bytes 3080 | tf_op jit(solution)/shard_map/ppermute | solution.py:337
  28.8 9.4 %collective-permute-start.1 = (f32[2,128]{1,0:T(2,128)S(1)}, f32[2,128]{1,0:T(2,128)S(1)}, u32[]{:S(2)}, u32[]{:S(2)}) collective-permute-start(f32[2,128]{1,0:T(2,128)S(1)} %fusion), channel_id=1, source_target_pairs={{0,4},{1,5},{2,6},{3,7},{4,0},{5,1},{6,2},{7,3},{8,12},{9,13},{10,... | collective-permute-start | bytes 3080 | tf_op jit(solution)/shard_map/ppermute | solution.py:337
  38.2 6.4 %collective-permute-start.2 = (f32[2,128]{1,0:T(2,128)S(1)}, f32[2,128]{1,0:T(2,128)S(1)}, u32[]{:S(2)}, u32[]{:S(2)}) collective-permute-start(f32[2,128]{1,0:T(2,128)S(1)} %fusion.1), channel_id=1, source_target_pairs={{0,2},{1,3},{2,0},{3,1},{4,6},{5,7},{6,4},{7,5},{8,10},{9,11},{10,... | collective-permute-start | bytes 3080 | tf_op jit(solution)/shard_map/ppermute | solution.py:337
  44.6 5.5 %collective-permute-start.3 = (f32[2,128]{1,0:T(2,128)S(1)}, f32[2,128]{1,0:T(2,128)S(1)}, u32[]{:S(2)}, u32[]{:S(2)}) collective-permute-start(f32[2,128]{1,0:T(2,128)S(1)} %add.31), channel_id=1, source_target_pairs={{0,1},{1,0},{2,3},{3,2},{4,5},{5,4},{6,7},{7,6},{8,9},{9,8},{10,11... | collective-permute-start | bytes 3080 | tf_op jit(solution)/shard_map/ppermute | solution.py:337
  54.2 4.9 %collective-permute-start.4 = (bf16[32,128,128]{2,1,0:T(8,128)(2,1)}, bf16[32,128,128]{2,1,0:T(8,128)(2,1)}, u32[]{:S(2)}, u32[]{:S(2)}) collective-permute-start(bf16[32,128,128]{2,1,0:T(8,128)(2,1)} %slice.9), channel_id=1, source_target_pairs={{0,16},{16,0},{32,48},{48,32},{64,80},{80,64},{96,112},{112,96},{1... | collective-permute-start | bytes 3145736 | tf_op jit(solution)/shard_map/ppermute | solution.py:381
  82.8 8.0 %collective-permute-start.5 = (bf16[32,128,128]{2,1,0:T(8,128)(2,1)}, bf16[32,128,128]{2,1,0:T(8,128)(2,1)S(1)}, u32[]{:S(2)}, u32[]{:S(2)}) collective-permute-start(bf16[32,128,128]{2,1,0:T(8,128)(2,1)} %get-tuple-element.17), channel_id=1, source_target_pairs={{0,16},{16,0},{32,48},{48,32},{64,80},{80,64},{96,112},{112,96},{1... | collective-permute-start | bytes 3145736 | tf_op jit(solution)/shard_map/ppermute | solution.py:414
  84.9 12.7 %all-to-all-start.2 = ((f32[32,8,128]{2,1,0:T(8,128)}), f32[32,8,128]{2,1,0:T(8,128)S(1)}, u32[]{:S(2)}, u32[]{:S(2)}) async-start(f32[32,8,128]{2,1,0:T(8,128)} %get-tuple-element.22), calls=%async_computation.2 | async-start | bytes 262144 | tf_op jit(solution)/shard_map/all_to_all | solution.py:413
  92.9 46.7 %copy-start = (bf16[1,128,1024]{2,1,0:T(8,128)(2,1)S(1)}, bf16[1,128,1024]{2,1,0:T(8,128)(2,1)}, u32[]{:S(2)}) copy-start(bf16[1,128,1024]{2,1,0:T(8,128)(2,1)} %k_ref.1) | copy-start | bytes 786436
  97.5 42.1 %all-to-all-start.1 = ((bf16[32,256,128]{2,1,0:T(8,128)(2,1)}), bf16[32,256,128]{2,1,0:T(8,128)(2,1)S(1)}, u32[]{:S(2)}, u32[]{:S(2)}) async-start(bf16[32,256,128]{2,1,0:T(8,128)(2,1)} %shard_map.112), calls=%async_computation.1 | async-start | bytes 4194304 | tf_op jit(solution)/shard_map/all_to_all | solution.py:422
  102.7 5.5 %collective-permute-start.6 = (f32[2,128]{1,0:T(2,128)S(1)}, f32[2,128]{1,0:T(2,128)S(1)}, u32[]{:S(2)}, u32[]{:S(2)}) collective-permute-start(f32[2,128]{1,0:T(2,128)S(1)} %shard_map.114), channel_id=1, source_target_pairs={{0,1},{1,0},{2,3},{3,2},{4,5},{5,4},{6,7},{7,6},{8,9},{9,8},{10,11... | collective-permute-start | bytes 3080 | tf_op jit(solution)/shard_map/ppermute | solution.py:337
  108.1 15.2 %collective-permute-start.7 = (f32[2,128]{1,0:T(2,128)S(1)}, f32[2,128]{1,0:T(2,128)S(1)}, u32[]{:S(2)}, u32[]{:S(2)}) collective-permute-start(f32[2,128]{1,0:T(2,128)S(1)} %add.33), channel_id=1, source_target_pairs={{0,8},{1,9},{2,10},{3,11},{4,12},{5,13},{6,14},{7,15},{8,0},{9,1},... | collective-permute-start | bytes 3080 | tf_op jit(solution)/shard_map/ppermute | solution.py:337
  123.3 9.4 %collective-permute-start.8 = (f32[2,128]{1,0:T(2,128)S(1)}, f32[2,128]{1,0:T(2,128)S(1)}, u32[]{:S(2)}, u32[]{:S(2)}) collective-permute-start(f32[2,128]{1,0:T(2,128)S(1)} %add.34), channel_id=1, source_target_pairs={{0,4},{1,5},{2,6},{3,7},{4,0},{5,1},{6,2},{7,3},{8,12},{9,13},{10,... | collective-permute-start | bytes 3080 | tf_op jit(solution)/shard_map/ppermute | solution.py:337
  132.7 6.4 %collective-permute-start.9 = (f32[2,128]{1,0:T(2,128)S(1)}, f32[2,128]{1,0:T(2,128)S(1)}, u32[]{:S(2)}, u32[]{:S(2)}) collective-permute-start(f32[2,128]{1,0:T(2,128)S(1)} %add.35), channel_id=1, source_target_pairs={{0,2},{1,3},{2,0},{3,1},{4,6},{5,7},{6,4},{7,5},{8,10},{9,11},{10,... | collective-permute-start | bytes 3080 | tf_op jit(solution)/shard_map/ppermute | solution.py:337

commit v6 on v5

--- a/solution.py
+++ b/solution.py
@@ -79,7 +79,8 @@
 SCALE = 1.0 / math.sqrt(HD)
 SCALE2 = SCALE * math.log2(math.e)
 CHUNK = 16
-GROUPS = [list(range(s, s + 2)) for s in range(0, SLOTS, 2)]
+GROUPS = [list(range(s, s + 3)) for s in range(0, SLOTS, 3)]
+KEY_GROUPS = [list(range(s, s + 2)) for s in range(0, SLOTS, 2)]
 
 
 def attend_kernel(
@@ -113,7 +114,7 @@
     other_copy.start()
     lax.fori_loop(0, blocks, normalise_queries, 0, unroll=8)
     other_copy.wait()
-    lax.fori_loop(0, blocks, normalise_keys, 0, unroll=4)
+    lax.fori_loop(0, blocks, normalise_keys, 0, unroll=8)
 
     def pair_of(b):
         d_low = got_ref[b, BLK : 2 * BLK, :]
@@ -222,7 +223,7 @@
         delta = jnp.sum(sums[1], axis=0, keepdims=True) * inv_total
         pair = pair_of(b)
         index = named_blocks(pat_ref, b)[1]
-        for slots in GROUPS:
+        for slots in KEY_GROUPS:
             terms = grads_slots(side, slots, pair, inv_total, inv_total * SCALE, delta)
             for n, s in enumerate(slots):
                 acc_ref[index[s]] += terms[n * BLK : (n + 1) * BLK]
@@ -257,7 +258,7 @@
     step_blocks = blocks // OUTS
     out_copies = []
     for n in range(OUTS):
-        k_part = lax.fori_loop(n * step_blocks, (n + 1) * step_blocks, finish, k_part, unroll=2)
+        k_part = lax.fori_loop(n * step_blocks, (n + 1) * step_blocks, finish, k_part, unroll=4)
         chunk = pl.ds(n * step_blocks, step_blocks)
         for ref, out, copy_sems in ((give_ref, give_any, give_sems), (keep_ref, keep_any, keep_sems)):
             out_copies.append(pltpu.make_async_copy(ref.at[chunk], out.at[chunk], copy_sems.at[n]))

time: 143 us -> 142 us (level)
  no operation moved by 1% of the time
where the time goes in v6:
time: 142 us
  starting transfers between devices  75.5 us (53%)
  waiting for transfers between devices  32.5 us (23%)
  Pallas kernels  30.8 us (22%)
  local copies, waits for them, and re-layouts  1.92 us (1%)
    ppermute x8, starting transfers between devices, dp_step(): lax.ppermute(values, 'dp', [(z, z ^ step) for z in range(dp_count)])  50.9 us
    pallas_call x1, Pallas kernels, shards(): call(functools.partial(attend_kernel, blocks), [SMEM_SPEC] + [VMEM_SPEC]...  23.5 us
    ppermute x8, waiting for transfers between devices, dp_step(): lax.ppermute(values, 'dp', [(z, z ^ step) for z in range(dp_count)])  21.8 us
    all_to_all x1, starting transfers between devices, shards(): arrived = lax.all_to_all(sent, 'seq', 0, 0, tiled=True)  9.62 us
    all_to_all x1, starting transfers between devices, shards(): parts = lax.all_to_all(parts, 'seq', 0, 0, tiled=True)  5.95 us
    all_to_all x1, starting transfers between devices, shards(): back = lax.all_to_all(send, 'seq', 0, 0, tiled=True)  5.08 us
    all_to_all x1, waiting for transfers between devices, shards(): parts = lax.all_to_all(parts, 'seq', 0, 0, tiled=True)  4.59 us
    all_to_all x1, waiting for transfers between devices, shards(): arrived = lax.all_to_all(sent, 'seq', 0, 0, tiled=True)  3.15 us
  transfers between devices with their start and end apart: 13, of which 11 were waited for; matrix products, arithmetic and copies ran while one was open for 1% of the time, Pallas kernels for 1%

profile of v6, /device:TPU:2, one launch (start us, length us, event | category | flops | bytes accessed | tf_op | source)
XLA Modules:
  0.0 141.7 jit_solution(1537751538888595104)
XLA Ops:
  0.6 3.0 %shard_map.110 = bf16[32,384,128]{2,1,0:T(8,128)(2,1)} custom-call(bf16[1,128,4096]{2,1,0:T(8,128)(2,1)} %q_any.1, bf16[1,128,4096]{2,1,0:T(8,128)(2,1)} %d_any.1, bf16[1,128,1024]{2,1,0:T(8,128)(2,1)} %k_ref.1, bf16[1,128,1024]{2,1,0:T(8,128)(2,1)} %v_any.1), custom_call_target="tpu_custom_call" | custom-call | tf_op jit(solution)/shard_map/pallas_call | solution.py:364
  3.6 9.6 %all-to-all-start = ((bf16[32,384,128]{2,1,0:T(8,128)(2,1)}), bf16[32,384,128]{2,1,0:T(8,128)(2,1)S(1)}, u32[]{:S(2)}, u32[]{:S(2)}) async-start(bf16[32,384,128]{2,1,0:T(8,128)(2,1)} %shard_map.110), calls=%async_computation | async-start | bytes 6291456 | tf_op jit(solution)/shard_map/all_to_all | solution.py:378
  13.4 0.1 broadcast_in_dim_tile.7
  13.5 13.7 %collective-permute-start = (f32[2,128]{1,0:T(2,128)S(1)}, f32[2,128]{1,0:T(2,128)S(1)}, u32[]{:S(2)}, u32[]{:S(2)}) collective-permute-start(f32[2,128]{1,0:T(2,128)S(1)} %compare_select_fusion), channel_id=1, source_target_pairs={{0,8},{1,9},{2,10},{3,11},{4,12},{5,13},{6,14},{7,15},{8,0},{9,1},... | collective-permute-start | bytes 3080 | tf_op jit(solution)/shard_map/ppermute | solution.py:338
  27.3 1.5 %collective-permute-done = f32[2,128]{1,0:T(2,128)S(1)} collective-permute-done((f32[2,128]{1,0:T(2,128)S(1)}, f32[2,128]{1,0:T(2,128)S(1)}, u32[]{:S(2)}, u32[]{:S(2)}) %collective-permute-start) | collective-permute-done | bytes 1056 | tf_op jit(solution)/shard_map/ppermute | solution.py:338
  28.8 6.0 %collective-permute-start.1 = (f32[2,128]{1,0:T(2,128)S(1)}, f32[2,128]{1,0:T(2,128)S(1)}, u32[]{:S(2)}, u32[]{:S(2)}) collective-permute-start(f32[2,128]{1,0:T(2,128)S(1)} %fusion), channel_id=1, source_target_pairs={{0,4},{1,5},{2,6},{3,7},{4,0},{5,1},{6,2},{7,3},{8,12},{9,13},{10,... | collective-permute-start | bytes 3080 | tf_op jit(solution)/shard_map/ppermute | solution.py:338
  34.9 3.4 %collective-permute-done.1 = f32[2,128]{1,0:T(2,128)S(1)} collective-permute-done((f32[2,128]{1,0:T(2,128)S(1)}, f32[2,128]{1,0:T(2,128)S(1)}, u32[]{:S(2)}, u32[]{:S(2)}) %collective-permute-start.1) | collective-permute-done | bytes 1056 | tf_op jit(solution)/shard_map/ppermute | solution.py:338
  38.2 3.4 %collective-permute-start.2 = (f32[2,128]{1,0:T(2,128)S(1)}, f32[2,128]{1,0:T(2,128)S(1)}, u32[]{:S(2)}, u32[]{:S(2)}) collective-permute-start(f32[2,128]{1,0:T(2,128)S(1)} %fusion.1), channel_id=1, source_target_pairs={{0,2},{1,3},{2,0},{3,1},{4,6},{5,7},{6,4},{7,5},{8,10},{9,11},{10,... | collective-permute-start | bytes 3080 | tf_op jit(solution)/shard_map/ppermute | solution.py:338
  41.6 3.0 %collective-permute-done.2 = f32[2,128]{1,0:T(2,128)S(1)} collective-permute-done((f32[2,128]{1,0:T(2,128)S(1)}, f32[2,128]{1,0:T(2,128)S(1)}, u32[]{:S(2)}, u32[]{:S(2)}) %collective-permute-start.2) | collective-permute-done | bytes 1056 | tf_op jit(solution)/shard_map/ppermute | solution.py:338
  44.6 2.9 %collective-permute-start.3 = (f32[2,128]{1,0:T(2,128)S(1)}, f32[2,128]{1,0:T(2,128)S(1)}, u32[]{:S(2)}, u32[]{:S(2)}) collective-permute-start(f32[2,128]{1,0:T(2,128)S(1)} %add.31), channel_id=1, source_target_pairs={{0,1},{1,0},{2,3},{3,2},{4,5},{5,4},{6,7},{7,6},{8,9},{9,8},{10,11... | collective-permute-start | bytes 3080 | tf_op jit(solution)/shard_map/ppermute | solution.py:338
  47.5 2.5 %collective-permute-done.3 = f32[2,128]{1,0:T(2,128)S(1)} collective-permute-done((f32[2,128]{1,0:T(2,128)S(1)}, f32[2,128]{1,0:T(2,128)S(1)}, u32[]{:S(2)}, u32[]{:S(2)}) %collective-permute-start.3) | collective-permute-done | bytes 1056 | tf_op jit(solution)/shard_map/ppermute | solution.py:338
  50.1 3.1 %all-to-all-done.got_ref = bf16[32,384,128]{2,1,0:T(8,128)(2,1)S(1)} async-done(((bf16[32,384,128]{2,1,0:T(8,128)(2,1)}), bf16[32,384,128]{2,1,0:T(8,128)(2,1)S(1)}, u32[]{:S(2)}, u32[]{:S(2)}) %all-to-all-start) | async-done | bytes 3145760 | tf_op jit(solution)/shard_map/all_to_all | solution.py:378
  53.2 1.0 slice.9
  54.2 1.9 %collective-permute-start.4 = (bf16[32,128,128]{2,1,0:T(8,128)(2,1)}, bf16[32,128,128]{2,1,0:T(8,128)(2,1)}, u32[]{:S(2)}, u32[]{:S(2)}) collective-permute-start(bf16[32,128,128]{2,1,0:T(8,128)(2,1)} %slice.9), channel_id=1, source_target_pairs={{0,16},{16,0},{32,48},{48,32},{64,80},{80,64},{96,112},{112,96},{1... | collective-permute-start | bytes 3145736 | tf_op jit(solution)/shard_map/ppermute | solution.py:382
  56.2 0.1 copy.14.pat_ref
  56.3 2.9 %collective-permute-done.4.other_any = bf16[32,128,128]{2,1,0:T(8,128)(2,1)} collective-permute-done((bf16[32,128,128]{2,1,0:T(8,128)(2,1)}, bf16[32,128,128]{2,1,0:T(8,128)(2,1)}, u32[]{:S(2)}, u32[]{:S(2)}) %collective-permute-start.4) | collective-permute-done | bytes 1048608 | tf_op jit(solution)/shard_map/ppermute | solution.py:382
  59.1 23.5 %shard_map.111 = (bf16[32,256,128]{2,1,0:T(8,128)(2,1)}, bf16[32,128,128]{2,1,0:T(8,128)(2,1)}, bf16[32,128,128]{2,1,0:T(8,128)(2,1)}, f32[32,8,128]{2,1,0:T(8,128)}) custom-call(s32[1,32,6]{2,1,0:T(8,128)S(1)} %copy.14.pat_ref, f32[2,128]{1,0:T(2,128)S(1)} %add.32.gains_ref, bf16[32,384,128]{2,1,0:T(8,128)(2,1)S(1)} %all-to-all-done.got_ref, ...), custom_call_target="tpu_custom_call" | custom-call | tf_op jit(solution)/shard_map/pallas_call | solution.py:384
  82.6 2.0 %collective-permute-start.5 = (bf16[32,128,128]{2,1,0:T(8,128)(2,1)}, bf16[32,128,128]{2,1,0:T(8,128)(2,1)S(1)}, u32[]{:S(2)}, u32[]{:S(2)}) collective-permute-start(bf16[32,128,128]{2,1,0:T(8,128)(2,1)} %get-tuple-element.17), channel_id=1, source_target_pairs={{0,16},{16,0},{32,48},{48,32},{64,80},{80,64},{96,112},{112,96},{1... | collective-permute-start | bytes 3145736 | tf_op jit(solution)/shard_map/ppermute | solution.py:415
  84.7 5.9 %all-to-all-start.2 = ((f32[32,8,128]{2,1,0:T(8,128)}), f32[32,8,128]{2,1,0:T(8,128)S(1)}, u32[]{:S(2)}, u32[]{:S(2)}) async-start(f32[32,8,128]{2,1,0:T(8,128)} %get-tuple-element.22), calls=%async_computation.2 | async-start | bytes 262144 | tf_op jit(solution)/shard_map/all_to_all | solution.py:414
  90.6 2.1 %shard_map.112 = bf16[32,256,128]{2,1,0:T(8,128)(2,1)} custom-call(bf16[32,128,128]{2,1,0:T(8,128)(2,1)} %get-tuple-element.16.keep_any, bf16[32,128,128]{2,1,0:T(8,128)(2,1)S(1)} %collective-permute-done.5.got_ref, bf16[32,256,128]{2,1,0:T(8,128)(2,1)} %get-tuple-element.18.send_any), custom_call_target="tpu_custom_call", output_to_operand_aliasing={{}: (2, {})} | custom-call | tf_op jit(solution)/shard_map/pallas_call | solution.py:416
  92.7 4.6 %all-to-all-done.2.in_ref = f32[32,8,128]{2,1,0:T(8,128)S(1)} async-done(((f32[32,8,128]{2,1,0:T(8,128)}), f32[32,8,128]{2,1,0:T(8,128)S(1)}, u32[]{:S(2)}, u32[]{:S(2)}) %all-to-all-start.2) | async-done | bytes 131104 | tf_op jit(solution)/shard_map/all_to_all | solution.py:414
  97.3 5.1 %all-to-all-start.1 = ((bf16[32,256,128]{2,1,0:T(8,128)(2,1)}), bf16[32,256,128]{2,1,0:T(8,128)(2,1)S(1)}, u32[]{:S(2)}, u32[]{:S(2)}) async-start(bf16[32,256,128]{2,1,0:T(8,128)(2,1)} %shard_map.112), calls=%async_computation.1 | async-start | bytes 4194304 | tf_op jit(solution)/shard_map/all_to_all | solution.py:423
  102.5 1.9 %collective-permute-start.6 = (f32[2,128]{1,0:T(2,128)S(1)}, f32[2,128]{1,0:T(2,128)S(1)}, u32[]{:S(2)}, u32[]{:S(2)}) collective-permute-start(f32[2,128]{1,0:T(2,128)S(1)} %shard_map.114), channel_id=1, source_target_pairs={{0,1},{1,0},{2,3},{3,2},{4,5},{5,4},{6,7},{7,6},{8,9},{9,8},{10,11... | collective-permute-start | bytes 3080 | tf_op jit(solution)/shard_map/ppermute | solution.py:338
  104.4 3.5 %collective-permute-done.6 = f32[2,128]{1,0:T(2,128)S(1)} collective-permute-done((f32[2,128]{1,0:T(2,128)S(1)}, f32[2,128]{1,0:T(2,128)S(1)}, u32[]{:S(2)}, u32[]{:S(2)}) %collective-permute-start.6) | collective-permute-done | bytes 1056 | tf_op jit(solution)/shard_map/ppermute | solution.py:338
  107.9 13.6 %collective-permute-start.7 = (f32[2,128]{1,0:T(2,128)S(1)}, f32[2,128]{1,0:T(2,128)S(1)}, u32[]{:S(2)}, u32[]{:S(2)}) collective-permute-start(f32[2,128]{1,0:T(2,128)S(1)} %add.33), channel_id=1, source_target_pairs={{0,8},{1,9},{2,10},{3,11},{4,12},{5,13},{6,14},{7,15},{8,0},{9,1},... | collective-permute-start | bytes 3080 | tf_op jit(solution)/shard_map/ppermute | solution.py:338
  121.6 1.5 %collective-permute-done.7 = f32[2,128]{1,0:T(2,128)S(1)} collective-permute-done((f32[2,128]{1,0:T(2,128)S(1)}, f32[2,128]{1,0:T(2,128)S(1)}, u32[]{:S(2)}, u32[]{:S(2)}) %collective-permute-start.7) | collective-permute-done | bytes 1056 | tf_op jit(solution)/shard_map/ppermute | solution.py:338
  123.1 6.0 %collective-permute-start.8 = (f32[2,128]{1,0:T(2,128)S(1)}, f32[2,128]{1,0:T(2,128)S(1)}, u32[]{:S(2)}, u32[]{:S(2)}) collective-permute-start(f32[2,128]{1,0:T(2,128)S(1)} %add.34), channel_id=1, source_target_pairs={{0,4},{1,5},{2,6},{3,7},{4,0},{5,1},{6,2},{7,3},{8,12},{9,13},{10,... | collective-permute-start | bytes 3080 | tf_op jit(solution)/shard_map/ppermute | solution.py:338
  129.1 3.4 %collective-permute-done.8 = f32[2,128]{1,0:T(2,128)S(1)} collective-permute-done((f32[2,128]{1,0:T(2,128)S(1)}, f32[2,128]{1,0:T(2,128)S(1)}, u32[]{:S(2)}, u32[]{:S(2)}) %collective-permute-start.8) | collective-permute-done | bytes 1056 | tf_op jit(solution)/shard_map/ppermute | solution.py:338
  132.5 3.3 %collective-permute-start.9 = (f32[2,128]{1,0:T(2,128)S(1)}, f32[2,128]{1,0:T(2,128)S(1)}, u32[]{:S(2)}, u32[]{:S(2)}) collective-permute-start(f32[2,128]{1,0:T(2,128)S(1)} %add.35), channel_id=1, source_target_pairs={{0,2},{1,3},{2,0},{3,1},{4,6},{5,7},{6,4},{7,5},{8,10},{9,11},{10,... | collective-permute-start | bytes 3080 | tf_op jit(solution)/shard_map/ppermute | solution.py:338
  135.8 3.0 %collective-permute-done.9 = f32[2,128]{1,0:T(2,128)S(1)} collective-permute-done((f32[2,128]{1,0:T(2,128)S(1)}, f32[2,128]{1,0:T(2,128)S(1)}, u32[]{:S(2)}, u32[]{:S(2)}) %collective-permute-start.9) | collective-permute-done | bytes 1056 | tf_op jit(solution)/shard_map/ppermute | solution.py:338
  138.9 0.5 slice_bitcast_fusion
  139.4 2.2 %shard_map.113 = (bf16[1,128,4096]{2,1,0:T(8,128)(2,1)}, bf16[1,128,1024]{2,1,0:T(8,128)(2,1)}, bf16[1,128,1024]{2,1,0:T(8,128)(2,1)}) custom-call(bf16[32,256,128]{2,1,0:T(8,128)(2,1)S(1)} %all-to-all-done.1.in_ref, bf16[1,128,1024]{2,1,0:T(8,128)(2,1)S(1)} %copy-done, f32[2,128]{1,0:T(2,128)S(1)} %add.32.gains_ref), custom_call_target="tpu_custom_call" | custom-call | tf_op jit(solution)/shard_map/pallas_call | solution.py:433
  (26 shorter events, 0.3 us)
Async XLA Ops:
  3.6 9.7 %copy-start.2 = (f32[8]{0:T(128)S(1)}, f32[8]{0:T(128)}, u32[]{:S(2)}) copy-start(f32[8]{0:T(128)} %param.10) | copy-start | bytes 100
  3.6 9.8 %copy-start.3 = (f32[8]{0:T(128)S(1)}, f32[8]{0:T(128)}, u32[]{:S(2)}) copy-start(f32[8]{0:T(128)} %param.11) | copy-start | bytes 100
  3.6 49.6 %all-to-all-start = ((bf16[32,384,128]{2,1,0:T(8,128)(2,1)}), bf16[32,384,128]{2,1,0:T(8,128)(2,1)S(1)}, u32[]{:S(2)}, u32[]{:S(2)}) async-start(bf16[32,384,128]{2,1,0:T(8,128)(2,1)} %shard_map.110), calls=%async_computation | async-start | bytes 6291456 | tf_op jit(solution)/shard_map/all_to_all | solution.py:378
  13.3 42.9 %copy-start.1 = (s32[1,32,6]{1,0,2:T(1,128)S(1)}, s32[1,32,6]{1,0,2:T(1,128)}, u32[]{:S(2)}) copy-start(s32[1,32,6]{1,0,2:T(1,128)} %param.12) | copy-start | bytes 2308
  13.5 15.3 %collective-permute-start = (f32[2,128]{1,0:T(2,128)S(1)}, f32[2,128]{1,0:T(2,128)S(1)}, u32[]{:S(2)}, u32[]{:S(2)}) collective-permute-start(f32[2,128]{1,0:T(2,128)S(1)} %compare_select_fusion), channel_id=1, source_target_pairs={{0,8},{1,9},{2,10},{3,11},{4,12},{5,13},{6,14},{7,15},{8,0},{9,1},... | collective-permute-start | bytes 3080 | tf_op jit(solution)/shard_map/ppermute | solution.py:338
  28.8 9.4 %collective-permute-start.1 = (f32[2,128]{1,0:T(2,128)S(1)}, f32[2,128]{1,0:T(2,128)S(1)}, u32[]{:S(2)}, u32[]{:S(2)}) collective-permute-start(f32[2,128]{1,0:T(2,128)S(1)} %fusion), channel_id=1, source_target_pairs={{0,4},{1,5},{2,6},{3,7},{4,0},{5,1},{6,2},{7,3},{8,12},{9,13},{10,... | collective-permute-start | bytes 3080 | tf_op jit(solution)/shard_map/ppermute | solution.py:338
  38.2 6.4 %collective-permute-start.2 = (f32[2,128]{1,0:T(2,128)S(1)}, f32[2,128]{1,0:T(2,128)S(1)}, u32[]{:S(2)}, u32[]{:S(2)}) collective-permute-start(f32[2,128]{1,0:T(2,128)S(1)} %fusion.1), channel_id=1, source_target_pairs={{0,2},{1,3},{2,0},{3,1},{4,6},{5,7},{6,4},{7,5},{8,10},{9,11},{10,... | collective-permute-start | bytes 3080 | tf_op jit(solution)/shard_map/ppermute | solution.py:338
  44.6 5.5 %collective-permute-start.3 = (f32[2,128]{1,0:T(2,128)S(1)}, f32[2,128]{1,0:T(2,128)S(1)}, u32[]{:S(2)}, u32[]{:S(2)}) collective-permute-start(f32[2,128]{1,0:T(2,128)S(1)} %add.31), channel_id=1, source_target_pairs={{0,1},{1,0},{2,3},{3,2},{4,5},{5,4},{6,7},{7,6},{8,9},{9,8},{10,11... | collective-permute-start | bytes 3080 | tf_op jit(solution)/shard_map/ppermute | solution.py:338
  54.2 4.9 %collective-permute-start.4 = (bf16[32,128,128]{2,1,0:T(8,128)(2,1)}, bf16[32,128,128]{2,1,0:T(8,128)(2,1)}, u32[]{:S(2)}, u32[]{:S(2)}) collective-permute-start(bf16[32,128,128]{2,1,0:T(8,128)(2,1)} %slice.9), channel_id=1, source_target_pairs={{0,16},{16,0},{32,48},{48,32},{64,80},{80,64},{96,112},{112,96},{1... | collective-permute-start | bytes 3145736 | tf_op jit(solution)/shard_map/ppermute | solution.py:382
  82.6 8.0 %collective-permute-start.5 = (bf16[32,128,128]{2,1,0:T(8,128)(2,1)}, bf16[32,128,128]{2,1,0:T(8,128)(2,1)S(1)}, u32[]{:S(2)}, u32[]{:S(2)}) collective-permute-start(bf16[32,128,128]{2,1,0:T(8,128)(2,1)} %get-tuple-element.17), channel_id=1, source_target_pairs={{0,16},{16,0},{32,48},{48,32},{64,80},{80,64},{96,112},{112,96},{1... | collective-permute-start | bytes 3145736 | tf_op jit(solution)/shard_map/ppermute | solution.py:415
  84.7 12.7 %all-to-all-start.2 = ((f32[32,8,128]{2,1,0:T(8,128)}), f32[32,8,128]{2,1,0:T(8,128)S(1)}, u32[]{:S(2)}, u32[]{:S(2)}) async-start(f32[32,8,128]{2,1,0:T(8,128)} %get-tuple-element.22), calls=%async_computation.2 | async-start | bytes 262144 | tf_op jit(solution)/shard_map/all_to_all | solution.py:414
  92.7 46.7 %copy-start = (bf16[1,128,1024]{2,1,0:T(8,128)(2,1)S(1)}, bf16[1,128,1024]{2,1,0:T(8,128)(2,1)}, u32[]{:S(2)}) copy-start(bf16[1,128,1024]{2,1,0:T(8,128)(2,1)} %k_ref.1) | copy-start | bytes 786436
  97.3 42.1 %all-to-all-start.1 = ((bf16[32,256,128]{2,1,0:T(8,128)(2,1)}), bf16[32,256,128]{2,1,0:T(8,128)(2,1)S(1)}, u32[]{:S(2)}, u32[]{:S(2)}) async-start(bf16[32,256,128]{2,1,0:T(8,128)(2,1)} %shard_map.112), calls=%async_computation.1 | async-start | bytes 4194304 | tf_op jit(solution)/shard_map/all_to_all | solution.py:423
  102.5 5.5 %collective-permute-start.6 = (f32[2,128]{1,0:T(2,128)S(1)}, f32[2,128]{1,0:T(2,128)S(1)}, u32[]{:S(2)}, u32[]{:S(2)}) collective-permute-start(f32[2,128]{1,0:T(2,128)S(1)} %shard_map.114), channel_id=1, source_target_pairs={{0,1},{1,0},{2,3},{3,2},{4,5},{5,4},{6,7},{7,6},{8,9},{9,8},{10,11... | collective-permute-start | bytes 3080 | tf_op jit(solution)/shard_map/ppermute | solution.py:338
  107.9 15.2 %collective-permute-start.7 = (f32[2,128]{1,0:T(2,128)S(1)}, f32[2,128]{1,0:T(2,128)S(1)}, u32[]{:S(2)}, u32[]{:S(2)}) collective-permute-start(f32[2,128]{1,0:T(2,128)S(1)} %add.33), channel_id=1, source_target_pairs={{0,8},{1,9},{2,10},{3,11},{4,12},{5,13},{6,14},{7,15},{8,0},{9,1},... | collective-permute-start | bytes 3080 | tf_op jit(solution)/shard_map/ppermute | solution.py:338
  123.1 9.4 %collective-permute-start.8 = (f32[2,128]{1,0:T(2,128)S(1)}, f32[2,128]{1,0:T(2,128)S(1)}, u32[]{:S(2)}, u32[]{:S(2)}) collective-permute-start(f32[2,128]{1,0:T(2,128)S(1)} %add.34), channel_id=1, source_target_pairs={{0,4},{1,5},{2,6},{3,7},{4,0},{5,1},{6,2},{7,3},{8,12},{9,13},{10,... | collective-permute-start | bytes 3080 | tf_op jit(solution)/shard_map/ppermute | solution.py:338
  132.5 6.4 %collective-permute-start.9 = (f32[2,128]{1,0:T(2,128)S(1)}, f32[2,128]{1,0:T(2,128)S(1)}, u32[]{:S(2)}, u32[]{:S(2)}) collective-permute-start(f32[2,128]{1,0:T(2,128)S(1)} %add.35), channel_id=1, source_target_pairs={{0,2},{1,3},{2,0},{3,1},{4,6},{5,7},{6,4},{7,5},{8,10},{9,11},{10,... | collective-permute-start | bytes 3080 | tf_op jit(solution)/shard_map/ppermute | solution.py:338
